TPU v7x, 32 devices: a whole 2x2x4 slice. The times are simulated.
32 devices in a mesh: fsdp: 32 (over z, y, x, core).
Axes of the slice: x: 2, y: 2, z: 4, core: 2. Of those that a mesh axis runs over, the one named last changes fastest.
Arguments:
- inputs: bfloat16 [64, 1024, 1280], P('fsdp'), may hold values from -6 to 6
- block_ids: int32 [64, 1024], P('fsdp'), may hold values from 0 to 3, never falling along the last dimension, each value on 1 to 512 neighbouring positions
- cotangent: bfloat16 [64, 1024, 1280], P('fsdp'), may hold values from -9 to 9
- first_gain: bfloat16 [1280], P('fsdp'), may hold values from 0.25 to 1.75
- query_weight: bfloat16 [1280, 1280], P(None, 'fsdp'), may hold values from -0.15625 to 0.15625
- key_weight: bfloat16 [1280, 1280], P(None, 'fsdp'), may hold values from -0.15625 to 0.15625
- value_weight: bfloat16 [1280, 1280], P(None, 'fsdp'), may hold values from -0.15625 to 0.15625
- output_weight: bfloat16 [1280, 1280], P(None, 'fsdp'), may hold values from -1.25 to 1.25
- second_gain: bfloat16 [1280], P('fsdp'), may hold values from 0.25 to 1.75
- up_weight: bfloat16 [1280, 1280], P(None, 'fsdp'), may hold values from -0.15625 to 0.15625
- down_weight: bfloat16 [1280, 1280], P(None, 'fsdp'), may hold values from -0.15625 to 0.15625
- query_scale: float32 [80], replicated, may hold values from 1 to 3
Outputs:
- layer_output: bfloat16 [64, 1024, 1280], P('fsdp')
- grad_inputs: float32 [64, 1024, 1280], P('fsdp')
- grad_first_gain: float32 [1280], P('fsdp')
- grad_query_weight: float32 [1280, 1280], P(None, 'fsdp')
- grad_key_weight: float32 [1280, 1280], P(None, 'fsdp')
- grad_value_weight: float32 [1280, 1280], P(None, 'fsdp')
- grad_output_weight: float32 [1280, 1280], P(None, 'fsdp')
- grad_second_gain: float32 [1280], P('fsdp')
- grad_up_weight: float32 [1280, 1280], P(None, 'fsdp')
- grad_down_weight: float32 [1280, 1280], P(None, 'fsdp')
- grad_query_scale: float32 [80], replicated
Inputs may be any that keep to these rules, and one draw needn't show every extreme that they name: `block_ids`: within a sequence the ids never fall, each of the 4 ids is used, by 1 to 512 consecutive tokens.
All inputs are finite; a program needn't handle non-finite values.
Results may differ from a plain program's by a relative error of at most 0.013.
The roundings to bfloat16 on the way count: a program that leaves them out, or rounds other values in their place, can miss the bound.
Values may be sent and summed in bfloat16 or wider, within the bound.
No kernel may reach another device: no remote copies, remote signals or barrier semaphores. Data moves between devices by JAX's collectives and lax.ppermute only.
A program may use at most 576 MiB of HBM per device.

v0:
```python
import math

import jax
import jax.numpy as jnp
from jax import lax
from jax.sharding import PartitionSpec as P

EPSILON = 1e-06


def multiply(left, right):
    return jnp.dot(left, right, preferred_element_type=jnp.float32)


def contract_rows(left, right):
    return lax.dot_general(
        left, right, (((0,), (0,)), ((), ())), preferred_element_type=jnp.float32
    )


def contract_last(left, right):
    return lax.dot_general(
        left, right, (((1,), (1,)), ((), ())), preferred_element_type=jnp.float32
    )


def norm_backward(grad_normed, source, root, gain):
    weighted = grad_normed * gain
    grad_gain = jnp.sum(grad_normed * source * root, axis=0)
    grad_source = root * weighted - source * root * root * root * jnp.mean(
        weighted * source, axis=-1, keepdims=True
    )
    return (grad_source, grad_gain)


def attention_forward(scaled, key_heads, value_heads, visible):
    length = scaled.shape[0]
    block_rows = min(512, length)
    context_parts = []
    logsum_parts = []
    for offset in range(0, length, block_rows):
        scores = jnp.einsum(
            "qhd,khd->hqk",
            scaled[offset : offset + block_rows],
            key_heads,
            preferred_element_type=jnp.float32,
        )
        scores = jnp.where(visible[None, offset : offset + block_rows], scores, -1e30)
        row_peak = jnp.max(scores, axis=-1, keepdims=True)
        weights = jnp.exp(scores - row_peak)
        row_total = jnp.sum(weights, axis=-1, keepdims=True)
        probability = (weights / row_total).astype(jnp.bfloat16)
        context_parts.append(
            jnp.einsum("hqk,khd->qhd", probability, value_heads, preferred_element_type=jnp.float32)
        )
        logsum_parts.append(row_peak + jnp.log(row_total))
    return (jnp.concatenate(context_parts, 0), jnp.concatenate(logsum_parts, 1))


def attention_backward(scaled, key_heads, value_heads, visible, log_totals, grad_context):
    length = scaled.shape[0]
    block_rows = min(512, length)
    grad_keys = jnp.zeros(key_heads.shape, jnp.float32)
    grad_values = jnp.zeros(value_heads.shape, jnp.float32)
    grad_scaled_parts = []
    for offset in range(0, length, block_rows):
        query_rows = scaled[offset : offset + block_rows]
        grad_rows = grad_context[offset : offset + block_rows]
        scores = jnp.einsum(
            "qhd,khd->hqk", query_rows, key_heads, preferred_element_type=jnp.float32
        )
        scores = jnp.where(visible[None, offset : offset + block_rows], scores, -1e30)
        probability = jnp.exp(scores - log_totals[:, offset : offset + block_rows])
        grad_values = grad_values + jnp.einsum(
            "hqk,qhd->khd",
            probability.astype(jnp.bfloat16),
            grad_rows,
            preferred_element_type=jnp.float32,
        )
        grad_probability = jnp.einsum(
            "qhd,khd->hqk", grad_rows, value_heads, preferred_element_type=jnp.float32
        )
        centre = jnp.sum(grad_probability * probability, axis=-1, keepdims=True)
        grad_scores = (probability * (grad_probability - centre)).astype(jnp.bfloat16)
        grad_scaled_parts.append(
            jnp.einsum("hqk,khd->qhd", grad_scores, key_heads, preferred_element_type=jnp.float32)
        )
        grad_keys = grad_keys + jnp.einsum(
            "hqk,qhd->khd", grad_scores, query_rows, preferred_element_type=jnp.float32
        )
    return (jnp.concatenate(grad_scaled_parts, 0), grad_keys, grad_values)


def unpack_weights(gathered):
    gain_pair, query_weight, key_weight, value_weight, output_weight, up_weight, down_weight = (
        gathered
    )
    return (
        gain_pair[0],
        query_weight,
        key_weight,
        value_weight,
        output_weight,
        gain_pair[1],
        up_weight,
        down_weight,
    )


def layer_forward(weights, source, sequence_ids, query_scale):
    (
        gain_first,
        query_weight,
        key_weight,
        value_weight,
        output_weight,
        gain_second,
        up_weight,
        down_weight,
    ) = weights
    length, model_width = source.shape
    head_size = query_scale.shape[0]
    head_count = model_width // head_size
    factor = query_scale / math.sqrt(head_size)
    widened = source.astype(jnp.float32)
    root_first = lax.rsqrt(jnp.mean(widened * widened, axis=-1, keepdims=True) + EPSILON)
    normed = (widened * root_first * gain_first.astype(jnp.float32)).astype(jnp.bfloat16)
    query_heads = multiply(normed, query_weight).reshape(length, head_count, head_size)
    key_heads = (
        multiply(normed, key_weight).astype(jnp.bfloat16).reshape(length, head_count, head_size)
    )
    value_heads = (
        multiply(normed, value_weight).astype(jnp.bfloat16).reshape(length, head_count, head_size)
    )
    scaled = (query_heads * factor).astype(jnp.bfloat16)
    visible = sequence_ids[None, :] <= sequence_ids[:, None]
    context, log_totals = attention_forward(scaled, key_heads, value_heads, visible)
    context = context.astype(jnp.bfloat16).reshape(length, model_width)
    hidden = widened + multiply(context, output_weight)
    root_second = lax.rsqrt(jnp.mean(hidden * hidden, axis=-1, keepdims=True) + EPSILON)
    normed_second = (hidden * root_second * gain_second.astype(jnp.float32)).astype(jnp.bfloat16)
    upward = multiply(normed_second, up_weight)
    activated = jax.nn.silu(upward).astype(jnp.bfloat16)
    output = (hidden + multiply(activated, down_weight)).astype(jnp.bfloat16)
    saved = (
        widened,
        root_first,
        normed,
        query_heads,
        scaled,
        key_heads,
        value_heads,
        visible,
        log_totals,
        context,
        hidden,
        root_second,
        normed_second,
        upward,
        activated,
    )
    return (output, saved)


def layer_backward(weights, saved, grad_output, query_scale):
    (
        gain_first,
        query_weight,
        key_weight,
        value_weight,
        output_weight,
        gain_second,
        up_weight,
        down_weight,
    ) = weights
    (
        widened,
        root_first,
        normed,
        query_heads,
        scaled,
        key_heads,
        value_heads,
        visible,
        log_totals,
        context,
        hidden,
        root_second,
        normed_second,
        upward,
        activated,
    ) = saved
    length, model_width = widened.shape
    head_size = query_scale.shape[0]
    head_count = model_width // head_size
    factor = query_scale / math.sqrt(head_size)
    grad_down = contract_rows(activated, grad_output)
    grad_activated = contract_last(grad_output, down_weight)
    sigmoid = jax.nn.sigmoid(upward)
    grad_upward = (grad_activated * sigmoid * (1.0 + upward * (1.0 - sigmoid))).astype(jnp.bfloat16)
    grad_up = contract_rows(normed_second, grad_upward)
    grad_normed_second = contract_last(grad_upward, up_weight)
    grad_hidden, grad_gain_second = norm_backward(
        grad_normed_second, hidden, root_second, gain_second.astype(jnp.float32)
    )
    grad_hidden = grad_hidden + grad_output.astype(jnp.float32)
    grad_branch = grad_hidden.astype(jnp.bfloat16)
    grad_output_weight = contract_rows(context, grad_branch)
    grad_context = (
        contract_last(grad_branch, output_weight)
        .astype(jnp.bfloat16)
        .reshape(length, head_count, head_size)
    )
    grad_scaled, grad_keys, grad_values = attention_backward(
        scaled, key_heads, value_heads, visible, log_totals, grad_context
    )
    grad_query = (grad_scaled * factor).astype(jnp.bfloat16).reshape(length, model_width)
    scale_grad = jnp.sum(grad_scaled * query_heads, axis=(0, 1)) / math.sqrt(head_size)
    grad_keys = grad_keys.astype(jnp.bfloat16).reshape(length, model_width)
    grad_values = grad_values.astype(jnp.bfloat16).reshape(length, model_width)
    grad_query_weight = contract_rows(normed, grad_query)
    grad_key_weight = contract_rows(normed, grad_keys)
    grad_value_weight = contract_rows(normed, grad_values)
    grad_normed = (
        contract_last(grad_query, query_weight)
        + contract_last(grad_keys, key_weight)
        + contract_last(grad_values, value_weight)
    )
    grad_source, grad_gain_first = norm_backward(
        grad_normed, widened, root_first, gain_first.astype(jnp.float32)
    )
    grad_source = grad_source + grad_hidden
    gain_grads = jnp.stack([grad_gain_first, grad_gain_second])
    weight_grads = (
        gain_grads,
        grad_query_weight,
        grad_key_weight,
        grad_value_weight,
        grad_output_weight,
        grad_up,
        grad_down,
    )
    return (grad_source, weight_grads, scale_grad)


def on_device(
    inputs,
    block_ids,
    cotangent,
    first_gain,
    query_weight,
    key_weight,
    value_weight,
    output_weight,
    second_gain,
    up_weight,
    down_weight,
    query_scale,
):
    gain_pair = jnp.stack([first_gain, second_gain])
    scale_total = jnp.zeros(query_scale.shape, jnp.float32)
    grad_totals = None
    collected = []
    grad_list = []
    for sequence in range(inputs.shape[0]):
        gathered = unpack_weights(
            (
                lax.all_gather(gain_pair, "fsdp", axis=1, tiled=True),
                lax.all_gather(query_weight, "fsdp", axis=1, tiled=True),
                lax.all_gather(key_weight, "fsdp", axis=1, tiled=True),
                lax.all_gather(value_weight, "fsdp", axis=1, tiled=True),
                lax.all_gather(output_weight, "fsdp", axis=1, tiled=True),
                lax.all_gather(up_weight, "fsdp", axis=1, tiled=True),
                lax.all_gather(down_weight, "fsdp", axis=1, tiled=True),
            )
        )
        output, saved = layer_forward(gathered, inputs[sequence], block_ids[sequence], query_scale)
        collected.append(output)
        gathered = unpack_weights(
            (
                lax.all_gather(gain_pair, "fsdp", axis=1, tiled=True),
                lax.all_gather(query_weight, "fsdp", axis=1, tiled=True),
                lax.all_gather(key_weight, "fsdp", axis=1, tiled=True),
                lax.all_gather(value_weight, "fsdp", axis=1, tiled=True),
                lax.all_gather(output_weight, "fsdp", axis=1, tiled=True),
                lax.all_gather(up_weight, "fsdp", axis=1, tiled=True),
                lax.all_gather(down_weight, "fsdp", axis=1, tiled=True),
            )
        )
        grad_source, weight_grads, scale_grad = layer_backward(
            gathered, saved, cotangent[sequence], query_scale
        )
        grad_list.append(grad_source)
        scale_total = scale_total + scale_grad
        if sequence == 0:
            grad_totals = tuple(weight_grads)
        else:
            grad_totals = tuple(jax.tree.map(jnp.add, tuple(grad_totals), tuple(weight_grads)))
    grad_shards = (
        lax.psum_scatter(grad_totals[0], "fsdp", scatter_dimension=1, tiled=True),
        lax.psum_scatter(grad_totals[1], "fsdp", scatter_dimension=1, tiled=True),
        lax.psum_scatter(grad_totals[2], "fsdp", scatter_dimension=1, tiled=True),
        lax.psum_scatter(grad_totals[3], "fsdp", scatter_dimension=1, tiled=True),
        lax.psum_scatter(grad_totals[4], "fsdp", scatter_dimension=1, tiled=True),
        lax.psum_scatter(grad_totals[5], "fsdp", scatter_dimension=1, tiled=True),
        lax.psum_scatter(grad_totals[6], "fsdp", scatter_dimension=1, tiled=True),
    )
    scale_total = lax.psum(scale_total, "fsdp")
    gain_shards = grad_shards[0]
    return (
        jnp.stack(collected),
        jnp.stack(grad_list),
        gain_shards[0],
        grad_shards[1],
        grad_shards[2],
        grad_shards[3],
        grad_shards[4],
        gain_shards[1],
        grad_shards[5],
        grad_shards[6],
        scale_total,
    )


def solution(mesh):
    in_specs = (
        P("fsdp", None, None),
        P("fsdp", None),
        P("fsdp", None, None),
        P("fsdp"),
        P(None, "fsdp"),
        P(None, "fsdp"),
        P(None, "fsdp"),
        P(None, "fsdp"),
        P("fsdp"),
        P(None, "fsdp"),
        P(None, "fsdp"),
        P(),
    )
    out_specs = (
        P("fsdp", None, None),
        P("fsdp", None, None),
        P("fsdp"),
        P(None, "fsdp"),
        P(None, "fsdp"),
        P(None, "fsdp"),
        P(None, "fsdp"),
        P("fsdp"),
        P(None, "fsdp"),
        P(None, "fsdp"),
        P(),
    )
    return jax.shard_map(
        on_device, mesh=mesh, in_specs=in_specs, out_specs=out_specs, check_vma=False
    )
```

profile of v0, /device:TPU:0, one launch (start us, length us, event | category | flops | bytes accessed | tf_op | source)
XLA Modules:
  0.0 1296.1 jit_solution(1678462744060282050)
XLA Ops:
  17.0 43.0 %all-gather = bf16[32,40,2]{1,2,0:T(2,128)(2,1)S(1)} all-gather(bf16[1,40,2]{1,2,0:T(2,128)(2,1)S(1)} %maximum_bitcast_fusion), channel_id=1, replica_groups=mesh['fsdp'=32] {'fsdp'}, dimensions={0}, use_global_device_ids=true | all-gather | bytes 5280 | tf_op jit(solution)/shard_map/all_gather | solution.py:268
  83.9 50.0 %all-gather.8.cloned.1.call-done = bf16[1280,1280]{0,1:T(8,128)(2,1)} async-done(((bf16[1280,40]{0,1:T(8,128)(2,1)}), bf16[1280,1280]{0,1:T(8,128)(2,1)}) %all-gather.8.cloned.1.call-update) | async-done | bytes 3276816 | tf_op jit(solution)/shard_map/all_gather | solution.py:271
  170.9 24.1 %all-gather.10.cloned.1.call-done = bf16[1280,1280]{0,1:T(8,128)(2,1)} async-done(((bf16[1280,40]{0,1:T(8,128)(2,1)}), bf16[1280,1280]{0,1:T(8,128)(2,1)}) %all-gather.10.cloned.1.call-update) | async-done | bytes 3276816 | tf_op jit(solution)/shard_map/all_gather | solution.py:269
  211.5 13.7 %select_reduce_fusion.2 = (f32[16,512]{1,0:T(8,128)S(1)}, f32[16,512,1024]{2,1,0:T(8,128)}) fusion(pred[512,1024]{1,0:T(8,128)(4,1)S(1)} %get-tuple-element.36, bf16[1024,16,80]{0,2,1:T(8,128)(2,1)S(1)} %bitcast.254, bf16[1024,16,80]{0,2,1:T(8,128)(2,1)S(1)} %get-tuple-element.45), kind=kOutput, calls=%fused_computation.26 | convolution fusion | flops 1358946304 | bytes 38043648 | tf_op jit(solution)/shard_map/qhd,khd->hqk/dot_general | solution.py:42
  225.2 13.6 %select_reduce_fusion.3 = (f32[16,512]{1,0:T(8,128)S(1)}, f32[16,512,1024]{2,1,0:T(8,128)}) fusion(pred[512,1024]{1,0:T(8,128)(4,1)S(1)} %copy-done.12, bf16[1024,16,80]{0,2,1:T(8,128)(2,1)S(1)} %bitcast.255, bf16[1024,16,80]{0,2,1:T(8,128)(2,1)S(1)} %get-tuple-element.45), kind=kOutput, calls=%fused_computation.27 | convolution fusion | flops 1358946304 | bytes 38043648 | tf_op jit(solution)/shard_map/qhd,khd->hqk/dot_general | solution.py:42
  238.9 14.7 %fusion.1 = f32[16,512]{1,0:T(8,128)S(1)} fusion(f32[16,512,1024]{2,1,0:T(8,128)} %get-tuple-element.55, f32[16,512]{1,0:T(8,128)S(1)} %get-tuple-element.54, pred[512,1024]{1,0:T(8,128)(4,1)S(1)} %get-tuple-element.36), kind=kLoop, calls=%fused_computation.21 | loop fusion | flops 25157632 | bytes 34144256 | tf_op jit(solution)/shard_map/reduce_sum | solution.py:51
  253.7 15.0 %fusion.102 = bf16[16,80,512]{2,1,0:T(8,128)(2,1)} fusion(bf16[1024,16,80]{0,2,1:T(8,128)(2,1)S(1)} %bitcast.263, f32[16,512,1024]{2,1,0:T(8,128)} %get-tuple-element.55, f32[16,512]{1,0:T(8,128)S(1)} %fusion.1, f32[16,512]{1,0:T(8,128)S(1)} %get-tuple-element.54, pred[512,1024]{1,0:T(8,128)(4,1)S(1)} %get-tuple-element.36), kind=kOutput, calls=%fused_computation.170 | convolution fusion | flops 1376387072 | bytes 38076416 | tf_op jit(solution)/shard_map/hqk,khd->qhd/dot_general | solution.py:54
  268.7 14.5 %fusion = f32[16,512]{1,0:T(8,128)S(1)} fusion(f32[16,512,1024]{2,1,0:T(8,128)} %get-tuple-element.57, f32[16,512]{1,0:T(8,128)S(1)} %get-tuple-element.56, pred[512,1024]{1,0:T(8,128)(4,1)S(1)} %copy-done.12), kind=kLoop, calls=%fused_computation.20 | loop fusion | flops 25157632 | bytes 34144256 | tf_op jit(solution)/shard_map/reduce_sum | solution.py:51
  283.3 15.8 %fusion.103 = bf16[16,80,512]{2,1,0:T(8,128)(2,1)} fusion(bf16[1024,16,80]{0,2,1:T(8,128)(2,1)S(1)} %bitcast.264, f32[16,512,1024]{2,1,0:T(8,128)} %get-tuple-element.57, f32[16,512]{1,0:T(8,128)S(1)} %fusion, f32[16,512]{1,0:T(8,128)S(1)} %get-tuple-element.56, pred[512,1024]{1,0:T(8,128)(4,1)S(1)} %copy-done.12), kind=kOutput, calls=%fused_computation.171 | convolution fusion | flops 1376387072 | bytes 38076416 | tf_op jit(solution)/shard_map/hqk,khd->qhd/dot_general | solution.py:54
  299.1 13.9 %select_reduce_fusion = (f32[16,512]{1,0:T(8,128)S(1)}, f32[16,512,1024]{2,1,0:T(8,128)}) fusion(pred[512,1024]{1,0:T(8,128)(4,1)S(1)} %copy-done.7, bf16[1024,16,80]{0,2,1:T(8,128)(2,1)S(1)} %bitcast.250, bf16[1024,16,80]{0,2,1:T(8,128)(2,1)S(1)} %copy-done.14), kind=kOutput, calls=%fused_computation.24 | convolution fusion | flops 1358946304 | bytes 38043648 | tf_op jit(solution)/shard_map/qhd,khd->hqk/dot_general | solution.py:42
  313.0 13.4 %select_reduce_fusion.1 = (f32[16,512]{1,0:T(8,128)S(1)}, f32[16,512,1024]{2,1,0:T(8,128)}) fusion(pred[512,1024]{1,0:T(8,128)(4,1)S(1)} %copy-done.9, bf16[1024,16,80]{0,2,1:T(8,128)(2,1)S(1)} %bitcast.251, bf16[1024,16,80]{0,2,1:T(8,128)(2,1)S(1)} %copy-done.14), kind=kOutput, calls=%fused_computation.25 | convolution fusion | flops 1358946304 | bytes 38043648 | tf_op jit(solution)/shard_map/qhd,khd->hqk/dot_general | solution.py:42
  326.5 14.7 %fusion.3 = f32[16,512]{1,0:T(8,128)S(1)} fusion(f32[16,512,1024]{2,1,0:T(8,128)} %get-tuple-element.49, f32[16,512]{1,0:T(8,128)S(1)} %get-tuple-element.48, pred[512,1024]{1,0:T(8,128)(4,1)S(1)} %copy-done.7), kind=kLoop, calls=%fused_computation.23 | loop fusion | flops 25157632 | bytes 34144256 | tf_op jit(solution)/shard_map/reduce_sum | solution.py:51
  341.2 15.1 %fusion.100 = bf16[16,80,512]{2,1,0:T(8,128)(2,1)} fusion(bf16[1024,16,80]{0,2,1:T(8,128)(2,1)S(1)} %bitcast.260, f32[16,512,1024]{2,1,0:T(8,128)} %get-tuple-element.49, f32[16,512]{1,0:T(8,128)S(1)} %fusion.3, f32[16,512]{1,0:T(8,128)S(1)} %get-tuple-element.48, pred[512,1024]{1,0:T(8,128)(4,1)S(1)} %copy-done.7), kind=kOutput, calls=%fused_computation.168 | convolution fusion | flops 1376387072 | bytes 38076416 | tf_op jit(solution)/shard_map/hqk,khd->qhd/dot_general | solution.py:54
  356.3 14.9 %fusion.2 = f32[16,512]{1,0:T(8,128)S(1)} fusion(f32[16,512,1024]{2,1,0:T(8,128)} %get-tuple-element.51, f32[16,512]{1,0:T(8,128)S(1)} %get-tuple-element.50, pred[512,1024]{1,0:T(8,128)(4,1)S(1)} %copy-done.9), kind=kLoop, calls=%fused_computation.22 | loop fusion | flops 25157632 | bytes 34144256 | tf_op jit(solution)/shard_map/reduce_sum | solution.py:51
  371.3 15.2 %fusion.101 = bf16[16,80,512]{2,1,0:T(8,128)(2,1)} fusion(bf16[1024,16,80]{0,2,1:T(8,128)(2,1)S(1)} %bitcast.261, f32[16,512,1024]{2,1,0:T(8,128)} %get-tuple-element.51, f32[16,512]{1,0:T(8,128)S(1)} %fusion.2, f32[16,512]{1,0:T(8,128)S(1)} %get-tuple-element.50, pred[512,1024]{1,0:T(8,128)(4,1)S(1)} %copy-done.9), kind=kOutput, calls=%fused_computation.169 | convolution fusion | flops 1376387072 | bytes 38076416 | tf_op jit(solution)/shard_map/hqk,khd->qhd/dot_general | solution.py:54
  503.5 16.8 %fusion.12 = f32[16,80,1024]{2,1,0:T(8,128)} fusion(bf16[512,16,80]{0,2,1:T(8,128)(2,1)S(1)} %bitcast.278, f32[16,512,1024]{2,1,0:T(8,128)} %get-tuple-element.55, f32[16,512]{1,0:T(8,128)S(1)} %log_add_fusion.2, pred[512,1024]{1,0:T(8,128)(4,1)S(1)} %copy-done.11), kind=kOutput, calls=%fused_computation.34 | convolution fusion | flops 1367343104 | bytes 40665088 | tf_op jit(solution)/shard_map/hqk,qhd->khd/dot_general | solution.py:74
  529.7 17.9 %add_convert_fusion.2 = bf16[16,80,1024]{2,1,0:T(8,128)(2,1)} fusion(f32[16,80,1024]{2,1,0:T(8,128)} %fusion.12, bf16[512,16,80]{0,2,1:T(8,128)(2,1)S(1)} %bitcast.281, f32[16,512,1024]{2,1,0:T(8,128)} %get-tuple-element.57, f32[16,512]{1,0:T(8,128)S(1)} %log_add_fusion.3, pred[512,1024]{1,0:T(8,128)(4,1)S(1)} %copy-done.13), kind=kOutput, calls=%fused_computation.118 | convolution fusion | flops 1369964544 | bytes 43286528 | tf_op jit(solution)/shard_map/hqk,qhd->khd/dot_general | solution.py:74
  566.4 25.0 %multiply_reduce_fusion.3 = (f32[16,512]{1,0:T(8,128)S(1)}, f32[16,512,1024]{2,1,0:T(8,128)}) fusion(f32[16,512,1024]{2,1,0:T(8,128)} %get-tuple-element.57, f32[16,512]{1,0:T(8,128)S(1)} %log_add_fusion.3, pred[512,1024]{1,0:T(8,128)(4,1)S(1)} %copy-done.13, bf16[512,16,80]{0,2,1:T(8,128)(2,1)} %bitcast.280, bf16[1024,16,80]{0,2,1:T(8,128)(2,1)S(1)} %bitcast.265), kind=kOutput, calls=%fused_computation.10 | convolution fusion | flops 1375723520 | bytes 71630848 | tf_op jit(solution)/shard_map/qhd,khd->hqk/dot_general | solution.py:80
  591.3 38.2 %multiply_convert_fusion.3 = bf16[16,512,1024]{2,1,0:T(8,128)(2,1)} fusion(f32[16,512,1024]{2,1,0:T(8,128)} %get-tuple-element.64, f32[16,512,1024]{2,1,0:T(8,128)} %get-tuple-element.57, f32[16,512]{1,0:T(8,128)S(1)} %get-tuple-element.63, f32[16,512]{1,0:T(8,128)S(1)} %log_add_fusion.3, pred[512,1024]{1,0:T(8,128)(4,1)S(1)} %copy-done.13), kind=kLoop, calls=%fused_computation.9 | loop fusion | flops 41943040 | bytes 84475904 | tf_op jit(solution)/shard_map/convert_element_type | solution.py:84
  643.2 17.3 %fusion.8 = f32[16,80,1024]{2,1,0:T(8,128)} fusion(bf16[512,16,80]{0,2,1:T(8,128)(2,1)} %bitcast.274, f32[16,512,1024]{2,1,0:T(8,128)} %get-tuple-element.49, f32[16,512]{1,0:T(8,128)S(1)} %log_add_fusion, pred[512,1024]{1,0:T(8,128)(4,1)S(1)} %copy-done.8), kind=kOutput, calls=%fused_computation.32 | convolution fusion | flops 1367343104 | bytes 40665088 | tf_op jit(solution)/shard_map/hqk,qhd->khd/dot_general | solution.py:74
  660.5 20.6 %add_convert_fusion = bf16[16,80,1024]{2,1,0:T(8,128)(2,1)} fusion(f32[16,80,1024]{2,1,0:T(8,128)} %fusion.8, bf16[512,16,80]{0,2,1:T(8,128)(2,1)} %bitcast.276, f32[16,512,1024]{2,1,0:T(8,128)} %get-tuple-element.51, f32[16,512]{1,0:T(8,128)S(1)} %log_add_fusion.1, pred[512,1024]{1,0:T(8,128)(4,1)} %get-tuple-element.37), kind=kOutput, calls=%fused_computation.112 | convolution fusion | flops 1369964544 | bytes 43286528 | tf_op jit(solution)/shard_map/hqk,qhd->khd/dot_general | solution.py:74
  692.1 26.0 %multiply_reduce_fusion.2 = (f32[16,512]{1,0:T(8,128)S(1)}, f32[16,512,1024]{2,1,0:T(8,128)}) fusion(f32[16,512,1024]{2,1,0:T(8,128)} %get-tuple-element.55, f32[16,512]{1,0:T(8,128)S(1)} %log_add_fusion.2, pred[512,1024]{1,0:T(8,128)(4,1)} %copy-done.10, bf16[512,16,80]{0,2,1:T(8,128)(2,1)} %bitcast.279, bf16[1024,16,80]{0,2,1:T(8,128)(2,1)} %bitcast.262), kind=kOutput, calls=%fused_computation.7 | convolution fusion | flops 1375723520 | bytes 71630848 | tf_op jit(solution)/shard_map/qhd,khd->hqk/dot_general | solution.py:80
  718.1 28.3 %multiply_convert_fusion.2 = bf16[16,512,1024]{2,1,0:T(8,128)(2,1)} fusion(f32[16,512,1024]{2,1,0:T(8,128)} %get-tuple-element.62, f32[16,512,1024]{2,1,0:T(8,128)} %get-tuple-element.55, f32[16,512]{1,0:T(8,128)S(1)} %get-tuple-element.61, f32[16,512]{1,0:T(8,128)S(1)} %log_add_fusion.2, pred[512,1024]{1,0:T(8,128)(4,1)} %copy-done.10), kind=kLoop, calls=%fused_computation.6 | loop fusion | flops 41943040 | bytes 84475904 | tf_op jit(solution)/shard_map/convert_element_type | solution.py:84
  746.4 12.6 fusion.164
  759.0 25.6 %multiply_reduce_fusion.1 = (f32[16,512]{1,0:T(8,128)S(1)}, f32[16,512,1024]{2,1,0:T(8,128)}) fusion(f32[16,512,1024]{2,1,0:T(8,128)} %get-tuple-element.51, f32[16,512]{1,0:T(8,128)S(1)} %log_add_fusion.1, pred[512,1024]{1,0:T(8,128)(4,1)} %get-tuple-element.37, bf16[512,16,80]{0,2,1:T(8,128)(2,1)} %bitcast.277, bf16[1024,16,80]{0,2,1:T(8,128)(2,1)} %bitcast.258), kind=kOutput, calls=%fused_computation.4 | convolution fusion | flops 1375723520 | bytes 71630848 | tf_op jit(solution)/shard_map/qhd,khd->hqk/dot_general | solution.py:80
  795.5 28.5 %multiply_convert_fusion.1 = bf16[16,512,1024]{2,1,0:T(8,128)(2,1)} fusion(f32[16,512,1024]{2,1,0:T(8,128)} %get-tuple-element.68, f32[16,512,1024]{2,1,0:T(8,128)} %get-tuple-element.51, f32[16,512]{1,0:T(8,128)S(1)} %get-tuple-element.67, f32[16,512]{1,0:T(8,128)S(1)} %log_add_fusion.1, pred[512,1024]{1,0:T(8,128)(4,1)} %get-tuple-element.37), kind=kLoop, calls=%fused_computation.3 | loop fusion | flops 41943040 | bytes 84475904 | tf_op jit(solution)/shard_map/convert_element_type | solution.py:84
  836.5 25.5 %multiply_reduce_fusion = (f32[16,512]{1,0:T(8,128)S(1)}, f32[16,512,1024]{2,1,0:T(8,128)}) fusion(f32[16,512,1024]{2,1,0:T(8,128)} %get-tuple-element.49, f32[16,512]{1,0:T(8,128)S(1)} %log_add_fusion, pred[512,1024]{1,0:T(8,128)(4,1)S(1)} %copy-done.8, bf16[512,16,80]{0,2,1:T(8,128)(2,1)} %bitcast.275, bf16[1024,16,80]{0,2,1:T(8,128)(2,1)} %bitcast.259), kind=kOutput, calls=%fused_computation.1 | convolution fusion | flops 1375723520 | bytes 71630848 | tf_op jit(solution)/shard_map/qhd,khd->hqk/dot_general | solution.py:80
  862.0 28.3 %multiply_convert_fusion = bf16[16,512,1024]{2,1,0:T(8,128)(2,1)} fusion(f32[16,512,1024]{2,1,0:T(8,128)} %get-tuple-element.66, f32[16,512,1024]{2,1,0:T(8,128)} %get-tuple-element.49, f32[16,512]{1,0:T(8,128)S(1)} %get-tuple-element.65, f32[16,512]{1,0:T(8,128)S(1)} %log_add_fusion, pred[512,1024]{1,0:T(8,128)(4,1)S(1)} %copy-done.8), kind=kLoop, calls=%fused_computation | loop fusion | flops 41943040 | bytes 84475904 | tf_op jit(solution)/shard_map/convert_element_type | solution.py:84
  1009.7 13.5 %fusion.61 = (f32[1280]{0:T(1024)S(1)}, f32[1024]{0:T(1024)S(1)}, f32[1024]{0:T(1024)S(1)}, f32[1280]{0:T(1024)S(1)}, f32[1024,1280]{1,0:T(8,128)}) fusion(f32[1024]{0:T(1024)S(1)} %copy-done.57, bf16[2,1024,1280]{2,1,0:T(8,128)(2,1)S(1)} %bitcast.273, f32[1280]{0:T(1024)S(1)} %copy-done.47, f32[1024,1280]{1,0:T(8,128)S(1)} %add_add_fusion, ...), kind=kOutput, calls=%fused_computation.92 | convolution fusion | flops 3376410112 | bytes 32144384 | tf_op jit(solution)/shard_map/dot_general | solution.py:22
  1030.0 41.1 %all-reduce.1 = (f32[2,1280]{1,0:T(2,128)S(1)}, f32[80]{0:T(128)}) all-reduce(f32[2,1280]{1,0:T(2,128)S(1)} %maximum_add_fusion, f32[80]{0:T(128)S(1)} %add_multiply_fusion), channel_id=2, replica_groups=mesh['fsdp'=32] {'fsdp'}, use_global_device_ids=true, to_apply=%region_24.25.clone | all-reduce | flops 2640 | bytes 21120
  1109.0 36.3 %reduce-scatter.8.cloned.1.call-done = f32[1280,40]{0,1:T(8,128)} async-done(((f32[1280,1280]{0,1:T(8,128)}), f32[1280,40]{0,1:T(8,128)}) %reduce-scatter.8.cloned.1.call-update) | async-done | bytes 204816 | tf_op jit(solution)/shard_map/reduce_scatter | solution.py:301
  1145.3 143.8 %reduce-scatter.10.cloned.1.call-done = f32[1280,40]{0,1:T(8,128)} async-done(((f32[1280,1280]{0,1:T(8,128)}), f32[1280,40]{0,1:T(8,128)}) %reduce-scatter.10.cloned.1.call-update) | async-done | bytes 204816 | tf_op jit(solution)/shard_map/reduce_scatter | solution.py:302
  (343 shorter events, 443.2 us)
Async XLA Ops:
  7.2 65.7 %all-gather.12.cloned.1.call-start = ((), (), s32[]{:S(2)}) async-start(), calls=%async_computation.8 | async-start | bytes 3379200 | tf_op jit(solution)/shard_map/all_gather | solution.py:270
  7.9 126.0 %all-gather.8.cloned.1.call-start = ((), (), s32[]{:S(2)}) async-start(), calls=%async_computation.6 | async-start | bytes 3379200 | tf_op jit(solution)/shard_map/all_gather | solution.py:271
  8.7 186.3 %all-gather.10.cloned.1.call-start = ((), (), s32[]{:S(2)}) async-start(), calls=%async_computation.7 | async-start | bytes 3379200 | tf_op jit(solution)/shard_map/all_gather | solution.py:269
  9.4 377.1 %all-gather.14.cloned.1.call-start = ((), (), s32[]{:S(2)}) async-start(), calls=%async_computation.9 | async-start | bytes 3379200 | tf_op jit(solution)/shard_map/all_gather | solution.py:272
  10.0 392.0 %all-gather.16.cloned.1.call-start = ((), (), s32[]{:S(2)}) async-start(), calls=%async_computation.10 | async-start | bytes 3379200 | tf_op jit(solution)/shard_map/all_gather | solution.py:273
  10.6 412.2 %all-gather.18.cloned.1.call-start = ((), (), s32[]{:S(2)}) async-start(), calls=%async_computation.11 | async-start | bytes 3379200 | tf_op jit(solution)/shard_map/all_gather | solution.py:274
  11.2 1097.8 %reduce-scatter.18.cloned.1.call-start = ((), (), s32[]{:S(2)}) async-start(), calls=%async_computation.17 | async-start | bytes 6758400 | tf_op jit(solution)/shard_map/reduce_scatter | solution.py:306
  60.8 140.7 %copy-start.46 = (f32[1280]{0:T(1024)}, f32[1280]{0:T(1024)S(1)}, u32[]{:S(2)}) copy-start(f32[1280]{0:T(1024)S(1)} %get-tuple-element.24) | copy-start | bytes 15364
  64.0 189.6 %copy-start.10 = (pred[512,1024]{1,0:T(8,128)(4,1)}, pred[512,1024]{1,0:T(8,128)(4,1)S(1)}, u32[]{:S(2)}) copy-start(pred[512,1024]{1,0:T(8,128)(4,1)S(1)} %get-tuple-element.36) | copy-start | bytes 1572868
  64.0 130.9 %copy-start.49 = (f32[1024]{0:T(1024)}, f32[1024]{0:T(1024)S(1)}, u32[]{:S(2)}) copy-start(f32[1024]{0:T(1024)S(1)} %get-tuple-element.70) | copy-start | bytes 12292
  64.0 137.5 %copy-start.53 = (f32[1024]{0:T(1024)}, f32[1024]{0:T(1024)S(1)}, u32[]{:S(2)}) copy-start(f32[1024]{0:T(1024)S(1)} %get-tuple-element.71) | copy-start | bytes 12292
  83.9 141.3 %copy-start.2 = (bf16[1024,1280]{0,1:T(8,128)(2,1)}, bf16[1024,1280]{0,1:T(8,128)(2,1)S(1)}, u32[]{:S(2)}) copy-start(bf16[1024,1280]{0,1:T(8,128)(2,1)S(1)} %copy.58) | copy-start | bytes 7864324
  225.2 28.4 %copy-start.34 = (f32[16,512]{1,0:T(8,128)}, f32[16,512]{1,0:T(8,128)S(1)}, u32[]{:S(2)}) copy-start(f32[16,512]{1,0:T(8,128)S(1)} %get-tuple-element.54) | copy-start | bytes 98308
  238.9 44.4 %copy-start.36 = (f32[16,512]{1,0:T(8,128)}, f32[16,512]{1,0:T(8,128)S(1)}, u32[]{:S(2)}) copy-start(f32[16,512]{1,0:T(8,128)S(1)} %get-tuple-element.56) | copy-start | bytes 98308
  313.0 28.2 %copy-start.38 = (f32[16,512]{1,0:T(8,128)}, f32[16,512]{1,0:T(8,128)S(1)}, u32[]{:S(2)}) copy-start(f32[16,512]{1,0:T(8,128)S(1)} %get-tuple-element.48) | copy-start | bytes 98308
  422.5 686.5 %reduce-scatter.16.cloned.1.call-start = ((), (), s32[]{:S(2)}) async-start(), calls=%async_computation.16 | async-start | bytes 6758400 | tf_op jit(solution)/shard_map/reduce_scatter | solution.py:305
  432.9 26.0 %slice-start.14 = ((s8[5242880]{0:T(1024)(128)(4,1)}), s8[4194304]{0:T(1024)(128)(4,1)S(1)}, s32[]{:S(2)}) async-start(s8[5242880]{0:T(1024)(128)(4,1)} %bitcast.300), calls=%async_computation.32 | async-start | bytes 8388608
  438.6 20.3 %slice-start.15 = ((s8[5242880]{0:T(1024)(128)(4,1)}), s8[1048576]{0:T(1024)(128)(4,1)S(1)}, s32[]{:S(2)}) async-start(s8[5242880]{0:T(1024)(128)(4,1)} %bitcast.300), calls=%async_computation.33 | async-start | bytes 2097152
  502.4 606.5 %reduce-scatter.14.cloned.1.call-start = ((), (), s32[]{:S(2)}) async-start(), calls=%async_computation.15 | async-start | bytes 6758400 | tf_op jit(solution)/shard_map/reduce_scatter | solution.py:304
  529.7 18.0 %copy-start.47 = (f32[1280]{0:T(1024)S(1)}, f32[1280]{0:T(1024)}, u32[]{:S(2)}) copy-start(f32[1280]{0:T(1024)} %copy-done.46) | copy-start | bytes 15364
  529.7 18.0 %copy-start.54 = (f32[1024]{0:T(1024)S(1)}, f32[1024]{0:T(1024)}, u32[]{:S(2)}) copy-start(f32[1024]{0:T(1024)} %copy-done.53) | copy-start | bytes 12292
  591.3 38.2 %copy-start.3 = (bf16[1024,1280]{0,1:T(8,128)(2,1)S(1)}, bf16[1024,1280]{0,1:T(8,128)(2,1)}, u32[]{:S(2)}) copy-start(bf16[1024,1280]{0,1:T(8,128)(2,1)} %copy-done.2) | copy-start | bytes 7864324
  642.1 466.8 %reduce-scatter.12.cloned.1.call-start = ((), (), s32[]{:S(2)}) async-start(), calls=%async_computation.14 | async-start | bytes 6758400 | tf_op jit(solution)/shard_map/reduce_scatter | solution.py:303
  660.5 20.6 %copy-start.50 = (f32[1024]{0:T(1024)S(1)}, f32[1024]{0:T(1024)}, u32[]{:S(2)}) copy-start(f32[1024]{0:T(1024)} %copy-done.49) | copy-start | bytes 12292
  784.6 360.6 %reduce-scatter.8.cloned.1.call-start = ((), (), s32[]{:S(2)}) async-start(), calls=%async_computation.12 | async-start | bytes 6758400 | tf_op jit(solution)/shard_map/reduce_scatter | solution.py:301
  795.5 28.5 %copy-start.1 = (bf16[1024,1280]{0,1:T(8,128)(2,1)S(1)}, bf16[1024,1280]{0,1:T(8,128)(2,1)}, u32[]{:S(2)}) copy-start(bf16[1024,1280]{0,1:T(8,128)(2,1)} %copy.60) | copy-start | bytes 7864324
  914.7 374.3 %reduce-scatter.10.cloned.1.call-start = ((), (), s32[]{:S(2)}) async-start(), calls=%async_computation.13 | async-start | bytes 6758400 | tf_op jit(solution)/shard_map/reduce_scatter | solution.py:302
  916.5 19.7 %slice-start.8 = ((s8[5242880]{0:T(1024)(128)(4,1)}), s8[4194304]{0:T(1024)(128)(4,1)S(1)}, s32[]{:S(2)}) async-start(s8[5242880]{0:T(1024)(128)(4,1)} %bitcast.270), calls=%async_computation.26 | async-start | bytes 8388608
  936.2 19.9 %slice-start = ((s8[16777216]{0:T(1024)(128)(4,1)}), s8[4194304]{0:T(1024)(128)(4,1)S(1)}, s32[]{:S(2)}) async-start(s8[16777216]{0:T(1024)(128)(4,1)} %bitcast.248), calls=%async_computation.18 | async-start | bytes 8388608
  936.2 19.9 %slice-start.1 = ((s8[16777216]{0:T(1024)(128)(4,1)}), s8[4194304]{0:T(1024)(128)(4,1)S(1)}, s32[]{:S(2)}) async-start(s8[16777216]{0:T(1024)(128)(4,1)} %bitcast.248), calls=%async_computation.19 | async-start | bytes 8388608
  1071.7 20.7 %slice-start.4 = ((s8[5242880]{0:T(1024)(128)(4,1)}), s8[4194304]{0:T(1024)(128)(4,1)S(1)}, s32[]{:S(2)}) async-start(s8[5242880]{0:T(1024)(128)(4,1)} %bitcast.266), calls=%async_computation.22 | async-start | bytes 8388608
  1071.7 20.6 %slice-start.6 = ((s8[5242880]{0:T(1024)(128)(4,1)}), s8[4194304]{0:T(1024)(128)(4,1)S(1)}, s32[]{:S(2)}) async-start(s8[5242880]{0:T(1024)(128)(4,1)} %bitcast.268), calls=%async_computation.24 | async-start | bytes 8388608
  (86 other events, 743.9 us)
Sparse Core Ops, SparseCore 0:
  10.9 61.9 all-gather.11
  75.7 58.1 all-gather.7
  136.8 58.1 all-gather.9
  197.7 58.1 all-gather.13
  258.5 58.1 all-gather.15
  319.4 58.2 all-gather.17
  422.6 144.6 reduce-scatter.17
  570.2 141.3 reduce-scatter.15
  714.5 141.3 reduce-scatter.13
  858.6 141.4 reduce-scatter.11
  1003.0 142.2 reduce-scatter.7
  1148.0 140.9 reduce-scatter.9
where the time goes:
time: 1300 us
  matrix products  668 us (51%)
  waiting for transfers between devices  267 us (21%)
  other arithmetic  224 us (17%)
  blocking collectives  84.2 us (6%)
  local copies, waits for them, and re-layouts  36.8 us (3%)
  between operations  15.8 us (1%)
    reduce_scatter x1, waiting for transfers between devices, on_device(): lax.psum_scatter(grad_totals[2], 'fsdp', scatter_dimension=1, tiled=True)  144 us
    convert_element_type x4, other arithmetic, attention_backward(): (probability * (grad_probability - centre)).astype(jnp.bfloat16)  123 us
    dot_general x12, matrix products, contract_rows(): lax.dot_general(left, right, (((0,), (0,)), ((), ())), preferred_element_...  105 us
    dot_general x4, matrix products, attention_backward(): jnp.einsum('qhd,khd->hqk', grad_rows, value_heads, preferred_element_type...  102 us
    dot_general x12, matrix products, contract_last(): lax.dot_general(left, right, (((1,), (1,)), ((), ())), preferred_element_...  92 us
    dot_general x12, matrix products, multiply(): return jnp.dot(left, right, preferred_element_type=jnp.float32)  91.9 us
    dot_general x4, matrix products, attention_backward(): jnp.einsum('hqk,qhd->khd', probability.astype(jnp.bfloat16), grad_rows, p...  72.7 us
    dot_general x4, matrix products, attention_forward(): jnp.einsum('hqk,khd->qhd', probability, value_heads, preferred_element_ty...  61.1 us
  transfers between devices with their start and end apart: 12, of which 5 were waited for; matrix products, arithmetic and copies ran while one was open for 71% of the time, Pallas kernels for 0%

commit v1 on v0

v1 whole, which is shorter than its diff:
```python
import functools
import math

import jax
import jax.numpy as jnp
from jax import lax
from jax.experimental import pallas as pl
from jax.experimental.pallas import tpu as pltpu
from jax.sharding import PartitionSpec as P

EPSILON = 1e-06
AXIS = "fsdp"
BLOCKS = 4
TILE = 256
EXTRA = 16
HEADS_PER_STEP = 4
LOW = jnp.bfloat16
LOG2E = math.log2(math.e)
LN2 = math.log(2.0)
NN = (((1,), (0,)), ((), ()))
NT = (((1,), (1,)), ((), ()))
TN = (((0,), (0,)), ((), ()))
TT = (((0,), (1,)), ((), ()))


def dot(left, right, dims):
    return lax.dot_general(left, right, dims, preferred_element_type=jnp.float32)


def three_rows(value, base, at):
    row = lax.broadcasted_iota(jnp.int32, (EXTRA, value.shape[1]), 0)
    first = value.astype(LOW).astype(jnp.float32)
    rest = value - first
    second = rest.astype(LOW).astype(jnp.float32)
    third = rest - second
    rows = jnp.where(row == at + 1, second, jnp.where(row == at + 2, third, base))
    return jnp.where(row == at, first, rows).astype(LOW)


def fold(x, op):
    return op(x.reshape(x.shape[0] // 8, 8, x.shape[1]), axis=0)


def for_each_tile(length, count_of, body):
    @pl.loop(0, length // TILE)
    def _(t):
        count = count_of(t)
        for n in range(1, length // TILE + 1):

            @pl.when(count == n)
            def _(n=n):
                body(pl.ds(pl.multiple_of(t * TILE, TILE), TILE), n)


def attention_forward_kernel(
    heads, depth, length, counts, q_ref, k_ref, v_ref, qx_ref, kx_ref, o_ref, lse_ref, kn, sb
):
    s = pl.program_id(1)
    for h in range(heads):
        kn[h] = jnp.concatenate([k_ref[h * depth : (h + 1) * depth, :], kx_ref[...]], axis=0).T

    def tile(qs, n):
        qx = qx_ref[:, qs]
        peaks = [None] * (heads + 1)
        for h in range(heads + 1):
            out = total = None
            if h > 0:
                peak = jnp.max(peaks[h - 1], axis=0, keepdims=True)
            for c in range(n):
                ks = slice(c * TILE, (c + 1) * TILE)
                if h < heads:
                    q = jnp.concatenate([q_ref[h * depth : (h + 1) * depth, qs], qx], axis=0)
                    scores = dot(kn[h, ks, :], q, NN)
                    sb[h % 2, ks, :] = scores
                    part = fold(scores, jnp.max)
                    peaks[h] = part if c == 0 else jnp.maximum(peaks[h], part)
                if h > 0:
                    p = jnp.exp2(sb[(h - 1) % 2, ks, :] - peak)
                    part = fold(p, jnp.sum)
                    total = part if c == 0 else total + part
                    part = dot(v_ref[(h - 1) * depth : h * depth, ks], p.astype(LOW), NN)
                    out = part if c == 0 else out + part
            if h > 0:
                total = jnp.sum(total, axis=0, keepdims=True)
                o_ref[(h - 1) * depth : h * depth, qs] = (out * (1.0 / total)).astype(LOW)
                lse_ref[h - 1, :, qs] = peak + jnp.log2(total)

    for_each_tile(length, lambda t: counts[s, t], tile)


def attention_forward(qkv, qx, kx, counts, depth, length):
    heads = HEADS_PER_STEP
    rows = qkv.shape[1]
    head_count, seqs = rows // depth, qkv.shape[2] // length
    group = heads * depth

    def third(i):
        return pl.BlockSpec((None, group, length), lambda h, s, counts: (i, h, s))

    extra = pl.BlockSpec((EXTRA, length), lambda h, s, counts: (0, s))
    return pl.pallas_call(
        functools.partial(attention_forward_kernel, heads, depth, length),
        grid_spec=pltpu.PrefetchScalarGridSpec(
            num_scalar_prefetch=1,
            grid=(head_count // heads, seqs),
            in_specs=[third(0), third(1), third(2), extra, extra],
            out_specs=[
                pl.BlockSpec((group, length), lambda h, s, counts: (h, s)),
                pl.BlockSpec((heads, 1, length), lambda h, s, counts: (h, 0, s)),
            ],
            scratch_shapes=[
                pltpu.VMEM((heads, length, depth + EXTRA), LOW),
                pltpu.VMEM((2, length, TILE), jnp.float32),
            ],
        ),
        out_shape=[
            jax.ShapeDtypeStruct((rows, seqs * length), LOW),
            jax.ShapeDtypeStruct((head_count, 1, seqs * length), jnp.float32),
        ],
        cost_estimate=pl.CostEstimate(
            flops=4 * head_count * 256 * length * length * seqs,
            bytes_accessed=8 * rows * seqs * length,
            transcendentals=head_count * length * length * seqs,
        ),
        name="attention_forward",
    )(counts, qkv, qkv, qkv, qx, kx)


def attention_backward_kernel(
    heads,
    depth,
    length,
    ahead,
    counts,
    q_ref,
    k_ref,
    v_ref,
    o_ref,
    do_ref,
    lse_ref,
    qx_ref,
    kx_ref,
    factor_ref,
    d_ref,
    scale_ref,
    kn,
    vn,
    dka,
    dva,
):
    s = pl.program_id(1)

    @pl.when((pl.program_id(0) == 0) & (s == 0))
    def _():
        scale_ref[...] = jnp.zeros_like(scale_ref)

    dka[...] = jnp.zeros_like(dka)
    dva[...] = jnp.zeros_like(dva)
    ones = jnp.where(lax.broadcasted_iota(jnp.int32, (EXTRA, length), 0) < 3, 1.0, 0.0).astype(LOW)
    for h in range(heads):
        hs = slice(h * depth, (h + 1) * depth)
        kn[h] = jnp.concatenate([k_ref[hs, :], kx_ref[...]], axis=0).T
        vn[h] = jnp.concatenate([v_ref[hs, :], ones], axis=0).T

    def tile(qs, n):
        base = qx_ref[:, qs].astype(jnp.float32)
        queries, grads = [], []
        items = [(h, c) for h in range(heads) for c in range(n)]

        def first(i):
            h, c = items[i]
            hs, ks = slice(h * depth, (h + 1) * depth), slice(c * TILE, (c + 1) * TILE)
            if c == 0:
                q, do, o = q_ref[hs, qs], do_ref[hs, qs], o_ref[hs, qs]
                centre = jnp.sum(
                    do.astype(jnp.float32) * o.astype(jnp.float32), axis=0, keepdims=True
                )
                queries.append(
                    jnp.concatenate([q, three_rows(-lse_ref[h, :, qs], base, 4)], axis=0)
                )
                grads.append(jnp.concatenate([do, three_rows(-centre, 0.0, 0)], axis=0))
            return dot(kn[h, ks, :], queries[h], NN), dot(vn[h, ks, :], grads[h], NN)

        pending = [first(i) for i in range(min(ahead, len(items)))]
        dq = None
        for i, (h, c) in enumerate(items):
            if i + ahead < len(items):
                pending.append(first(i + ahead))
            scores, dp = pending[i]
            pending[i] = None
            hs, ks = slice(h * depth, (h + 1) * depth), slice(c * TILE, (c + 1) * TILE)
            p = jnp.exp2(scores)
            ds = (p * dp).astype(LOW)
            dva[hs, ks] += dot(do_ref[hs, qs], p.astype(LOW), NT)
            dka[hs, ks] += dot(q_ref[hs, qs], ds, NT)
            part = dot(k_ref[hs, ks], ds, NN)
            dq = part if c == 0 else dq + part
            if c == n - 1:
                d_ref[0, hs, qs] = (dq * factor_ref[...]).astype(LOW)
                scale_ref[...] += dq * q_ref[hs, qs].astype(jnp.float32)

    for_each_tile(length, lambda t: counts[s, t], tile)
    d_ref[1] = (dka[...] * LN2).astype(LOW)
    d_ref[2] = dva[...].astype(LOW)


def attention_backward(qkv, context, grad_context, lse, qx, kx, counts, factor, depth, length, groups):
    heads = HEADS_PER_STEP
    seqs = qkv.shape[2] // length
    group = heads * depth
    start, step, count = groups

    def at(h):
        return start + h * step

    def third(i):
        return pl.BlockSpec((None, group, length), lambda h, s, counts: (i, at(h), s))

    whole = pl.BlockSpec((group, length), lambda h, s, counts: (at(h), s))
    extra = pl.BlockSpec((EXTRA, length), lambda h, s, counts: (0, s))
    return pl.pallas_call(
        functools.partial(attention_backward_kernel, heads, depth, length, 1),
        grid_spec=pltpu.PrefetchScalarGridSpec(
            num_scalar_prefetch=1,
            grid=(count, seqs),
            in_specs=[
                third(0),
                third(1),
                third(2),
                whole,
                whole,
                pl.BlockSpec((heads, 1, length), lambda h, s, counts: (at(h), 0, s)),
                extra,
                extra,
                pl.BlockSpec((depth, TILE), lambda h, s, counts: (0, 0)),
            ],
            out_specs=[
                pl.BlockSpec((3, group, length), lambda h, s, counts: (0, h, s)),
                pl.BlockSpec((depth, TILE), lambda h, s, counts: (0, 0)),
            ],
            scratch_shapes=[
                pltpu.VMEM((heads, length, depth + EXTRA), LOW),
                pltpu.VMEM((heads, length, depth + EXTRA), LOW),
                pltpu.VMEM((group, length), jnp.float32),
                pltpu.VMEM((group, length), jnp.float32),
            ],
        ),
        out_shape=[
            jax.ShapeDtypeStruct((3, count * group, seqs * length), LOW),
            jax.ShapeDtypeStruct((depth, TILE), jnp.float32),
        ],
        cost_estimate=pl.CostEstimate(
            flops=7 * count * heads * 256 * length * length * seqs,
            bytes_accessed=16 * count * group * seqs * length,
            transcendentals=count * heads * length * length * seqs,
        ),
        name="attention_backward",
    )(counts, qkv, qkv, qkv, context, grad_context, lse, qx, kx, factor)


def exchange(x, bit, n):
    return lax.ppermute(x, AXIS, [(i, i ^ bit) for i in range(n)])


def halve(x, dim, bit, n):
    mine = (lax.axis_index(AXIS) // bit) % 2
    away = lax.dynamic_index_in_dim(x, 1 - mine, dim, keepdims=False)
    keep = lax.dynamic_index_in_dim(x, mine, dim, keepdims=False)
    came = exchange(away, bit, n)
    return (keep.astype(jnp.float32) + came.astype(jnp.float32)).astype(LOW)


def planes_to_mine(x, n):
    x = halve(x, 4, 1, n)
    half = x.shape[-1] // 2
    left, right = x[..., :half], x[..., half:]
    left = halve(left, 3, 2, n)
    right = halve(right, 2, 4, n)
    left = halve(left, 2, 4, n)
    right = halve(right, 2, 2, n)
    return jnp.concatenate([left, right], axis=-1)


def scatter_all(parts, n):
    if n != 32:
        return lax.psum_scatter(jnp.stack(parts), AXIS, scatter_dimension=1, tiled=True)
    rows, width = parts[0].shape
    x = jnp.stack([p.astype(LOW) for p in parts])
    x = x.reshape(len(parts), 4, 2, 2, 2, rows // n, width)
    x = planes_to_mine(x, n)
    x = halve(x.reshape(len(parts), 2, 2, rows // n, width), 1, 16, n)
    return halve(x, 1, 8, n).astype(jnp.float32)


def scatter_half(x, parity, n):
    three, heads, depth, width = x.shape
    x = x.astype(LOW).reshape(three, 2, 2, 2, 2, depth // 2, width)
    x = planes_to_mine(x, n)
    x = halve(x, 1, 16, n)
    senders = [(i, i ^ 8) for i in range(n) if (i // 8) % 2 != parity]
    return x.astype(jnp.float32) + lax.ppermute(x, AXIS, senders).astype(jnp.float32)


def sum_all(x, n):
    if n & (n - 1):
        return lax.psum(x, AXIS)
    bit = 1
    while bit < n:
        x = x + exchange(x, bit, n)
        bit *= 2
    return x


def on_device(n, *arguments):
    (
        inputs,
        block_ids,
        cotangent,
        first_gain,
        query_weight,
        key_weight,
        value_weight,
        output_weight,
        second_gain,
        up_weight,
        down_weight,
        query_scale,
    ) = arguments
    seqs, length, width = inputs.shape
    tokens = seqs * length
    depth = query_scale.shape[0]
    shard = first_gain.shape[0]
    me = lax.axis_index(AXIS)

    gains = lax.all_gather(
        jnp.stack([first_gain, second_gain]).astype(jnp.float32), AXIS, axis=1, tiled=True
    )
    wide = jnp.stack([query_weight.T, key_weight.T, value_weight.T])
    qkv_weight = lax.all_gather(wide, AXIS, axis=1, tiled=True).reshape(3 * width, width)
    late = jnp.stack([output_weight.T, up_weight.T, down_weight.T])
    late = lax.all_gather(late, AXIS, axis=1, tiled=True)
    output_t, up_t, down_t = late[0], late[1], late[2]

    ids = block_ids.reshape(1, tokens)
    row = lax.broadcasted_iota(jnp.int32, (EXTRA, tokens), 0)
    qx = ((ids == row) & (row < BLOCKS)).astype(LOW)
    kx = jnp.where(
        row < BLOCKS, jnp.where(ids > row, -1e30, 0.0), jnp.where(row < BLOCKS + 3, 1.0, 0.0)
    ).astype(LOW)
    last = block_ids[:, TILE - 1 :: TILE]
    seen = jnp.sum(block_ids[:, None, :] <= last[:, :, None], axis=-1)
    counts = ((seen + TILE - 1) // TILE).astype(jnp.int32)

    x = inputs.reshape(tokens, width).astype(jnp.float32)
    g = cotangent.reshape(tokens, width)
    root1 = lax.rsqrt(jnp.mean(x * x, axis=-1, keepdims=True) + EPSILON)
    normed = (x * root1 * gains[0]).astype(LOW)
    factor = query_scale / math.sqrt(depth)
    heads = width // depth
    row_scale = jnp.concatenate(
        [jnp.tile(factor * LOG2E, heads), jnp.ones((2 * width,), jnp.float32)]
    )
    qkv = (dot(qkv_weight, normed, NT) * row_scale[:, None]).astype(LOW)
    qkv = qkv.reshape(3, width, tokens)
    context, lse = attention_forward(qkv, qx, kx, counts, depth, length)
    hidden = x + dot(context, output_t, TT)
    root2 = lax.rsqrt(jnp.mean(hidden * hidden, axis=-1, keepdims=True) + EPSILON)
    normed2 = (hidden * root2 * gains[1]).astype(LOW)
    upward = dot(normed2, up_t, NT)
    s = jax.nn.sigmoid(upward)
    activated = (upward * s).astype(LOW)
    output = (hidden + dot(activated, down_t, NT)).astype(LOW)

    grad_down = dot(g, activated, TN)
    grad_activated = dot(g, down_t, NN)
    grad_upward = (grad_activated * s * (1.0 + upward * (1.0 - s))).astype(LOW)
    grad_up = dot(grad_upward, normed2, TN)
    grad_normed2 = dot(grad_upward, up_t, NN)
    grad_gain2 = jnp.sum(grad_normed2 * hidden * root2, axis=0)
    w = grad_normed2 * gains[1]
    grad_hidden = (
        g.astype(jnp.float32)
        + root2 * w
        - hidden * (root2 * root2 * root2) * jnp.mean(w * hidden, axis=-1, keepdims=True)
    )
    grad_branch = grad_hidden.astype(LOW)
    grad_output = dot(grad_branch, context, (((0,), (1,)), ((), ())))
    grad_context = dot(output_t, grad_branch, TT).astype(LOW)
    late_grads = scatter_all([grad_output, grad_up, grad_down], n)

    factor_rows = jnp.broadcast_to(factor[:, None], (depth, TILE))
    pairs = []
    for parity in range(2):
        pairs.append(
            attention_backward(
                qkv, context, grad_context, lse, qx, kx, counts, factor_rows, depth, length,
                (parity, 2, heads // HEADS_PER_STEP // 2),
            )
        )
    scale_part = jnp.sum(pairs[0][1] + pairs[1][1], axis=1) / (factor * LOG2E) / math.sqrt(depth)
    weight_parts = [
        dot(d.reshape(-1, tokens), normed, NN).reshape(3, heads // 2, depth, width)
        for d, _ in pairs
    ]
    if n == 32:
        own = (me // 8) % 2
        halves = [scatter_half(part, parity, n) for parity, part in enumerate(weight_parts)]
        early_grads = jnp.where(own == 0, halves[0], halves[1])
    else:
        both = [p.reshape(3, 2, 1, -1, width) for p in weight_parts]
        both = jnp.concatenate(both, axis=2).reshape(3, width, width)
        early_grads = lax.psum_scatter(both, AXIS, scatter_dimension=1, tiled=True)

    weight = qkv_weight.reshape(3, 2, 2, -1, width)
    grad_normed = sum(
        dot(d.reshape(-1, tokens), weight[:, :, parity].reshape(-1, width), TN)
        for parity, (d, _) in enumerate(pairs)
    )
    grad_gain1 = jnp.sum(grad_normed * x * root1, axis=0)
    w = grad_normed * gains[0]
    grad_inputs = (
        grad_hidden
        + root1 * w
        - x * (root1 * root1 * root1) * jnp.mean(w * x, axis=-1, keepdims=True)
    )
    small = jnp.concatenate([grad_gain1, grad_gain2, scale_part])
    small = sum_all(small, n)
    gain1 = lax.dynamic_slice_in_dim(small, me * shard, shard)
    gain2 = lax.dynamic_slice_in_dim(small, width + me * shard, shard)
    scale_total = small[2 * width :]

    return (
        output.reshape(seqs, length, width),
        grad_inputs.reshape(seqs, length, width),
        gain1,
        early_grads[0].T,
        early_grads[1].T,
        early_grads[2].T,
        late_grads[0].T,
        gain2,
        late_grads[1].T,
        late_grads[2].T,
        scale_total,
    )


def solution(mesh):
    rows, columns = P(AXIS), P(None, AXIS)
    in_specs = (rows, rows, rows, rows, *[columns] * 4, rows, columns, columns, P())
    out_specs = (rows, rows, rows, *[columns] * 4, rows, columns, columns, P())
    return jax.shard_map(
        functools.partial(on_device, mesh.shape[AXIS]),
        mesh=mesh,
        in_specs=in_specs,
        out_specs=out_specs,
        check_vma=False,
    )
```

time: 1300 us -> 640 us (0.49)
  matrix products: 668 us -> 214 us
  other arithmetic: 224 us -> 50.7 us
  waiting for transfers between devices: 267 us -> 128 us
  Pallas kernels: 0 us -> 133 us
  blocking collectives: 84.2 us -> 43.3 us
  starting transfers between devices: 1.3 us -> 21.5 us
    dot_general x60 -> x14, matrix products: 668 us -> 214 us  [dot(): lax.dot_general(left, right, dims, preferred_element_type=jnp.float32)]
    reduce_scatter x6 -> x0, waiting for transfers between devices: 180 us -> none  [the longest x1 144 us: on_device(): lax.psum_scatter(grad_totals[2], 'fsdp', scatter_dimension=1, tiled=True)]
    pallas_call x0 -> x3, Pallas kernels: none -> 133 us  [the longest x2 85.1 us: attention_backward(): pl.pallas_call(functools.partial(attention_backward_kernel, heads, depth,...]
    convert_element_type x4 -> x22, other arithmetic: 123 us -> 18 us  [the longest x18 10 us: halve(): return (keep.astype(jnp.float32) + came.astype(jnp.float32)).astype(LOW)]
    ppermute x0 -> x26, waiting for transfers between devices: none -> 91.2 us  [the longest x24 91.2 us: exchange(): return lax.ppermute(x, AXIS, [(i, i ^ bit) for i in range(n)])]
    reduce_sum x7 -> x3, other arithmetic: 69.2 us -> 3.91 us  [the longest x1 3.58 us: on_device(): root1 = lax.rsqrt(jnp.mean(x * x, axis=-1, keepdims=True) + EPSILON)]
    all_gather x6 -> x2, waiting for transfers between devices: 82.9 us -> 36.8 us  [the longest x1 27.1 us: on_device(): lax.all_gather(wide, AXIS, axis=1, tiled=True).reshape(3 * width, width)]
    unnamed x1 -> x0, blocking collectives: 41.1 us -> none
  transfers between devices with their start and end apart: 12 -> 28, of which waited for: 5 -> 14; matrix products, arithmetic and copies ran while one was open for 71% -> 26% of each run, Pallas kernels for 0% -> 8%
where the time goes in v1:
time: 640 us; the launch traced here: 637 us
  matrix products  214 us (33%)
  Pallas kernels  133 us (21%)
  waiting for transfers between devices  128 us (20%)
  other arithmetic  50.7 us (8%)
  blocking collectives  43.3 us (7%)
  local copies, waits for them, and re-layouts  30.8 us (5%)
  starting transfers between devices  21.5 us (3%)
  between operations  15.2 us (2%)
    dot_general x14, matrix products, dot(): lax.dot_general(left, right, dims, preferred_element_type=jnp.float32)  214 us
    ppermute x24, waiting for transfers between devices, exchange(): return lax.ppermute(x, AXIS, [(i, i ^ bit) for i in range(n)])  91.2 us
    pallas_call x2, Pallas kernels, attention_backward(): pl.pallas_call(functools.partial(attention_backward_kernel, heads, depth,...  85.1 us
    pallas_call x1, Pallas kernels, attention_forward(): pl.pallas_call(functools.partial(attention_forward_kernel, heads, depth,...  48.1 us
    all_gather x1, blocking collectives, on_device(): lax.all_gather(jnp.stack([first_gain, second_gain]).astype(jnp.float32),...  43.3 us
    all_gather x1, waiting for transfers between devices, on_device(): lax.all_gather(wide, AXIS, axis=1, tiled=True).reshape(3 * width, width)  27.1 us
    ppermute x24, starting transfers between devices, exchange(): return lax.ppermute(x, AXIS, [(i, i ^ bit) for i in range(n)])  18 us
  transfers between devices with their start and end apart: 28, of which 14 were waited for; matrix products, arithmetic and copies ran while one was open for 26% of the time, Pallas kernels for 8%

profile of v1, /device:TPU:0, one launch (start us, length us, event | category | flops | bytes accessed | tf_op | source)
XLA Modules:
  0.0 636.8 jit_solution(1644385409513578028)
XLA Ops:
  18.0 43.3 %all-gather = f32[32,40,2]{1,2,0:T(2,128)S(1)} all-gather(f32[1,40,2]{1,2,0:T(2,128)S(1)} %convert_bitcast_fusion), channel_id=1, replica_groups=mesh['fsdp'=32] {'fsdp'}, dimensions={0}, use_global_device_ids=true | all-gather | bytes 10560 | tf_op jit(solution)/shard_map/all_gather | solution.py:335
  64.3 6.5 %fusion.4 = bf16[2,1024,1280]{2,1,0:T(8,128)(2,1)} fusion(bf16[2,1024,1280]{2,1,0:T(8,128)(2,1)} %param.12, f32[1280]{0:T(1024)S(1)} %get-tuple-element.28, f32[2,1024]{1,0:T(2,128)S(1)} %get-tuple-element.52), kind=kLoop, calls=%fused_computation.12 | loop fusion | flops 10485760 | bytes 10499072 | tf_op jit(solution)/shard_map/convert_element_type | solution.py:357
  70.8 27.1 %all-gather.4.cloned.1.call-done = bf16[3,1280,1280]{2,1,0:T(8,128)(2,1)} async-done(((bf16[3,40,1280]{2,1,0:T(8,128)(2,1)}), bf16[3,1280,1280]{2,1,0:T(8,128)(2,1)}) %all-gather.4.cloned.1.call-update) | async-done | bytes 9830416 | tf_op jit(solution)/shard_map/all_gather | solution.py:339
  97.9 27.6 %multiply_convert_fusion = bf16[3840,2048]{1,0:T(8,128)(2,1)} fusion(bf16[3840,1280]{1,0:T(8,128)(2,1)} %bitcast.254, bf16[2048,1280]{1,0:T(8,128)(2,1)} %bitcast.256, f32[3840]{0:T(1024)S(1)} %concatenate.16), kind=kOutput, calls=%fused_computation | convolution fusion | flops 20148387840 | bytes 30817280 | tf_op jit(solution)/shard_map/dot_general | solution.py:27
  125.5 48.1 %attention_forward.1 = (bf16[1280,2048]{1,0:T(8,128)(2,1)}, f32[16,1,2048]{2,1,0:T(1,128)}) custom-call(s32[2,4]{1,0:T(2,128)} %and_select_fusion.counts, bf16[3,1280,2048]{2,1,0:T(8,128)(2,1)} %bitcast.289, bf16[3,1280,2048]{2,1,0:T(8,128)(2,1)} %bitcast.290, bf16[3,1280,2048]{2,1,0:T(8,128)(2,1)} %bitcast.291, bf16[16,2048]{1,0:T(8,128)(2,1)} %fusion.43.qx_ref, ...), custom_call_target="tpu_custom_call" | custom-call | flops 34359738368 | bytes 20971520 | tf_op jit(solution)/shard_map/attention_forward/pallas_call | solution.py:101
  173.6 9.6 %all-gather.6.cloned.1.call-done = bf16[3,1280,1280]{2,1,0:T(8,128)(2,1)} async-done(((bf16[3,40,1280]{2,1,0:T(8,128)(2,1)}), bf16[3,1280,1280]{2,1,0:T(8,128)(2,1)}) %all-gather.6.cloned.1.call-update) | async-done | bytes 9830416 | tf_op jit(solution)/shard_map/all_gather | solution.py:341
  183.2 11.1 %multiply_reduce_fusion.2 = (f32[2048]{0:T(1024)S(1)}, f32[2048,1280]{1,0:T(8,128)S(1)}) fusion(bf16[1280,2048]{1,0:T(8,128)(2,1)} %get-tuple-element.17.o_ref, bf16[3,1280,1280]{2,1,0:T(8,128)(2,1)} %all-gather.6.cloned.1.call-done, bf16[2,1024,1280]{2,1,0:T(8,128)(2,1)} %param.12), kind=kOutput, calls=%fused_computation.25 | convolution fusion | flops 6721370112 | bytes 24256512 | tf_op jit(solution)/shard_map/dot_general | solution.py:27
  194.3 15.1 %fusion.14 = f32[2048,1280]{1,0:T(8,128)} fusion(bf16[3,1280,1280]{2,1,0:T(8,128)(2,1)} %all-gather.6.cloned.1.call-done, f32[2048,1280]{1,0:T(8,128)S(1)} %get-tuple-element.58, f32[1280]{0:T(1024)S(1)} %get-tuple-element.27, f32[2048]{0:T(1024)S(1)} %get-tuple-element.54), kind=kOutput, calls=%fused_computation.45 | convolution fusion | flops 6718750720 | bytes 24261632 | tf_op jit(solution)/shard_map/dot_general | solution.py:27
  209.4 13.8 %convolution_convert_fusion.1 = bf16[1280,1280]{0,1:T(8,128)(2,1)} fusion(bf16[2048,1280]{1,0:T(8,128)(2,1)} %bitcast.261, f32[2048,1280]{1,0:T(8,128)} %fusion.14), kind=kOutput, calls=%fused_computation.31 | convolution fusion | flops 6725632000 | bytes 19005440 | tf_op jit(solution)/shard_map/dot_general | solution.py:27
  223.2 12.4 %fusion.1 = bf16[2048,1280]{1,0:T(8,128)(2,1)S(1)} fusion(f32[2048,1280]{1,0:T(8,128)} %fusion.14, bf16[2048,1280]{1,0:T(8,128)(2,1)S(1)} %bitcast.264, bf16[3,1280,1280]{2,1,0:T(8,128)(2,1)} %all-gather.6.cloned.1.call-done), kind=kOutput, calls=%fused_computation.3 | convolution fusion | flops 6734479360 | bytes 24248320 | tf_op jit(solution)/shard_map/dot_general | solution.py:27
  235.6 10.2 %convolution_convert_fusion.2 = bf16[1280,1280]{1,0:T(8,128)(2,1)} fusion(bf16[2048,1280]{1,0:T(8,128)(2,1)S(1)} %fusion.1, f32[2048,1280]{1,0:T(8,128)S(1)} %get-tuple-element.58, f32[1280]{0:T(1024)S(1)} %get-tuple-element.27, f32[2048]{0:T(1024)S(1)} %get-tuple-element.54), kind=kOutput, calls=%fused_computation.32 | convolution fusion | flops 6720389120 | bytes 19018752 | tf_op jit(solution)/shard_map/dot_general | solution.py:27
  245.8 12.8 %multiply_reduce_fusion = (f32[1280]{0:T(1024)}, f32[2048]{0:T(1024)S(1)}, f32[2048,1280]{1,0:T(8,128)}) fusion(f32[2048,1280]{1,0:T(8,128)S(1)} %get-tuple-element.58, f32[2048]{0:T(1024)S(1)} %get-tuple-element.54, f32[1280]{0:T(1024)S(1)} %get-tuple-element.27, bf16[2048,1280]{1,0:T(8,128)(2,1)S(1)} %fusion.1, ...), kind=kOutput, calls=%fused_computation.18 | convolution fusion | flops 6726611968 | bytes 29517824 | tf_op jit(solution)/shard_map/dot_general | solution.py:27
  258.6 7.2 %multiply_subtract_fusion = f32[2048,1280]{1,0:T(8,128)S(1)} fusion(f32[2048,1280]{1,0:T(8,128)S(1)} %get-tuple-element.58, f32[2048,1280]{1,0:T(8,128)} %get-tuple-element.59, f32[2048]{0:T(1024)S(1)} %broadcast_multiply_fusion.1, f32[2048]{0:T(1024)S(1)} %get-tuple-element.53, f32[1280]{0:T(1024)S(1)} %get-tuple-element.27, ...), kind=kLoop, calls=%fused_computation.19 | loop fusion | flops 18350080 | bytes 36729856 | tf_op jit(solution)/shard_map/sub | solution.py:382
  265.8 14.7 %convolution_convert_fusion.3 = bf16[1280,1280]{1,0:T(8,128)(2,1)} fusion(bf16[1280,2048]{1,0:T(8,128)(2,1)} %get-tuple-element.17.o_ref, f32[2048,1280]{1,0:T(8,128)S(1)} %multiply_subtract_fusion), kind=kOutput, calls=%fused_computation.33 | convolution fusion | flops 6715146240 | bytes 19005440 | tf_op jit(solution)/shard_map/dot_general | solution.py:27
  280.5 11.2 %convolution_convert_fusion.do_ref = bf16[1280,2048]{1,0:T(8,128)(2,1)} fusion(bf16[3,1280,1280]{2,1,0:T(8,128)(2,1)} %all-gather.6.cloned.1.call-done, f32[2048,1280]{1,0:T(8,128)S(1)} %multiply_subtract_fusion), kind=kOutput, calls=%fused_computation.30 | convolution fusion | flops 6716129280 | bytes 19005440 | tf_op jit(solution)/shard_map/dot_general | solution.py:27
  292.4 42.5 %attention_backward.3 = (bf16[3,640,2048]{2,1,0:T(8,128)(2,1)}, f32[80,256]{1,0:T(8,128)}) custom-call(s32[2,4]{1,0:T(2,128)} %and_select_fusion.counts, bf16[3,1280,2048]{2,1,0:T(8,128)(2,1)} %bitcast.292, bf16[3,1280,2048]{2,1,0:T(8,128)(2,1)} %bitcast.293, bf16[3,1280,2048]{2,1,0:T(8,128)(2,1)} %bitcast.294, bf16[1280,2048]{1,0:T(8,128)(2,1)} %get-tuple-element.17.o_ref, ...), custom_call_target="tpu_custom_call" | custom-call | flops 30064771072 | bytes 20971520 | tf_op jit(solution)/shard_map/attention_backward/pallas_call | solution.py:221
  334.9 42.6 %attention_backward.2 = (bf16[3,640,2048]{2,1,0:T(8,128)(2,1)}, f32[80,256]{1,0:T(8,128)}) custom-call(s32[2,4]{1,0:T(2,128)} %and_select_fusion.counts, bf16[3,1280,2048]{2,1,0:T(8,128)(2,1)} %bitcast.295, bf16[3,1280,2048]{2,1,0:T(8,128)(2,1)} %bitcast.296, bf16[3,1280,2048]{2,1,0:T(8,128)(2,1)} %bitcast.297, bf16[1280,2048]{1,0:T(8,128)(2,1)} %get-tuple-element.17.o_ref, ...), custom_call_target="tpu_custom_call" | custom-call | flops 30064771072 | bytes 20971520 | tf_op jit(solution)/shard_map/attention_backward/pallas_call | solution.py:221
  377.5 8.4 %fusion.45 = (bf16[3,2,1,320,1280]{4,3,2,1,0:T(8,128)(2,1)}, bf16[3,2,1,320,1280]{4,3,2,1,0:T(8,128)(2,1)}) fusion(bf16[3,2,2,320,1280]{4,3,2,1,0:T(8,128)(2,1)} %bitcast.255), kind=kLoop, calls=%fused_computation.161 | loop fusion | bytes 19660800 | tf_op jit(solution)/shard_map/slice | solution.py:416
  392.8 21.0 %fusion.50 = f32[2048,1280]{1,0:T(8,128)} fusion(bf16[1920,2048]{1,0:T(8,128)(2,1)} %bitcast.300, bf16[1920,1280]{1,0:T(8,128)(2,1)} %bitcast.268), kind=kOutput, calls=%fused_computation.166 | convolution fusion | flops 10066329600 | bytes 23265280 | tf_op jit(solution)/shard_map/dot_general | solution.py:27
  413.9 20.8 %fusion.9 = (f32[1280]{0:T(1024)S(1)}, f32[2048]{0:T(1024)S(1)}, f32[2048,1280]{1,0:T(8,128)}) fusion(bf16[2,1024,1280]{2,1,0:T(8,128)(2,1)S(1)} %bitcast.250, f32[2048]{0:T(1024)S(1)} %bitcast.285, f32[1280]{0:T(1024)S(1)} %copy-done.8, f32[2048,1280]{1,0:T(8,128)} %fusion.50, bf16[1920,2048]{1,0:T(8,128)(2,1)} %bitcast.298, bf16[1920,1280]{1,0:T(8,128)(2,1)} %bitcast.267), kind=kOutput, calls=%fused_computation.17 | convolution fusion | flops 10087298048 | bytes 39020544 | tf_op jit(solution)/shard_map/dot_general | solution.py:27
  434.8 14.2 %convolution_convert_fusion.5 = bf16[3,8,80,1280]{3,2,1,0:T(8,128)(2,1)} fusion(bf16[3,8,80,2048]{3,2,1,0:T(8,128)(2,1)} %bitcast.301, bf16[2048,1280,1,1]{1,0,3,2:T(8,128)(2,1)S(1)} %bitcast.259), kind=kOutput, calls=%fused_computation.35 | convolution fusion | flops 10068787200 | bytes 18022400 | tf_op jit(solution)/shard_map/dot_general | solution.py:27
  449.0 14.4 %convolution_convert_fusion.4 = bf16[3,8,80,1280]{3,2,1,0:T(8,128)(2,1)} fusion(bf16[3,8,80,2048]{3,2,1,0:T(8,128)(2,1)} %bitcast.299, bf16[2048,1280,1,1]{1,0,3,2:T(8,128)(2,1)S(1)} %bitcast.260), kind=kOutput, calls=%fused_computation.34 | convolution fusion | flops 10068787200 | bytes 18022400 | tf_op jit(solution)/shard_map/dot_general | solution.py:27
  464.9 6.1 constant_dynamic-slice_fusion.3
  476.4 15.0 %add_convert_fusion = bf16[2048,1280]{1,0:T(8,128)(2,1)} fusion(f32[2048,1280]{1,0:T(8,128)} %copy-done.2, bf16[3,1280,1280]{2,1,0:T(8,128)(2,1)} %all-gather.6.cloned.1.call-done, f32[2048,1280]{1,0:T(8,128)} %fusion.14), kind=kOutput, calls=%fused_computation.21 | convolution fusion | flops 6729236480 | bytes 29491200 | tf_op jit(solution)/shard_map/dot_general | solution.py:27
  496.9 11.5 %fusion.6 = f32[2048,1280]{1,0:T(8,128)} fusion(bf16[2,1024,1280]{2,1,0:T(8,128)(2,1)S(1)} %bitcast.250, f32[2048,1280]{1,0:T(8,128)} %copy-done, f32[2048,1280]{1,0:T(8,128)} %get-tuple-element.60, f32[2048]{0:T(1024)S(1)} %broadcast_multiply_fusion, f32[2048]{0:T(1024)S(1)} %copy-done.12, f32[1280]{0:T(1024)S(1)} %copy-done.8, f32[2048]{0:T(1024)S(1)} %bitcast.286), kind=kLoop, calls=%fused_computation.14 | loop fusion | flops 18350080 | bytes 36729856 | tf_op jit(solution)/shard_map/sub | solution.py:422
  516.8 11.5 %collective-permute-done.6 = bf16[3,2,2,40,640]{4,3,0,1,2:T(8,128)(2,1)S(1)} collective-permute-done((bf16[3,2,2,40,640]{4,3,0,1,2:T(8,128)(2,1)S(1)}, bf16[3,2,2,40,640]{4,3,0,1,2:T(8,128)(2,1)S(1)}, u32[]{:S(2)}, u32[]{:S(2)}) %collective-permute-start.6) | collective-permute-done | bytes 614432 | tf_op jit(solution)/shard_map/ppermute | solution.py:262
  530.9 10.6 %collective-permute-done.13 = bf16[3,2,2,40,640]{4,3,0,1,2:T(8,128)(2,1)S(1)} collective-permute-done((bf16[3,2,2,40,640]{4,3,0,1,2:T(8,128)(2,1)S(1)}, bf16[3,2,2,40,640]{4,3,0,1,2:T(8,128)(2,1)S(1)}, u32[]{:S(2)}, u32[]{:S(2)}) %collective-permute-start.13) | collective-permute-done | bytes 614432 | tf_op jit(solution)/shard_map/ppermute | solution.py:262
  559.1 12.3 %collective-permute-done.10 = bf16[3,40,1280]{2,1,0:T(8,128)(2,1)} collective-permute-done((bf16[3,40,1280]{2,1,0:T(8,128)(2,1)S(1)}, bf16[3,40,1280]{2,1,0:T(8,128)(2,1)}, u32[]{:S(2)}, u32[]{:S(2)}) %collective-permute-start.10) | collective-permute-done | bytes 307232 | tf_op jit(solution)/shard_map/ppermute | solution.py:262
  573.8 7.6 %collective-permute-done.22 = bf16[3,4,2,40,640]{4,3,2,1,0:T(8,128)(2,1)S(1)} collective-permute-done((bf16[3,4,2,40,640]{4,3,2,1,0:T(8,128)(2,1)S(1)}, bf16[3,4,2,40,640]{4,3,2,1,0:T(8,128)(2,1)S(1)}, u32[]{:S(2)}, u32[]{:S(2)}) %collective-permute-start.22) | collective-permute-done | bytes 1228832 | tf_op jit(solution)/shard_map/ppermute | solution.py:262
  587.0 6.8 %collective-permute-done.23 = bf16[3,4,40,640]{3,2,1,0:T(8,128)(2,1)S(1)} collective-permute-done((bf16[3,4,40,640]{3,2,1,0:T(8,128)(2,1)S(1)}, bf16[3,4,40,640]{3,2,1,0:T(8,128)(2,1)S(1)}, u32[]{:S(2)}, u32[]{:S(2)}) %collective-permute-start.23) | collective-permute-done | bytes 614432 | tf_op jit(solution)/shard_map/ppermute | solution.py:262
  597.9 21.5 %collective-permute-done.24 = bf16[3,2,40,1280]{3,2,0,1:T(8,128)(2,1)S(1)} collective-permute-done((bf16[3,2,40,1280]{3,2,0,1:T(8,128)(2,1)S(1)}, bf16[3,2,40,1280]{3,2,0,1:T(8,128)(2,1)S(1)}, u32[]{:S(2)}, u32[]{:S(2)}) %collective-permute-start.24) | collective-permute-done | bytes 614432 | tf_op jit(solution)/shard_map/ppermute | solution.py:262
  620.5 8.3 %collective-permute-done.25 = bf16[3,40,1280]{2,1,0:T(8,128)(2,1)S(1)} collective-permute-done((bf16[3,40,1280]{2,1,0:T(8,128)(2,1)S(1)}, bf16[3,40,1280]{2,1,0:T(8,128)(2,1)S(1)}, u32[]{:S(2)}, u32[]{:S(2)}) %collective-permute-start.25) | collective-permute-done | bytes 307232 | tf_op jit(solution)/shard_map/ppermute | solution.py:262
  (189 shorter events, 75.9 us)
Async XLA Ops:
  7.2 54.3 %copy-start.9 = (s32[2,1024]{1,0:T(2,128)S(1)}, s32[2,1024]{1,0:T(2,128)}, u32[]{:S(2)}) copy-start(s32[2,1024]{1,0:T(2,128)} %param.13) | copy-start | bytes 24580
  7.2 90.7 %all-gather.4.cloned.1.call-start = ((), (), s32[]{:S(2)}) async-start(), calls=%async_computation | async-start | bytes 10137600 | tf_op jit(solution)/shard_map/all_gather | solution.py:339
  9.0 174.2 %all-gather.6.cloned.1.call-start = ((), (), s32[]{:S(2)}) async-start(), calls=%async_computation.1 | async-start | bytes 10137600 | tf_op jit(solution)/shard_map/all_gather | solution.py:341
  194.3 64.3 %copy-start.2 = (f32[2048,1280]{1,0:T(8,128)}, f32[2048,1280]{1,0:T(8,128)S(1)}, u32[]{:S(2)}) copy-start(f32[2048,1280]{1,0:T(8,128)S(1)} %get-tuple-element.58) | copy-start | bytes 31457284
  392.6 157.9 %collective-permute-start.19 = (bf16[3,4,2,2,40,1280]{5,4,3,2,1,0:T(8,128)(2,1)}, bf16[3,4,2,2,40,1280]{5,4,3,2,1,0:T(8,128)(2,1)}, u32[]{:S(2)}, u32[]{:S(2)}) collective-permute-start(bf16[3,4,2,2,40,1280]{5,4,3,2,1,0:T(8,128)(2,1)} %dynamic-slice_bitcast_fusion), channel_id=1, source_target_pairs={{0,1},{1,0},{2,3},{3,2},{4,5},{5,4},{6,7},{7,6},{8,9},{9,8},{10,11... | collective-permute-start | bytes 14745608 | tf_op jit(solution)/shard_map/ppermute | solution.py:262
  392.8 41.9 %slice-start.5 = ((s8[5242880]{0:T(1024)(128)(4,1)}), s8[4194304]{0:T(1024)(128)(4,1)S(1)}, s32[]{:S(2)}) async-start(s8[5242880]{0:T(1024)(128)(4,1)} %bitcast.257), calls=%async_computation.7 | async-start | bytes 8388608
  434.7 28.7 %collective-permute-start = (f32[2640]{0:T(1024)S(1)}, f32[2640]{0:T(1024)S(1)}, u32[]{:S(2)}, u32[]{:S(2)}) collective-permute-start(f32[2640]{0:T(1024)S(1)} %pad_maximum_fusion.4), channel_id=1, source_target_pairs={{0,1},{1,0},{2,3},{3,2},{4,5},{5,4},{6,7},{7,6},{8,9},{9,8},{10,11... | collective-permute-start | bytes 31688 | tf_op jit(solution)/shard_map/ppermute | solution.py:262
  463.4 12.9 %collective-permute-start.1 = (f32[2640]{0:T(1024)S(1)}, f32[2640]{0:T(1024)S(1)}, u32[]{:S(2)}, u32[]{:S(2)}) collective-permute-start(f32[2640]{0:T(1024)S(1)} %fusion.67), channel_id=1, source_target_pairs={{0,2},{1,3},{2,0},{3,1},{4,6},{5,7},{6,4},{7,5},{8,10},{9,11},{10,... | collective-permute-start | bytes 31688 | tf_op jit(solution)/shard_map/ppermute | solution.py:262
  475.8 33.1 %collective-permute-start.5 = (bf16[3,2,2,2,40,1280]{5,4,0,1,3,2:T(8,128)(2,1)}, bf16[3,2,2,2,40,1280]{5,4,0,1,3,2:T(8,128)(2,1)}, u32[]{:S(2)}, u32[]{:S(2)}) collective-permute-start(bf16[3,2,2,2,40,1280]{5,4,0,1,3,2:T(8,128)(2,1)} %bitcast.245), channel_id=1, source_target_pairs={{0,1},{1,0},{2,3},{3,2},{4,5},{5,4},{6,7},{7,6},{8,9},{9,8},{10,11... | collective-permute-start | bytes 7372808 | tf_op jit(solution)/shard_map/ppermute | solution.py:262
  476.0 37.7 %collective-permute-start.12 = (bf16[3,2,2,2,40,1280]{5,4,0,1,3,2:T(8,128)(2,1)}, bf16[3,2,2,2,40,1280]{5,4,0,1,3,2:T(8,128)(2,1)S(1)}, u32[]{:S(2)}, u32[]{:S(2)}) collective-permute-start(bf16[3,2,2,2,40,1280]{5,4,0,1,3,2:T(8,128)(2,1)} %bitcast.244), channel_id=1, source_target_pairs={{0,1},{1,0},{2,3},{3,2},{4,5},{5,4},{6,7},{7,6},{8,9},{9,8},{10,11... | collective-permute-start | bytes 7372808 | tf_op jit(solution)/shard_map/ppermute | solution.py:262
  476.3 15.1 %collective-permute-start.2 = (f32[2640]{0:T(1024)S(1)}, f32[2640]{0:T(1024)S(1)}, u32[]{:S(2)}, u32[]{:S(2)}) collective-permute-start(f32[2640]{0:T(1024)S(1)} %add.261), channel_id=1, source_target_pairs={{0,4},{1,5},{2,6},{3,7},{4,0},{5,1},{6,2},{7,3},{8,12},{9,13},{10,... | collective-permute-start | bytes 31688 | tf_op jit(solution)/shard_map/ppermute | solution.py:262
  491.4 3.8 collective-permute-start.3
  495.1 13.2 %collective-permute-start.4 = (f32[2640]{0:T(1024)S(1)}, f32[2640]{0:T(1024)S(1)}, u32[]{:S(2)}, u32[]{:S(2)}) collective-permute-start(f32[2640]{0:T(1024)S(1)} %add.263), channel_id=1, source_target_pairs={{0,16},{1,17},{2,18},{3,19},{4,20},{5,21},{6,22},{7,23},{8,24},{9,... | collective-permute-start | bytes 31688 | tf_op jit(solution)/shard_map/ppermute | solution.py:262
  511.5 16.9 %collective-permute-start.6 = (bf16[3,2,2,40,640]{4,3,0,1,2:T(8,128)(2,1)S(1)}, bf16[3,2,2,40,640]{4,3,0,1,2:T(8,128)(2,1)S(1)}, u32[]{:S(2)}, u32[]{:S(2)}) collective-permute-start(bf16[3,2,2,40,640]{4,3,0,1,2:T(8,128)(2,1)S(1)} %dynamic-slice_bitcast_fusion.8), channel_id=1, source_target_pairs={{0,2},{1,3},{2,0},{3,1},{4,6},{5,7},{6,4},{7,5},{8,10},{9,11},{10,... | collective-permute-start | bytes 1843208 | tf_op jit(solution)/shard_map/ppermute | solution.py:262
  513.6 16.9 %collective-permute-start.8 = (bf16[3,2,2,40,640]{4,3,0,1,2:T(8,128)(2,1)S(1)}, bf16[3,2,2,40,640]{4,3,0,1,2:T(8,128)(2,1)S(1)}, u32[]{:S(2)}, u32[]{:S(2)}) collective-permute-start(bf16[3,2,2,40,640]{4,3,0,1,2:T(8,128)(2,1)S(1)} %dynamic-slice_bitcast_fusion.7), channel_id=1, source_target_pairs={{0,4},{1,5},{2,6},{3,7},{4,0},{5,1},{6,2},{7,3},{8,12},{9,13},{10,... | collective-permute-start | bytes 1843208 | tf_op jit(solution)/shard_map/ppermute | solution.py:262
  513.7 36.8 %slice-start.2 = ((s8[9830400]{0:T(1024)(128)(4,1)}), s8[4194304]{0:T(1024)(128)(4,1)S(1)}, s32[]{:S(2)}) async-start(s8[9830400]{0:T(1024)(128)(4,1)} %bitcast.251), calls=%async_computation.4 | async-start | bytes 8388608
  514.6 26.9 %collective-permute-start.13 = (bf16[3,2,2,40,640]{4,3,0,1,2:T(8,128)(2,1)S(1)}, bf16[3,2,2,40,640]{4,3,0,1,2:T(8,128)(2,1)S(1)}, u32[]{:S(2)}, u32[]{:S(2)}) collective-permute-start(bf16[3,2,2,40,640]{4,3,0,1,2:T(8,128)(2,1)S(1)} %dynamic-slice_bitcast_fusion.6), channel_id=1, source_target_pairs={{0,2},{1,3},{2,0},{3,1},{4,6},{5,7},{6,4},{7,5},{8,10},{9,11},{10,... | collective-permute-start | bytes 1843208 | tf_op jit(solution)/shard_map/ppermute | solution.py:262
  515.0 28.6 %collective-permute-start.15 = (bf16[3,2,2,40,640]{4,3,0,1,2:T(8,128)(2,1)S(1)}, bf16[3,2,2,40,640]{4,3,0,1,2:T(8,128)(2,1)S(1)}, u32[]{:S(2)}, u32[]{:S(2)}) collective-permute-start(bf16[3,2,2,40,640]{4,3,0,1,2:T(8,128)(2,1)S(1)} %dynamic-slice_bitcast_fusion.5), channel_id=1, source_target_pairs={{0,4},{1,5},{2,6},{3,7},{4,0},{5,1},{6,2},{7,3},{8,12},{9,13},{10,... | collective-permute-start | bytes 1843208 | tf_op jit(solution)/shard_map/ppermute | solution.py:262
  528.6 21.7 %collective-permute-start.7 = (bf16[3,2,40,640]{3,2,0,1:T(8,128)(2,1)S(1)}, bf16[3,2,40,640]{3,2,0,1:T(8,128)(2,1)S(1)}, u32[]{:S(2)}, u32[]{:S(2)}) collective-permute-start(bf16[3,2,40,640]{3,2,0,1:T(8,128)(2,1)S(1)} %dynamic-slice_bitcast_fusion.13), channel_id=1, source_target_pairs={{0,4},{1,5},{2,6},{3,7},{4,0},{5,1},{6,2},{7,3},{8,12},{9,13},{10,... | collective-permute-start | bytes 921608 | tf_op jit(solution)/shard_map/ppermute | solution.py:262
  530.7 19.6 %collective-permute-start.9 = (bf16[3,2,40,640]{3,2,0,1:T(8,128)(2,1)S(1)}, bf16[3,2,40,640]{3,2,0,1:T(8,128)(2,1)S(1)}, u32[]{:S(2)}, u32[]{:S(2)}) collective-permute-start(bf16[3,2,40,640]{3,2,0,1:T(8,128)(2,1)S(1)} %dynamic-slice_bitcast_fusion.12), channel_id=1, source_target_pairs={{0,2},{1,3},{2,0},{3,1},{4,6},{5,7},{6,4},{7,5},{8,10},{9,11},{10,... | collective-permute-start | bytes 921608 | tf_op jit(solution)/shard_map/ppermute | solution.py:262
  542.4 14.6 %collective-permute-start.14 = (bf16[3,2,40,640]{3,2,0,1:T(8,128)(2,1)}, bf16[3,2,40,640]{3,2,0,1:T(8,128)(2,1)S(1)}, u32[]{:S(2)}, u32[]{:S(2)}) collective-permute-start(bf16[3,2,40,640]{3,2,0,1:T(8,128)(2,1)} %dynamic-slice_bitcast_fusion.11), channel_id=1, source_target_pairs={{0,4},{1,5},{2,6},{3,7},{4,0},{5,1},{6,2},{7,3},{8,12},{9,13},{10,... | collective-permute-start | bytes 921608 | tf_op jit(solution)/shard_map/ppermute | solution.py:262
  543.8 15.1 %collective-permute-start.16 = (bf16[3,2,40,640]{3,2,0,1:T(8,128)(2,1)S(1)}, bf16[3,2,40,640]{3,2,0,1:T(8,128)(2,1)S(1)}, u32[]{:S(2)}, u32[]{:S(2)}) collective-permute-start(bf16[3,2,40,640]{3,2,0,1:T(8,128)(2,1)S(1)} %dynamic-slice_bitcast_fusion.10), channel_id=1, source_target_pairs={{0,2},{1,3},{2,0},{3,1},{4,6},{5,7},{6,4},{7,5},{8,10},{9,11},{10,... | collective-permute-start | bytes 921608 | tf_op jit(solution)/shard_map/ppermute | solution.py:262
  550.5 21.0 %collective-permute-start.10 = (bf16[3,40,1280]{2,1,0:T(8,128)(2,1)S(1)}, bf16[3,40,1280]{2,1,0:T(8,128)(2,1)}, u32[]{:S(2)}, u32[]{:S(2)}) collective-permute-start(bf16[3,40,1280]{2,1,0:T(8,128)(2,1)S(1)} %fusion.39), channel_id=1, source_target_pairs={{0,16},{1,17},{2,18},{3,19},{4,20},{5,21},{6,22},{7,23},{8,24},{9,... | collective-permute-start | bytes 921608 | tf_op jit(solution)/shard_map/ppermute | solution.py:262
  555.1 26.3 %collective-permute-start.22 = (bf16[3,4,2,40,640]{4,3,2,1,0:T(8,128)(2,1)S(1)}, bf16[3,4,2,40,640]{4,3,2,1,0:T(8,128)(2,1)S(1)}, u32[]{:S(2)}, u32[]{:S(2)}) collective-permute-start(bf16[3,4,2,40,640]{4,3,2,1,0:T(8,128)(2,1)S(1)} %dynamic-slice_bitcast_fusion.1), channel_id=1, source_target_pairs={{0,4},{1,5},{2,6},{3,7},{4,0},{5,1},{6,2},{7,3},{8,12},{9,13},{10,... | collective-permute-start | bytes 3686408 | tf_op jit(solution)/shard_map/ppermute | solution.py:262
  557.5 25.2 %collective-permute-start.20 = (bf16[3,4,2,40,640]{4,3,1,0,2:T(8,128)(2,1)S(1)}, bf16[3,4,2,40,640]{4,3,1,0,2:T(8,128)(2,1)S(1)}, u32[]{:S(2)}, u32[]{:S(2)}) collective-permute-start(bf16[3,4,2,40,640]{4,3,1,0,2:T(8,128)(2,1)S(1)} %bitcast.274), channel_id=1, source_target_pairs={{0,2},{1,3},{2,0},{3,1},{4,6},{5,7},{6,4},{7,5},{8,10},{9,11},{10,... | collective-permute-start | bytes 3686408 | tf_op jit(solution)/shard_map/ppermute | solution.py:262
  559.0 25.8 %collective-permute-start.17 = (bf16[3,40,1280]{2,1,0:T(8,128)(2,1)S(1)}, bf16[3,40,1280]{2,1,0:T(8,128)(2,1)S(1)}, u32[]{:S(2)}, u32[]{:S(2)}) collective-permute-start(bf16[3,40,1280]{2,1,0:T(8,128)(2,1)S(1)} %fusion.35), channel_id=1, source_target_pairs={{0,16},{1,17},{2,18},{3,19},{4,20},{5,21},{6,22},{7,23},{8,24},{9,... | collective-permute-start | bytes 921608 | tf_op jit(solution)/shard_map/ppermute | solution.py:262
  572.5 25.2 %collective-permute-start.11 = (bf16[3,40,1280]{2,1,0:T(8,128)(2,1)S(1)}, bf16[3,40,1280]{2,1,0:T(8,128)(2,1)S(1)}, u32[]{:S(2)}, u32[]{:S(2)}) collective-permute-start(bf16[3,40,1280]{2,1,0:T(8,128)(2,1)S(1)} %fusion.30), channel_id=1, source_target_pairs={{8,0},{9,1},{10,2},{11,3},{12,4},{13,5},{14,6},{15,7},{24,16},{25,... | collective-permute-start | bytes 921608 | tf_op jit(solution)/shard_map/ppermute | solution.py:301
  581.8 12.1 %collective-permute-start.23 = (bf16[3,4,40,640]{3,2,1,0:T(8,128)(2,1)S(1)}, bf16[3,4,40,640]{3,2,1,0:T(8,128)(2,1)S(1)}, u32[]{:S(2)}, u32[]{:S(2)}) collective-permute-start(bf16[3,4,40,640]{3,2,1,0:T(8,128)(2,1)S(1)} %dynamic-slice_bitcast_fusion.3), channel_id=1, source_target_pairs={{0,2},{1,3},{2,0},{3,1},{4,6},{5,7},{6,4},{7,5},{8,10},{9,11},{10,... | collective-permute-start | bytes 1843208 | tf_op jit(solution)/shard_map/ppermute | solution.py:262
  583.2 10.9 %collective-permute-start.21 = (bf16[3,4,40,640]{3,2,1,0:T(8,128)(2,1)S(1)}, bf16[3,4,40,640]{3,2,1,0:T(8,128)(2,1)S(1)}, u32[]{:S(2)}, u32[]{:S(2)}) collective-permute-start(bf16[3,4,40,640]{3,2,1,0:T(8,128)(2,1)S(1)} %dynamic-slice_bitcast_fusion.4), channel_id=1, source_target_pairs={{0,4},{1,5},{2,6},{3,7},{4,0},{5,1},{6,2},{7,3},{8,12},{9,13},{10,... | collective-permute-start | bytes 1843208 | tf_op jit(solution)/shard_map/ppermute | solution.py:262
  584.9 12.9 %collective-permute-start.18 = (bf16[3,40,1280]{2,1,0:T(8,128)(2,1)S(1)}, bf16[3,40,1280]{2,1,0:T(8,128)(2,1)S(1)}, u32[]{:S(2)}, u32[]{:S(2)}) collective-permute-start(bf16[3,40,1280]{2,1,0:T(8,128)(2,1)S(1)} %fusion.27), channel_id=1, source_target_pairs={{0,8},{1,9},{2,10},{3,11},{4,12},{5,13},{6,14},{7,15},{16,24},{17,... | collective-permute-start | bytes 921608 | tf_op jit(solution)/shard_map/ppermute | solution.py:301
  594.4 24.9 %collective-permute-start.24 = (bf16[3,2,40,1280]{3,2,0,1:T(8,128)(2,1)S(1)}, bf16[3,2,40,1280]{3,2,0,1:T(8,128)(2,1)S(1)}, u32[]{:S(2)}, u32[]{:S(2)}) collective-permute-start(bf16[3,2,40,1280]{3,2,0,1:T(8,128)(2,1)S(1)} %dynamic-slice_bitcast_fusion.2), channel_id=1, source_target_pairs={{0,16},{1,17},{2,18},{3,19},{4,20},{5,21},{6,22},{7,23},{8,24},{9,... | collective-permute-start | bytes 1843208 | tf_op jit(solution)/shard_map/ppermute | solution.py:262
  619.6 9.3 %collective-permute-start.25 = (bf16[3,40,1280]{2,1,0:T(8,128)(2,1)S(1)}, bf16[3,40,1280]{2,1,0:T(8,128)(2,1)S(1)}, u32[]{:S(2)}, u32[]{:S(2)}) collective-permute-start(bf16[3,40,1280]{2,1,0:T(8,128)(2,1)S(1)} %dynamic-slice_bitcast_fusion.9), channel_id=1, source_target_pairs={{0,8},{1,9},{2,10},{3,11},{4,12},{5,13},{6,14},{7,15},{8,0},{9,1},... | collective-permute-start | bytes 921608 | tf_op jit(solution)/shard_map/ppermute | solution.py:262
  (22 other events, 349.7 us)
Sparse Core Ops, SparseCore 0:
  11.5 86.3 all-gather.3
  100.8 82.3 all-gather.5

commit v2 on v1

--- a/solution.py
+++ b/solution.py
@@ -258,47 +258,267 @@
     )(counts, qkv, qkv, qkv, context, grad_context, lse, qx, kx, factor)
 
 
+def mean_rows(x):
+    return jnp.mean(x, axis=-1, keepdims=True)
+
+
+def front_kernel(x_ref, gain_ref, factor_ref, w_ref, normed_ref, qkv_ref):
+    x = x_ref[...].astype(jnp.float32)
+    normed = (x * lax.rsqrt(mean_rows(x * x) + EPSILON) * gain_ref[...]).astype(LOW)
+    normed_ref[...] = normed
+    for i in range(3):
+        y = dot(w_ref[i], normed, NT)
+        if i == 0:
+            y = y * jnp.concatenate([factor_ref[...]] * (y.shape[1] // 128), axis=1)
+        qkv_ref[i] = y.astype(LOW)
+
+
+def front(x, gain, factor_rows, weight):
+    tokens, width = x.shape
+    rows = weight.shape[1]
+    return pl.pallas_call(
+        front_kernel,
+        grid=(tokens // TILE,),
+        in_specs=[
+            pl.BlockSpec((TILE, width), lambda i: (i, 0)),
+            pl.BlockSpec((1, width), lambda i: (0, 0)),
+            pl.BlockSpec((rows, 128), lambda i: (0, 0)),
+            pl.BlockSpec((3, rows, width), lambda i: (0, 0, 0)),
+        ],
+        out_specs=[
+            pl.BlockSpec((TILE, width), lambda i: (i, 0)),
+            pl.BlockSpec((3, rows, TILE), lambda i: (0, 0, i)),
+        ],
+        out_shape=[
+            jax.ShapeDtypeStruct((tokens, width), LOW),
+            jax.ShapeDtypeStruct((3, rows, tokens), LOW),
+        ],
+        cost_estimate=pl.CostEstimate(
+            flops=6 * tokens * rows * width, bytes_accessed=16 * tokens * width, transcendentals=0
+        ),
+        name="front",
+    )(x, gain, factor_rows, weight)
+
+
+def middle_kernel(
+    unit,
+    core_ref,
+    x_ref,
+    context_ref,
+    g_ref,
+    gain_ref,
+    w_ref,
+    out_ref,
+    grad_hidden_ref,
+    grad_context_ref,
+    keep_ref,
+    send_ref,
+    gain_grad_ref,
+    total,
+):
+    step = pl.program_id(0)
+    width = x_ref.shape[1]
+
+    @pl.when(step == 0)
+    def _():
+        total[...] = jnp.zeros_like(total)
+        gain_grad_ref[...] = jnp.zeros_like(gain_grad_ref)
+
+    g = g_ref[...]
+    gain = gain_ref[...]
+    context = context_ref[...].T
+    hidden = x_ref[...].astype(jnp.float32) + dot(context, w_ref[0], NT)
+    root = lax.rsqrt(mean_rows(hidden * hidden) + EPSILON)
+    scaled = hidden * root
+    normed = (scaled * gain).astype(LOW)
+    upward = dot(normed, w_ref[1], NT)
+    s = jax.nn.sigmoid(upward)
+    activated = (upward * s).astype(LOW)
+    out_ref[...] = (hidden + dot(activated, w_ref[2], NT)).astype(LOW)
+    slope = s * (1.0 + upward * (1.0 - s))
+    grad_upward = (dot(g, w_ref[2], NN) * slope).astype(LOW)
+    total[2] += dot(g.T, activated, NN)
+    grad_normed = dot(grad_upward, w_ref[1], NN)
+    total[1] += dot(grad_upward.T, normed, NN)
+    gain_grad_ref[...] += fold(grad_normed * scaled, jnp.sum)
+    w = grad_normed * gain
+    grad_hidden = g.astype(jnp.float32) + root * (w - scaled * mean_rows(w * scaled))
+    grad_hidden_ref[...] = grad_hidden
+    branch = grad_hidden.astype(LOW)
+    grad_context_ref[...] = dot(branch, w_ref[0], NN).astype(LOW).T
+    total[0] += dot(branch.T, context, NN)
+
+    @pl.when(step == pl.num_programs(0) - 1)
+    def _():
+        core = core_ref[0]
+
+        @pl.loop(0, width // (2 * unit))
+        def _(j):
+            for i in range(3):
+                at = pl.multiple_of((2 * j + core) * unit, 8)
+                keep_ref[i, j] = total[i, pl.ds(at, unit), :].astype(LOW)
+                at = pl.multiple_of((2 * j + 1 - core) * unit, 8)
+                send_ref[i, j] = total[i, pl.ds(at, unit), :].astype(LOW)
+
+
+def middle(core, x, context, g, gain, weight, unit):
+    tokens, width = x.shape
+    chips = width // (2 * unit)
+    rows = pl.BlockSpec((TILE, width), lambda i, core: (i, 0))
+    columns = pl.BlockSpec((width, TILE), lambda i, core: (0, i))
+    once = pl.Buffered(1)
+    half = pl.BlockSpec((3, chips, unit, width), lambda i, core: (0, 0, 0, 0), pipeline_mode=once)
+    return pl.pallas_call(
+        functools.partial(middle_kernel, unit),
+        grid_spec=pltpu.PrefetchScalarGridSpec(
+            num_scalar_prefetch=1,
+            grid=(tokens // TILE,),
+            in_specs=[
+                rows,
+                columns,
+                rows,
+                pl.BlockSpec((1, width), lambda i, core: (0, 0)),
+                pl.BlockSpec((3, width, width), lambda i, core: (0, 0, 0), pipeline_mode=once),
+            ],
+            out_specs=[
+                rows,
+                rows,
+                columns,
+                half,
+                half,
+                pl.BlockSpec((8, width), lambda i, core: (0, 0)),
+            ],
+            scratch_shapes=[pltpu.VMEM((3, width, width), jnp.float32)],
+        ),
+        out_shape=[
+            jax.ShapeDtypeStruct((tokens, width), LOW),
+            jax.ShapeDtypeStruct((tokens, width), jnp.float32),
+            jax.ShapeDtypeStruct((width, tokens), LOW),
+            jax.ShapeDtypeStruct((3, chips, unit, width), LOW),
+            jax.ShapeDtypeStruct((3, chips, unit, width), LOW),
+            jax.ShapeDtypeStruct((8, width), jnp.float32),
+        ],
+        compiler_params=pltpu.CompilerParams(vmem_limit_bytes=66_000_000),
+        cost_estimate=pl.CostEstimate(
+            flops=18 * tokens * width * width,
+            bytes_accessed=14 * tokens * width + 12 * width * width,
+            transcendentals=tokens * width,
+        ),
+        name="middle",
+    )(core, x, context, g, gain, weight)
+
+
+def back_kernel(x_ref, grad_hidden_ref, gain_ref, w_ref, *rest):
+    *d_refs, out_ref, gain_grad_ref = rest
+    groups = len(d_refs)
+    rows = d_refs[0].shape[1]
+
+    @pl.when(pl.program_id(0) == 0)
+    def _():
+        gain_grad_ref[...] = jnp.zeros_like(gain_grad_ref)
+
+    x = x_ref[...].astype(jnp.float32)
+    root = lax.rsqrt(mean_rows(x * x) + EPSILON)
+    scaled = x * root
+    parts = [
+        d_refs[p][i].T for i in range(3) for p in range(groups)
+    ]
+    grad_normed = dot(jnp.concatenate(parts, axis=1), w_ref[...], NN)
+    gain_grad_ref[...] += fold(grad_normed * scaled, jnp.sum)
+    w = grad_normed * gain_ref[...]
+    out_ref[...] = grad_hidden_ref[...] + root * (w - scaled * mean_rows(w * scaled))
+
+
+def back(x, grad_hidden, gain, weight, grads):
+    tokens, width = x.shape
+    rows = pl.BlockSpec((TILE, width), lambda i: (i, 0))
+    group = grads[0].shape[1]
+    return pl.pallas_call(
+        back_kernel,
+        grid=(tokens // TILE,),
+        in_specs=[
+            rows,
+            rows,
+            pl.BlockSpec((1, width), lambda i: (0, 0)),
+            pl.BlockSpec(weight.shape, lambda i: (0, 0)),
+        ]
+        + [pl.BlockSpec((3, group, TILE), lambda i: (0, 0, i))] * len(grads),
+        out_specs=[rows, pl.BlockSpec((8, width), lambda i: (0, 0))],
+        out_shape=[
+            jax.ShapeDtypeStruct((tokens, width), jnp.float32),
+            jax.ShapeDtypeStruct((8, width), jnp.float32),
+        ],
+        cost_estimate=pl.CostEstimate(
+            flops=6 * tokens * width * width, bytes_accessed=18 * tokens * width, transcendentals=0
+        ),
+        name="back",
+    )(x, grad_hidden, gain, weight, *grads)
+
+
 def exchange(x, bit, n):
     return lax.ppermute(x, AXIS, [(i, i ^ bit) for i in range(n)])
 
 
-def halve(x, dim, bit, n):
+def tie(*values):
+    return lax.optimization_barrier(values)
+
+
+def pick(x, dim, bit):
     mine = (lax.axis_index(AXIS) // bit) % 2
-    away = lax.dynamic_index_in_dim(x, 1 - mine, dim, keepdims=False)
-    keep = lax.dynamic_index_in_dim(x, mine, dim, keepdims=False)
-    came = exchange(away, bit, n)
+    return (
+        lax.dynamic_index_in_dim(x, mine, dim, keepdims=False),
+        lax.dynamic_index_in_dim(x, 1 - mine, dim, keepdims=False),
+    )
+
+
+def plus(keep, came):
     return (keep.astype(jnp.float32) + came.astype(jnp.float32)).astype(LOW)
 
 
-def planes_to_mine(x, n):
-    x = halve(x, 4, 1, n)
-    half = x.shape[-1] // 2
-    left, right = x[..., :half], x[..., half:]
-    left = halve(left, 3, 2, n)
-    right = halve(right, 2, 4, n)
-    left = halve(left, 2, 4, n)
-    right = halve(right, 2, 2, n)
-    return jnp.concatenate([left, right], axis=-1)
-
-
-def scatter_all(parts, n):
-    if n != 32:
-        return lax.psum_scatter(jnp.stack(parts), AXIS, scatter_dimension=1, tiled=True)
-    rows, width = parts[0].shape
-    x = jnp.stack([p.astype(LOW) for p in parts])
-    x = x.reshape(len(parts), 4, 2, 2, 2, rows // n, width)
-    x = planes_to_mine(x, n)
-    x = halve(x.reshape(len(parts), 2, 2, rows // n, width), 1, 16, n)
-    return halve(x, 1, 8, n).astype(jnp.float32)
-
-
-def scatter_half(x, parity, n):
-    three, heads, depth, width = x.shape
-    x = x.astype(LOW).reshape(three, 2, 2, 2, 2, depth // 2, width)
-    x = planes_to_mine(x, n)
-    x = halve(x, 1, 16, n)
-    senders = [(i, i ^ 8) for i in range(n) if (i // 8) % 2 != parity]
-    return x.astype(jnp.float32) + lax.ppermute(x, AXIS, senders).astype(jnp.float32)
+class Scatter:
+    def __init__(self, keep, send, planes, n):
+        self.n = n
+        self.planes = planes
+        self.keep = [keep]
+        self.came = [exchange(send, 1, n)]
+        self.steps = iter([self.first, self.second, self.far, self.near])
+
+    def tie(self, *values):
+        count = len(self.came)
+        tied = tie(*self.came, *values)
+        self.came = list(tied[:count])
+        return tied[count:]
+
+    def step(self):
+        sums = [plus(k, c) for k, c in zip(self.keep, self.came)]
+        next(self.steps)(*sums)
+
+    def send(self, *pairs):
+        self.keep = [keep for keep, _, _ in pairs]
+        self.came = [exchange(away, bit, self.n) for _, away, bit in pairs]
+
+    def first(self, x):
+        half = x.shape[-1] // 2
+        self.send((*pick(x[..., :half], 3, 2), 2), (*pick(x[..., half:], 2, 4), 4))
+
+    def second(self, left, right):
+        self.send((*pick(left, 2, 4), 4), (*pick(right, 2, 2), 2))
+
+    def far(self, left, right):
+        x = jnp.concatenate([left, right], axis=-1)
+        x = x.reshape(x.shape[0], 2, -1, *x.shape[2:])
+        self.send((*pick(x, 1, 16), 16))
+
+    def near(self, x):
+        if self.planes is None:
+            self.send((*pick(x, 1, 8), 8))
+        else:
+            x = x[:, 0]
+            senders = [(i, i ^ 8) for i in range(self.n) if (i // 8) % 2 != self.planes]
+            self.keep, self.came = [x], [lax.ppermute(x, AXIS, senders)]
+
+    def result(self):
+        return self.keep[0].astype(jnp.float32) + self.came[0].astype(jnp.float32)
 
 
 def sum_all(x, n):
@@ -336,10 +556,9 @@
         jnp.stack([first_gain, second_gain]).astype(jnp.float32), AXIS, axis=1, tiled=True
     )
     wide = jnp.stack([query_weight.T, key_weight.T, value_weight.T])
-    qkv_weight = lax.all_gather(wide, AXIS, axis=1, tiled=True).reshape(3 * width, width)
+    early = lax.all_gather(wide, AXIS, axis=1, tiled=True)
     late = jnp.stack([output_weight.T, up_weight.T, down_weight.T])
     late = lax.all_gather(late, AXIS, axis=1, tiled=True)
-    output_t, up_t, down_t = late[0], late[1], late[2]
 
     ids = block_ids.reshape(1, tokens)
     row = lax.broadcasted_iota(jnp.int32, (EXTRA, tokens), 0)
@@ -351,78 +570,95 @@
     seen = jnp.sum(block_ids[:, None, :] <= last[:, :, None], axis=-1)
     counts = ((seen + TILE - 1) // TILE).astype(jnp.int32)
 
-    x = inputs.reshape(tokens, width).astype(jnp.float32)
+    x = inputs.reshape(tokens, width)
     g = cotangent.reshape(tokens, width)
-    root1 = lax.rsqrt(jnp.mean(x * x, axis=-1, keepdims=True) + EPSILON)
-    normed = (x * root1 * gains[0]).astype(LOW)
     factor = query_scale / math.sqrt(depth)
     heads = width // depth
-    row_scale = jnp.concatenate(
-        [jnp.tile(factor * LOG2E, heads), jnp.ones((2 * width,), jnp.float32)]
+    factor_rows = jnp.broadcast_to(factor[:, None], (depth, TILE))
+    row_scale = jnp.broadcast_to(jnp.tile(factor * LOG2E, heads)[:, None], (width, 128))
+    normed, qkv = front(x, gains[:1], row_scale, early)
+    context, lse = attention_forward(qkv, qx, kx, counts, depth, length)
+    core = (me % 2).reshape(1)
+    unit = depth // 2
+    output, grad_hidden, grad_context, keep, send, gain2_rows = middle(
+        core, x, context, g, gains[1:], late, unit
     )
-    qkv = (dot(qkv_weight, normed, NT) * row_scale[:, None]).astype(LOW)
-    qkv = qkv.reshape(3, width, tokens)
-    context, lse = attention_forward(qkv, qx, kx, counts, depth, length)
-    hidden = x + dot(context, output_t, TT)
-    root2 = lax.rsqrt(jnp.mean(hidden * hidden, axis=-1, keepdims=True) + EPSILON)
-    normed2 = (hidden * root2 * gains[1]).astype(LOW)
-    upward = dot(normed2, up_t, NT)
-    s = jax.nn.sigmoid(upward)
-    activated = (upward * s).astype(LOW)
-    output = (hidden + dot(activated, down_t, NT)).astype(LOW)
-
-    grad_down = dot(g, activated, TN)
-    grad_activated = dot(g, down_t, NN)
-    grad_upward = (grad_activated * s * (1.0 + upward * (1.0 - s))).astype(LOW)
-    grad_up = dot(grad_upward, normed2, TN)
-    grad_normed2 = dot(grad_upward, up_t, NN)
-    grad_gain2 = jnp.sum(grad_normed2 * hidden * root2, axis=0)
-    w = grad_normed2 * gains[1]
-    grad_hidden = (
-        g.astype(jnp.float32)
-        + root2 * w
-        - hidden * (root2 * root2 * root2) * jnp.mean(w * hidden, axis=-1, keepdims=True)
-    )
-    grad_branch = grad_hidden.astype(LOW)
-    grad_output = dot(grad_branch, context, (((0,), (1,)), ((), ())))
-    grad_context = dot(output_t, grad_branch, TT).astype(LOW)
-    late_grads = scatter_all([grad_output, grad_up, grad_down], n)
-
-    factor_rows = jnp.broadcast_to(factor[:, None], (depth, TILE))
-    pairs = []
-    for parity in range(2):
-        pairs.append(
-            attention_backward(
-                qkv, context, grad_context, lse, qx, kx, counts, factor_rows, depth, length,
-                (parity, 2, heads // HEADS_PER_STEP // 2),
-            )
+
+    def spatial(x, planes):
+        return x.reshape(3, planes, 2, 2, unit, width)
+
+    def backward(plane, grad_context):
+        return attention_backward(
+            qkv, context, grad_context, lse, qx, kx, counts, factor_rows, depth, length,
+            (plane, 1, 1),
         )
-    scale_part = jnp.sum(pairs[0][1] + pairs[1][1], axis=1) / (factor * LOG2E) / math.sqrt(depth)
-    weight_parts = [
-        dot(d.reshape(-1, tokens), normed, NN).reshape(3, heads // 2, depth, width)
-        for d, _ in pairs
-    ]
+
+    def weight_grads(*parts):
+        rows = [
+            dot(d.reshape(-1, tokens), normed, NN).astype(LOW).reshape(3, -1, 2, unit, width)
+            for d in parts
+        ]
+        rows = [pick(r, 2, 1) for r in rows]
+        return [jnp.concatenate([r[i] for r in rows], axis=1) for i in range(2)]
+
+    grads = [None] * 4
     if n == 32:
-        own = (me // 8) % 2
-        halves = [scatter_half(part, parity, n) for parity, part in enumerate(weight_parts)]
-        early_grads = jnp.where(own == 0, halves[0], halves[1])
+        send, grad_context = tie(send, grad_context)
+        late_sum = Scatter(spatial(keep, 4), spatial(send, 4), None, n)
+        grads[0], part0 = backward(0, grad_context)
+        (grads[0],) = late_sum.tie(grads[0])
+        late_sum.step()
+        *late_sum.keep, grad_context, d0 = tie(*late_sum.keep, grad_context, grads[0])
+        grads[2], part2 = backward(2, grad_context)
+        keep, send = weight_grads(d0, grads[2])
+        even_sum = Scatter(spatial(keep, 2), spatial(send, 2), 0, n)
+        keep, grad_context = tie(keep, grad_context)
+        even_sum.keep = [spatial(keep, 2)]
+        grads[1], part1 = backward(1, grad_context)
+        (grads[1],) = late_sum.tie(grads[1])
+        late_sum.step()
+        (d1,) = even_sum.tie(grads[1])
+        even_sum.step()
+        *even_sum.keep, k0, k1, grad_context = tie(*even_sum.keep, *late_sum.keep, grad_context)
+        late_sum.keep = [k0, k1]
+        grads[3], part3 = backward(3, grad_context)
+        (d3,) = late_sum.tie(grads[3])
+        late_sum.step()
+        (d3,) = even_sum.tie(d3)
+        even_sum.step()
+        keep, send = weight_grads(d1, d3)
+        odd_sum = Scatter(spatial(keep, 2), spatial(send, 2), 1, n)
+        *late_sum.keep, keep, d3 = tie(*late_sum.keep, keep, d3)
+        odd_sum.keep = [spatial(keep, 2)]
+        grads[3] = d3
     else:
-        both = [p.reshape(3, 2, 1, -1, width) for p in weight_parts]
-        both = jnp.concatenate(both, axis=2).reshape(3, width, width)
+        parts = [backward(p, grad_context) for p in range(4)]
+        grads = [d for d, _ in parts]
+        part0, part1, part2, part3 = [part for _, part in parts]
+        mine = me % 2 == 0
+        even, odd = jnp.where(mine, keep, send), jnp.where(mine, send, keep)
+        both = jnp.stack([even, odd], axis=2).reshape(3, width, width).astype(jnp.float32)
+        late_grads = lax.psum_scatter(both, AXIS, scatter_dimension=1, tiled=True)
+        rows = [dot(d.reshape(-1, tokens), normed, NN).reshape(3, -1, width) for d in grads]
+        both = jnp.concatenate(rows, axis=1)
         early_grads = lax.psum_scatter(both, AXIS, scatter_dimension=1, tiled=True)
 
-    weight = qkv_weight.reshape(3, 2, 2, -1, width)
-    grad_normed = sum(
-        dot(d.reshape(-1, tokens), weight[:, :, parity].reshape(-1, width), TN)
-        for parity, (d, _) in enumerate(pairs)
-    )
-    grad_gain1 = jnp.sum(grad_normed * x * root1, axis=0)
-    w = grad_normed * gains[0]
-    grad_inputs = (
-        grad_hidden
-        + root1 * w
-        - x * (root1 * root1 * root1) * jnp.mean(w * x, axis=-1, keepdims=True)
-    )
+    grad_inputs, gain1_rows = back(x, grad_hidden, gains[:1], early.reshape(-1, width), grads)
+    if n == 32:
+        (grad_inputs,) = odd_sum.tie(grad_inputs)
+        odd_sum.step()
+        (grad_inputs,) = even_sum.tie(grad_inputs)
+        even_sum.step()
+        late_sum.step()
+        odd_sum.step()
+        even_sum.step()
+        late_grads = late_sum.result()
+        odd_sum.step()
+        odd_sum.step()
+        early_grads = jnp.where((me // 8) % 2 == 0, even_sum.result(), odd_sum.result())
+    scale_part = jnp.sum(part0 + part1 + part2 + part3, axis=1)
+    scale_part = scale_part / (factor * LOG2E) / math.sqrt(depth)
+    grad_gain1, grad_gain2 = jnp.sum(gain1_rows, axis=0), jnp.sum(gain2_rows, axis=0)
     small = jnp.concatenate([grad_gain1, grad_gain2, scale_part])
     small = sum_all(small, n)
     gain1 = lax.dynamic_slice_in_dim(small, me * shard, shard)

time: 640 us -> 559 us (0.87)
  matrix products: 214 us -> 30.4 us
  Pallas kernels: 133 us -> 284 us
  waiting for transfers between devices: 128 us -> 97.8 us
  other arithmetic: 50.7 us -> 31.4 us
    dot_general x14 -> x4, matrix products: 214 us -> 30.4 us  [dot(): lax.dot_general(left, right, dims, preferred_element_type=jnp.float32)]
    pallas_call x0 -> x3, Pallas kernels: none -> 148 us  [the longest x1 82.3 us: middle(): pl.pallas_call(functools.partial(middle_kernel, unit), grid_spec=pltpu.Pr...]
    ppermute x24, waiting for transfers between devices: 91.2 us -> 46.8 us  [exchange(): return lax.ppermute(x, AXIS, [(i, i ^ bit) for i in range(n)])]
    sub x2 -> x0, other arithmetic: 18.7 us -> none  [the longest x1 11.5 us: on_device(): grad_hidden + root1 * w]
    all_gather x1, waiting for transfers between devices: 27.1 us -> 37.3 us  [on_device(): early = lax.all_gather(wide, AXIS, axis=1, tiled=True)]
    slice x5 -> x4, local copies, waits for them, and re-layouts: 9.42 us -> 1.58 us  [the longest x3 0.97 us: first(): self.send((*pick(x[..., :half], 3, 2), 2), (*pick(x[..., half:], 2, 4), 4))]
    pallas_call x2 -> x4, Pallas kernels: 85.1 us -> 90.6 us  [attention_backward(): pl.pallas_call(functools.partial(attention_backward_kernel, heads, depth,...]
    convert_element_type x20 -> x15, other arithmetic: 16.6 us -> 19.8 us  [plus(): return (keep.astype(jnp.float32) + came.astype(jnp.float32)).astype(LOW)]
  transfers between devices with their start and end apart: 28 -> 28, of which waited for: 14 -> 16; matrix products, arithmetic and copies ran while one was open for 26% -> 10% of each run, Pallas kernels for 8% -> 32%
where the time goes in v2:
time: 559 us; the launch traced here: 553 us
  Pallas kernels  284 us (51%)
  waiting for transfers between devices  97.8 us (17%)
  blocking collectives  43.3 us (8%)
  other arithmetic  31.4 us (6%)
  matrix products  30.4 us (5%)
  starting transfers between devices  25.8 us (5%)
  local copies, waits for them, and re-layouts  25.8 us (5%)
  between operations  14.9 us (3%)
    pallas_call x4, Pallas kernels, attention_backward(): pl.pallas_call(functools.partial(attention_backward_kernel, heads, depth,...  90.6 us
    pallas_call x1, Pallas kernels, middle(): pl.pallas_call(functools.partial(middle_kernel, unit), grid_spec=pltpu.Pr...  82.3 us
    ppermute x24, waiting for transfers between devices, exchange(): return lax.ppermute(x, AXIS, [(i, i ^ bit) for i in range(n)])  46.8 us
    pallas_call x1, Pallas kernels, attention_forward(): pl.pallas_call(functools.partial(attention_forward_kernel, heads, depth,...  45 us
    all_gather x1, blocking collectives, on_device(): lax.all_gather(jnp.stack([first_gain, second_gain]).astype(jnp.float32),...  43.3 us
    all_gather x1, waiting for transfers between devices, on_device(): early = lax.all_gather(wide, AXIS, axis=1, tiled=True)  37.3 us
    pallas_call x1, Pallas kernels, back(): pl.pallas_call(back_kernel, grid=(tokens // TILE,), in_specs=[rows, rows,...  36.7 us
    dot_general x4, matrix products, dot(): lax.dot_general(left, right, dims, preferred_element_type=jnp.float32)  30.4 us
  transfers between devices with their start and end apart: 28, of which 16 were waited for; matrix products, arithmetic and copies ran while one was open for 10% of the time, Pallas kernels for 32%

profile of v2, /device:TPU:0, one launch (start us, length us, event | category | flops | bytes accessed | tf_op | source)
XLA Modules:
  0.0 552.9 jit_solution(3189948774305909216)
XLA Ops:
  13.7 43.3 %all-gather = f32[32,40,2]{1,2,0:T(2,128)S(1)} all-gather(f32[1,40,2]{1,2,0:T(2,128)S(1)} %convert_bitcast_fusion), channel_id=1, replica_groups=mesh['fsdp'=32] {'fsdp'}, dimensions={0}, use_global_device_ids=true | all-gather | bytes 10560 | tf_op jit(solution)/shard_map/all_gather | solution.py:555
  60.6 37.3 %all-gather.4.cloned.1.call-done.w_ref = bf16[3,1280,1280]{2,1,0:T(8,128)(2,1)} async-done(((bf16[3,40,1280]{2,1,0:T(8,128)(2,1)}), bf16[3,1280,1280]{2,1,0:T(8,128)(2,1)}) %all-gather.4.cloned.1.call-update) | async-done | bytes 9830416 | tf_op jit(solution)/shard_map/all_gather | solution.py:559
  99.0 29.1 %front.1 = (bf16[2048,1280]{1,0:T(8,128)(2,1)}, bf16[3,1280,2048]{2,1,0:T(8,128)(2,1)}) custom-call(bf16[2048,1280]{1,0:T(8,128)(2,1)} %bitcast.202, f32[1,1280]{1,0:T(1,128)} %get-tuple-element.156.gain_ref, f32[1280,128]{1,0:T(8,128)} %broadcast_in_dim.30.factor_ref, bf16[3,1280,1280]{2,1,0:T(8,128)(2,1)} %all-gather.4.cloned.1.call-done.w_ref), custom_call_target="tpu_custom_call" | custom-call | flops 20132659200 | bytes 41943040 | tf_op jit(solution)/shard_map/front/pallas_call | solution.py:279
  128.1 45.0 %attention_forward.1 = (bf16[1280,2048]{1,0:T(8,128)(2,1)}, f32[16,1,2048]{2,1,0:T(1,128)}) custom-call(s32[2,4]{1,0:T(2,128)} %and_select_fusion.counts, bf16[3,1280,2048]{2,1,0:T(8,128)(2,1)} %get-tuple-element.65.q_ref.k_ref.v_ref, bf16[3,1280,2048]{2,1,0:T(8,128)(2,1)} %get-tuple-element.65.q_ref.k_ref.v_ref, ...), custom_call_target="tpu_custom_call" | custom-call | flops 34359738368 | bytes 20971520 | tf_op jit(solution)/shard_map/attention_forward/pallas_call | solution.py:101
  173.1 10.2 %all-gather.6.cloned.1.call-done.w_ref = bf16[3,1280,1280]{2,1,0:T(8,128)(2,1)} async-done(((bf16[3,40,1280]{2,1,0:T(8,128)(2,1)}), bf16[3,1280,1280]{2,1,0:T(8,128)(2,1)}) %all-gather.6.cloned.1.call-update) | async-done | bytes 9830416 | tf_op jit(solution)/shard_map/all_gather | solution.py:561
  183.3 82.3 %middle.1 = (bf16[2048,1280]{1,0:T(8,128)(2,1)}, f32[2048,1280]{1,0:T(8,128)}, bf16[1280,2048]{1,0:T(8,128)(2,1)}, bf16[3,16,40,1280]{3,2,1,0:T(8,128)(2,1)}, bf...) custom-call(s32[1]{0:T(128)} %bitcast.core_ref, bf16[2048,1280]{1,0:T(8,128)(2,1)} %bitcast.203, ...), custom_call_target="tpu_custom_call" | custom-call | flops 60397977600 | bytes 56360960 | tf_op jit(solution)/shard_map/middle/pallas_call | solution.py:371
  266.6 22.9 %attention_backward.4 = (bf16[3,320,2048]{2,1,0:T(8,128)(2,1)}, f32[80,256]{1,0:T(8,128)}) custom-call(s32[2,4]{1,0:T(2,128)} %and_select_fusion.counts, bf16[3,1280,2048]{2,1,0:T(8,128)(2,1)} %get-tuple-element.65.q_ref.k_ref.v_ref, bf16[3,1280,2048]{2,1,0:T(8,128)(2,1)} %get-tuple-element.65.q_ref.k_ref.v_ref, ...), custom_call_target="tpu_custom_call" | custom-call | flops 15032385536 | bytes 10485760 | tf_op jit(solution)/shard_map/attention_backward/pallas_call | solution.py:221
  289.5 5.3 fusion
  298.0 22.5 %attention_backward.5 = (bf16[3,320,2048]{2,1,0:T(8,128)(2,1)}, f32[80,256]{1,0:T(8,128)}) custom-call(s32[2,4]{1,0:T(2,128)} %and_select_fusion.counts, bf16[3,1280,2048]{2,1,0:T(8,128)(2,1)} %get-tuple-element.65.q_ref.k_ref.v_ref, bf16[3,1280,2048]{2,1,0:T(8,128)(2,1)} %get-tuple-element.65.q_ref.k_ref.v_ref, ...), custom_call_target="tpu_custom_call" | custom-call | flops 15032385536 | bytes 10485760 | tf_op jit(solution)/shard_map/attention_backward/pallas_call | solution.py:221
  320.5 8.7 %convolution_convert_fusion.3 = bf16[960,1280]{1,0:T(8,128)(2,1)S(1)} fusion(bf16[960,2048]{1,0:T(8,128)(2,1)} %bitcast.206, bf16[2048,1280]{1,0:T(8,128)(2,1)} %get-tuple-element.78), kind=kOutput, calls=%fused_computation.9 | convolution fusion | flops 5034393600 | bytes 11632640 | tf_op jit(solution)/shard_map/dot_general | solution.py:27
  329.2 8.1 %convolution_convert_fusion.2 = bf16[960,1280]{1,0:T(8,128)(2,1)S(1)} fusion(bf16[960,2048]{1,0:T(8,128)(2,1)S(1)} %bitcast.207, bf16[2048,1280]{1,0:T(8,128)(2,1)} %get-tuple-element.78), kind=kOutput, calls=%fused_computation.8 | convolution fusion | flops 5034393600 | bytes 11632640 | tf_op jit(solution)/shard_map/dot_general | solution.py:27
  345.1 2.6 collective-permute-start.2
  348.0 22.3 %attention_backward.6 = (bf16[3,320,2048]{2,1,0:T(8,128)(2,1)}, f32[80,256]{1,0:T(8,128)}) custom-call(s32[2,4]{1,0:T(2,128)} %and_select_fusion.counts, bf16[3,1280,2048]{2,1,0:T(8,128)(2,1)} %get-tuple-element.65.q_ref.k_ref.v_ref, bf16[3,1280,2048]{2,1,0:T(8,128)(2,1)} %get-tuple-element.65.q_ref.k_ref.v_ref, ...), custom_call_target="tpu_custom_call" | custom-call | flops 15032385536 | bytes 10485760 | tf_op jit(solution)/shard_map/attention_backward/pallas_call | solution.py:221
  370.3 2.1 collective-permute-done.3
  372.4 3.1 collective-permute-done.2
  375.5 3.0 add_convert_fusion
  383.5 2.3 fusion.1
  389.4 22.9 %attention_backward.7 = (bf16[3,320,2048]{2,1,0:T(8,128)(2,1)}, f32[80,256]{1,0:T(8,128)}) custom-call(s32[2,4]{1,0:T(2,128)} %and_select_fusion.counts, bf16[3,1280,2048]{2,1,0:T(8,128)(2,1)} %get-tuple-element.65.q_ref.k_ref.v_ref, bf16[3,1280,2048]{2,1,0:T(8,128)(2,1)} %get-tuple-element.65.q_ref.k_ref.v_ref, ...), custom_call_target="tpu_custom_call" | custom-call | flops 15032385536 | bytes 10485760 | tf_op jit(solution)/shard_map/attention_backward/pallas_call | solution.py:221
  416.7 3.8 collective-permute-start.24
  420.5 8.0 %convolution_convert_fusion.1 = bf16[960,1280]{1,0:T(8,128)(2,1)S(1)} fusion(bf16[960,2048]{1,0:T(8,128)(2,1)S(1)} %bitcast.208, bf16[2048,1280]{1,0:T(8,128)(2,1)} %get-tuple-element.78), kind=kOutput, calls=%fused_computation.7 | convolution fusion | flops 5034393600 | bytes 11632640 | tf_op jit(solution)/shard_map/dot_general | solution.py:27
  429.0 2.1 copy-done.12
  431.1 5.6 %convolution_convert_fusion = bf16[960,1280]{1,0:T(8,128)(2,1)S(1)} fusion(bf16[960,2048]{1,0:T(8,128)(2,1)S(1)} %bitcast.209, bf16[2048,1280]{1,0:T(8,128)(2,1)S(1)} %bitcast.213), kind=kOutput, calls=%fused_computation.6 | convolution fusion | flops 5034393600 | bytes 11632640 | tf_op jit(solution)/shard_map/dot_general | solution.py:27
  438.9 36.7 %back.1 = (f32[2048,1280]{1,0:T(8,128)}, f32[8,1280]{1,0:T(8,128)}) custom-call(bf16[2048,1280]{1,0:T(8,128)(2,1)} %bitcast.204, f32[2048,1280]{1,0:T(8,128)} %get-tuple-element.99.grad_hidden_ref, f32[1,1280]{1,0:T(1,128)} %get-tuple-element.156.gain_ref, bf16[3840,1280]{1,0:T(8,128)(2,1)} %bitcast.200, bf16[3,320,2048]{2,1,0:T(8,128)(2,1)} %get-tuple-element.77.rest_0_, ...), custom_call_target="tpu_custom_call" | custom-call | flops 20132659200 | bytes 47185920 | tf_op jit(solution)/shard_map/back/pallas_call | solution.py:436
  479.8 3.6 collective-permute-done.12
  483.5 2.1 collective-permute-start.8
  488.6 2.5 collective-permute-done.14
  492.9 2.8 collective-permute-done.15
  496.7 2.3 fusion.2
  500.8 11.4 %collective-permute-done.18 = bf16[3,2,2,40,640]{4,3,0,1,2:T(8,128)(2,1)S(1)} collective-permute-done((bf16[3,2,2,40,640]{4,3,0,1,2:T(8,128)(2,1)S(1)}, bf16[3,2,2,40,640]{4,3,0,1,2:T(8,128)(2,1)S(1)}, u32[]{:S(2)}, u32[]{:S(2)}) %collective-permute-start.18) | collective-permute-done | bytes 614432 | tf_op jit(solution)/shard_map/ppermute | solution.py:459
  519.4 2.3 collective-permute-done.21
  523.2 11.3 %collective-permute-done.16 = bf16[3,1,40,1280]{3,2,1,0:T(8,128)(2,1)S(1)} collective-permute-done((bf16[3,1,40,1280]{3,2,1,0:T(8,128)(2,1)S(1)}, bf16[3,1,40,1280]{3,2,1,0:T(8,128)(2,1)S(1)}, u32[]{:S(2)}, u32[]{:S(2)}) %collective-permute-start.16) | collective-permute-done | bytes 307232 | tf_op jit(solution)/shard_map/ppermute | solution.py:459
  537.9 2.7 collective-permute-start.23
  (160 shorter events, 68.3 us)
Async XLA Ops:
  7.2 90.7 %all-gather.4.cloned.1.call-start = ((), (), s32[]{:S(2)}) async-start(), calls=%async_computation | async-start | bytes 10137600 | tf_op jit(solution)/shard_map/all_gather | solution.py:559
  9.0 174.3 %all-gather.6.cloned.1.call-start = ((), (), s32[]{:S(2)}) async-start(), calls=%async_computation.1 | async-start | bytes 10137600 | tf_op jit(solution)/shard_map/all_gather | solution.py:561
  265.6 23.9 %collective-permute-start = (bf16[3,4,2,2,40,1280]{5,4,3,2,1,0:T(8,128)(2,1)}, bf16[3,4,2,2,40,1280]{5,4,3,2,1,0:T(8,128)(2,1)}, u32[]{:S(2)}, u32[]{:S(2)}) collective-permute-start(bf16[3,4,2,2,40,1280]{5,4,3,2,1,0:T(8,128)(2,1)} %bitcast.205), channel_id=1, source_target_pairs={{0,1},{1,0},{2,3},{3,2},{4,5},{5,4},{6,7},{7,6},{8,9},{9,8},{10,11... | collective-permute-start | bytes 14745608 | tf_op jit(solution)/shard_map/ppermute | solution.py:459
  320.5 8.7 %copy-start.10 = (bf16[3,320,2048]{2,1,0:T(8,128)(2,1)S(1)}, bf16[3,320,2048]{2,1,0:T(8,128)(2,1)}, u32[]{:S(2)}) copy-start(bf16[3,320,2048]{2,1,0:T(8,128)(2,1)} %get-tuple-element.80.rest_2_) | copy-start | bytes 11796484
  341.5 42.0 %collective-permute-start.1 = (bf16[3,2,2,2,40,1280]{5,4,3,2,1,0:T(8,128)(2,1)}, bf16[3,2,2,2,40,1280]{5,4,3,2,1,0:T(8,128)(2,1)}, u32[]{:S(2)}, u32[]{:S(2)}) collective-permute-start(bf16[3,2,2,2,40,1280]{5,4,3,2,1,0:T(8,128)(2,1)} %bitcast.34), channel_id=1, source_target_pairs={{0,1},{1,0},{2,3},{3,2},{4,5},{5,4},{6,7},{7,6},{8,9},{9,8},{10,11... | collective-permute-start | bytes 7372808 | tf_op jit(solution)/shard_map/ppermute | solution.py:459
  342.7 29.7 %collective-permute-start.3 = (bf16[3,4,2,40,640]{4,3,1,0,2:T(8,128)(2,1)}, bf16[3,4,2,40,640]{4,3,1,0,2:T(8,128)(2,1)}, u32[]{:S(2)}, u32[]{:S(2)}) collective-permute-start(bf16[3,4,2,40,640]{4,3,1,0,2:T(8,128)(2,1)} %bitcast.169), channel_id=1, source_target_pairs={{0,4},{1,5},{2,6},{3,7},{4,0},{5,1},{6,2},{7,3},{8,12},{9,13},{10,... | collective-permute-start | bytes 3686408 | tf_op jit(solution)/shard_map/ppermute | solution.py:459
  345.1 30.3 %collective-permute-start.2 = (bf16[3,4,2,40,640]{4,3,1,0,2:T(8,128)(2,1)}, bf16[3,4,2,40,640]{4,3,1,0,2:T(8,128)(2,1)}, u32[]{:S(2)}, u32[]{:S(2)}) collective-permute-start(bf16[3,4,2,40,640]{4,3,1,0,2:T(8,128)(2,1)} %bitcast.170), channel_id=1, source_target_pairs={{0,2},{1,3},{2,0},{3,1},{4,6},{5,7},{6,4},{7,5},{8,10},{9,11},{10,... | collective-permute-start | bytes 3686408 | tf_op jit(solution)/shard_map/ppermute | solution.py:459
  379.5 32.8 %collective-permute-start.7 = (bf16[3,4,40,640]{3,2,1,0:T(8,128)(2,1)}, bf16[3,4,40,640]{3,2,1,0:T(8,128)(2,1)}, u32[]{:S(2)}, u32[]{:S(2)}) collective-permute-start(bf16[3,4,40,640]{3,2,1,0:T(8,128)(2,1)} %get-tuple-element.140), channel_id=1, source_target_pairs={{0,2},{1,3},{2,0},{3,1},{4,6},{5,7},{6,4},{7,5},{8,10},{9,11},{10,... | collective-permute-start | bytes 1843208 | tf_op jit(solution)/shard_map/ppermute | solution.py:459
  382.4 29.9 %collective-permute-start.6 = (bf16[3,4,40,640]{3,2,1,0:T(8,128)(2,1)}, bf16[3,4,40,640]{3,2,1,0:T(8,128)(2,1)}, u32[]{:S(2)}, u32[]{:S(2)}) collective-permute-start(bf16[3,4,40,640]{3,2,1,0:T(8,128)(2,1)} %get-tuple-element.142), channel_id=1, source_target_pairs={{0,4},{1,5},{2,6},{3,7},{4,0},{5,1},{6,2},{7,3},{8,12},{9,13},{10,... | collective-permute-start | bytes 1843208 | tf_op jit(solution)/shard_map/ppermute | solution.py:459
  387.0 41.9 %collective-permute-start.5 = (bf16[3,2,2,40,640]{4,3,1,0,2:T(8,128)(2,1)}, bf16[3,2,2,40,640]{4,3,1,0,2:T(8,128)(2,1)S(1)}, u32[]{:S(2)}, u32[]{:S(2)}) collective-permute-start(bf16[3,2,2,40,640]{4,3,1,0,2:T(8,128)(2,1)} %copy.59), channel_id=1, source_target_pairs={{0,4},{1,5},{2,6},{3,7},{4,0},{5,1},{6,2},{7,3},{8,12},{9,13},{10,... | collective-permute-start | bytes 1843208 | tf_op jit(solution)/shard_map/ppermute | solution.py:459
  389.1 39.9 %collective-permute-start.4 = (bf16[3,2,2,40,640]{4,3,2,1,0:T(8,128)(2,1)}, bf16[3,2,2,40,640]{4,3,2,1,0:T(8,128)(2,1)}, u32[]{:S(2)}, u32[]{:S(2)}) collective-permute-start(bf16[3,2,2,40,640]{4,3,2,1,0:T(8,128)(2,1)} %get-tuple-element.146), channel_id=1, source_target_pairs={{0,2},{1,3},{2,0},{3,1},{4,6},{5,7},{6,4},{7,5},{8,10},{9,11},{10,... | collective-permute-start | bytes 1843208 | tf_op jit(solution)/shard_map/ppermute | solution.py:459
  389.4 24.2 %copy-start.3 = (bf16[3,4,40,640]{3,2,1,0:T(8,128)(2,1)S(1)}, bf16[3,4,40,640]{3,2,1,0:T(8,128)(2,1)}, u32[]{:S(2)}) copy-start(bf16[3,4,40,640]{3,2,1,0:T(8,128)(2,1)} %get-tuple-element.100) | copy-start | bytes 1843204
  414.9 14.1 %slice-start = ((s8[5242880]{0:T(1024)(128)(4,1)}), s8[4194304]{0:T(1024)(128)(4,1)S(1)}, s32[]{:S(2)}) async-start(s8[5242880]{0:T(1024)(128)(4,1)} %bitcast.212), calls=%async_computation.2 | async-start | bytes 8388608
  416.7 70.6 %collective-permute-start.24 = (bf16[3,2,40,1280]{3,2,0,1:T(8,128)(2,1)}, bf16[3,2,40,1280]{3,2,0,1:T(8,128)(2,1)}, u32[]{:S(2)}, u32[]{:S(2)}) collective-permute-start(bf16[3,2,40,1280]{3,2,0,1:T(8,128)(2,1)} %bitcast.173), channel_id=1, source_target_pairs={{0,16},{1,17},{2,18},{3,19},{4,20},{5,21},{6,22},{7,23},{8,24},{9,... | collective-permute-start | bytes 1843208 | tf_op jit(solution)/shard_map/ppermute | solution.py:459
  438.9 57.8 %collective-permute-start.10 = (bf16[3,2,2,2,40,1280]{5,4,0,1,3,2:T(8,128)(2,1)}, bf16[3,2,2,2,40,1280]{5,4,0,1,3,2:T(8,128)(2,1)}, u32[]{:S(2)}, u32[]{:S(2)}) collective-permute-start(bf16[3,2,2,2,40,1280]{5,4,0,1,3,2:T(8,128)(2,1)} %copy.61), channel_id=1, source_target_pairs={{0,1},{1,0},{2,3},{3,2},{4,5},{5,4},{6,7},{7,6},{8,9},{9,8},{10,11... | collective-permute-start | bytes 7372808 | tf_op jit(solution)/shard_map/ppermute | solution.py:459
  476.4 10.9 %copy-start.2 = (bf16[3,1,2,40,1280]{4,3,0,2,1:T(8,128)(2,1)S(1)}, bf16[3,1,2,40,1280]{4,3,0,2,1:T(8,128)(2,1)}, u32[]{:S(2)}) copy-start(bf16[3,1,2,40,1280]{4,3,0,2,1:T(8,128)(2,1)} %copy.82) | copy-start | bytes 1843204
  476.4 3.2 collective-permute-start.11
  479.7 3.8 collective-permute-start.12
  483.4 3.9 collective-permute-start.13
  483.5 16.3 %collective-permute-start.8 = (bf16[3,2,40,640]{3,2,1,0:T(8,128)(2,1)S(1)}, bf16[3,2,40,640]{3,2,1,0:T(8,128)(2,1)S(1)}, u32[]{:S(2)}, u32[]{:S(2)}) collective-permute-start(bf16[3,2,40,640]{3,2,1,0:T(8,128)(2,1)S(1)} %dynamic-slice_bitcast_fusion.22), channel_id=1, source_target_pairs={{0,4},{1,5},{2,6},{3,7},{4,0},{5,1},{6,2},{7,3},{8,12},{9,13},{10,... | collective-permute-start | bytes 921608 | tf_op jit(solution)/shard_map/ppermute | solution.py:459
  485.6 14.2 %collective-permute-start.9 = (bf16[3,2,40,640]{3,2,1,0:T(8,128)(2,1)S(1)}, bf16[3,2,40,640]{3,2,1,0:T(8,128)(2,1)S(1)}, u32[]{:S(2)}, u32[]{:S(2)}) collective-permute-start(bf16[3,2,40,640]{3,2,1,0:T(8,128)(2,1)S(1)} %dynamic-slice_bitcast_fusion.21), channel_id=1, source_target_pairs={{0,2},{1,3},{2,0},{3,1},{4,6},{5,7},{6,4},{7,5},{8,10},{9,11},{10,... | collective-permute-start | bytes 921608 | tf_op jit(solution)/shard_map/ppermute | solution.py:459
  487.3 3.7 collective-permute-start.14
  491.0 4.6 collective-permute-start.15
  492.0 7.6 %collective-permute-start.25 = (bf16[3,40,1280]{2,1,0:T(8,128)(2,1)S(1)}, bf16[3,40,1280]{2,1,0:T(8,128)(2,1)S(1)}, u32[]{:S(2)}, u32[]{:S(2)}) collective-permute-start(bf16[3,40,1280]{2,1,0:T(8,128)(2,1)S(1)} %dynamic-slice_bitcast_fusion.18), channel_id=1, source_target_pairs={{0,8},{1,9},{2,10},{3,11},{4,12},{5,13},{6,14},{7,15},{8,0},{9,1},... | collective-permute-start | bytes 921608 | tf_op jit(solution)/shard_map/ppermute | solution.py:459
  499.3 12.9 %collective-permute-start.18 = (bf16[3,2,2,40,640]{4,3,0,1,2:T(8,128)(2,1)S(1)}, bf16[3,2,2,40,640]{4,3,0,1,2:T(8,128)(2,1)S(1)}, u32[]{:S(2)}, u32[]{:S(2)}) collective-permute-start(bf16[3,2,2,40,640]{4,3,0,1,2:T(8,128)(2,1)S(1)} %dynamic-slice_bitcast_fusion.9), channel_id=1, source_target_pairs={{0,2},{1,3},{2,0},{3,1},{4,6},{5,7},{6,4},{7,5},{8,10},{9,11},{10,... | collective-permute-start | bytes 1843208 | tf_op jit(solution)/shard_map/ppermute | solution.py:459
  499.8 14.8 %collective-permute-start.20 = (bf16[3,2,2,40,640]{4,3,0,1,2:T(8,128)(2,1)S(1)}, bf16[3,2,2,40,640]{4,3,0,1,2:T(8,128)(2,1)S(1)}, u32[]{:S(2)}, u32[]{:S(2)}) collective-permute-start(bf16[3,2,2,40,640]{4,3,0,1,2:T(8,128)(2,1)S(1)} %dynamic-slice_bitcast_fusion.8), channel_id=1, source_target_pairs={{0,4},{1,5},{2,6},{3,7},{4,0},{5,1},{6,2},{7,3},{8,12},{9,13},{10,... | collective-permute-start | bytes 1843208 | tf_op jit(solution)/shard_map/ppermute | solution.py:459
  512.4 6.9 %collective-permute-start.19 = (bf16[3,2,40,640]{3,2,0,1:T(8,128)(2,1)S(1)}, bf16[3,2,40,640]{3,2,0,1:T(8,128)(2,1)S(1)}, u32[]{:S(2)}, u32[]{:S(2)}) collective-permute-start(bf16[3,2,40,640]{3,2,0,1:T(8,128)(2,1)S(1)} %dynamic-slice_bitcast_fusion.20), channel_id=1, source_target_pairs={{0,4},{1,5},{2,6},{3,7},{4,0},{5,1},{6,2},{7,3},{8,12},{9,13},{10,... | collective-permute-start | bytes 921608 | tf_op jit(solution)/shard_map/ppermute | solution.py:459
  514.8 6.9 %collective-permute-start.21 = (bf16[3,2,40,640]{3,2,0,1:T(8,128)(2,1)S(1)}, bf16[3,2,40,640]{3,2,0,1:T(8,128)(2,1)S(1)}, u32[]{:S(2)}, u32[]{:S(2)}) collective-permute-start(bf16[3,2,40,640]{3,2,0,1:T(8,128)(2,1)S(1)} %dynamic-slice_bitcast_fusion.19), channel_id=1, source_target_pairs={{0,2},{1,3},{2,0},{3,1},{4,6},{5,7},{6,4},{7,5},{8,10},{9,11},{10,... | collective-permute-start | bytes 921608 | tf_op jit(solution)/shard_map/ppermute | solution.py:459
  516.1 18.4 %collective-permute-start.16 = (bf16[3,1,40,1280]{3,2,1,0:T(8,128)(2,1)S(1)}, bf16[3,1,40,1280]{3,2,1,0:T(8,128)(2,1)S(1)}, u32[]{:S(2)}, u32[]{:S(2)}) collective-permute-start(bf16[3,1,40,1280]{3,2,1,0:T(8,128)(2,1)S(1)} %fusion.13), channel_id=1, source_target_pairs={{0,16},{1,17},{2,18},{3,19},{4,20},{5,21},{6,22},{7,23},{8,24},{9,... | collective-permute-start | bytes 921608 | tf_op jit(solution)/shard_map/ppermute | solution.py:459
  521.8 16.0 %collective-permute-start.22 = (bf16[3,1,40,1280]{3,2,0,1:T(8,128)(2,1)S(1)}, bf16[3,1,40,1280]{3,2,0,1:T(8,128)(2,1)S(1)}, u32[]{:S(2)}, u32[]{:S(2)}) collective-permute-start(bf16[3,1,40,1280]{3,2,0,1:T(8,128)(2,1)S(1)} %fusion.11), channel_id=1, source_target_pairs={{0,16},{1,17},{2,18},{3,19},{4,20},{5,21},{6,22},{7,23},{8,24},{9,... | collective-permute-start | bytes 921608 | tf_op jit(solution)/shard_map/ppermute | solution.py:459
  534.6 8.7 %collective-permute-start.17 = (bf16[3,40,1280]{2,1,0:T(8,128)(2,1)S(1)}, bf16[3,40,1280]{2,1,0:T(8,128)(2,1)S(1)}, u32[]{:S(2)}, u32[]{:S(2)}) collective-permute-start(bf16[3,40,1280]{2,1,0:T(8,128)(2,1)S(1)} %fusion.9), channel_id=1, source_target_pairs={{8,0},{9,1},{10,2},{11,3},{12,4},{13,5},{14,6},{15,7},{24,16},{25,... | collective-permute-start | bytes 921608 | tf_op jit(solution)/shard_map/ppermute | solution.py:518
  537.9 7.0 %collective-permute-start.23 = (bf16[3,40,1280]{2,1,0:T(8,128)(2,1)S(1)}, bf16[3,40,1280]{2,1,0:T(8,128)(2,1)S(1)}, u32[]{:S(2)}, u32[]{:S(2)}) collective-permute-start(bf16[3,40,1280]{2,1,0:T(8,128)(2,1)S(1)} %fusion.10), channel_id=1, source_target_pairs={{0,8},{1,9},{2,10},{3,11},{4,12},{5,13},{6,14},{7,15},{16,24},{17,... | collective-permute-start | bytes 921608 | tf_op jit(solution)/shard_map/ppermute | solution.py:518
  (12 other events, 79.0 us)
Sparse Core Ops, SparseCore 0:
  11.5 86.4 all-gather.3
  100.8 82.4 all-gather.5

commit v3 on v1

v3 whole, which is shorter than its diff:
```python
import functools
import math

import jax
import jax.numpy as jnp
from jax import lax
from jax.experimental import pallas as pl
from jax.experimental.pallas import tpu as pltpu
from jax.sharding import PartitionSpec as P

EPSILON = 1e-06
AXIS = "fsdp"
BLOCKS = 4
TILE = 256
EXTRA = 16
HEADS_PER_STEP = 4
LOW = jnp.bfloat16
LOG2E = math.log2(math.e)
LN2 = math.log(2.0)
NN = (((1,), (0,)), ((), ()))
NT = (((1,), (1,)), ((), ()))
TN = (((0,), (0,)), ((), ()))
TT = (((0,), (1,)), ((), ()))


def dot(left, right, dims):
    return lax.dot_general(left, right, dims, preferred_element_type=jnp.float32)


def three_rows(value, base, at):
    row = lax.broadcasted_iota(jnp.int32, (EXTRA, value.shape[1]), 0)
    first = value.astype(LOW).astype(jnp.float32)
    rest = value - first
    second = rest.astype(LOW).astype(jnp.float32)
    third = rest - second
    rows = jnp.where(row == at + 1, second, jnp.where(row == at + 2, third, base))
    return jnp.where(row == at, first, rows).astype(LOW)


def fold(x, op):
    return op(x.reshape(x.shape[0] // 8, 8, x.shape[1]), axis=0)


def for_each_tile(length, count_of, body):
    @pl.loop(0, length // TILE)
    def _(t):
        count = count_of(t)
        for n in range(1, length // TILE + 1):

            @pl.when(count == n)
            def _(n=n):
                body(pl.ds(pl.multiple_of(t * TILE, TILE), TILE), n)


def attention_forward_kernel(
    heads, depth, length, counts, normed_ref, mine_ref, other_ref, factor_ref, qx_ref, kx_ref,
    qkv_ref, o_ref, lse_ref, kn, sb,
):
    s = pl.program_id(0)
    unit = depth // 2
    for at in range(0, length, TILE):
        normed = normed_ref[at : at + TILE, :]
        for part, w_ref in enumerate((mine_ref, other_ref)):
            y = dot(w_ref[...], normed, NT)
            for h in range(heads):
                for i in range(3):
                    rows = y[(3 * h + i) * unit : (3 * h + i + 1) * unit]
                    if i == 0:
                        rows = rows * factor_ref[part * unit : (part + 1) * unit, :]
                    start = h * depth + part * unit
                    qkv_ref[i, start : start + unit, at : at + TILE] = rows.astype(LOW)
    q_ref, k_ref, v_ref = qkv_ref.at[0], qkv_ref.at[1], qkv_ref.at[2]
    for h in range(heads):
        kn[h] = jnp.concatenate([k_ref[h * depth : (h + 1) * depth, :], kx_ref[...]], axis=0).T

    def tile(qs, n):
        qx = qx_ref[:, qs]
        peaks = [None] * (heads + 1)
        for h in range(heads + 1):
            out = total = None
            if h > 0:
                peak = jnp.max(peaks[h - 1], axis=0, keepdims=True)
            for c in range(n):
                ks = slice(c * TILE, (c + 1) * TILE)
                if h < heads:
                    q = jnp.concatenate([q_ref[h * depth : (h + 1) * depth, qs], qx], axis=0)
                    scores = dot(kn[h, ks, :], q, NN)
                    sb[h % 2, ks, :] = scores
                    part = fold(scores, jnp.max)
                    peaks[h] = part if c == 0 else jnp.maximum(peaks[h], part)
                if h > 0:
                    p = jnp.exp2(sb[(h - 1) % 2, ks, :] - peak)
                    part = fold(p, jnp.sum)
                    total = part if c == 0 else total + part
                    part = dot(v_ref[(h - 1) * depth : h * depth, ks], p.astype(LOW), NN)
                    out = part if c == 0 else out + part
            if h > 0:
                total = jnp.sum(total, axis=0, keepdims=True)
                o_ref[(h - 1) * depth : h * depth, qs] = (out * (1.0 / total)).astype(LOW)
                lse_ref[h - 1, :, qs] = peak + jnp.log2(total)

    for_each_tile(length, lambda t: counts[s, t], tile)


def attention_forward(normed, mine, other, factor, qx, kx, counts, depth, length):
    tokens, width = normed.shape
    seqs = tokens // length
    heads = mine.shape[0] * 2 // (3 * depth)
    group = heads * depth
    extra = pl.BlockSpec((EXTRA, length), lambda s, counts: (0, s))
    weight = pl.BlockSpec(mine.shape, lambda s, counts: (0, 0))
    return pl.pallas_call(
        functools.partial(attention_forward_kernel, heads, depth, length),
        grid_spec=pltpu.PrefetchScalarGridSpec(
            num_scalar_prefetch=1,
            grid=(seqs,),
            in_specs=[
                pl.BlockSpec((length, width), lambda s, counts: (s, 0)),
                weight,
                weight,
                pl.BlockSpec((depth, TILE), lambda s, counts: (0, 0)),
                extra,
                extra,
            ],
            out_specs=[
                pl.BlockSpec((3, group, length), lambda s, counts: (0, 0, s)),
                pl.BlockSpec((group, length), lambda s, counts: (0, s)),
                pl.BlockSpec((heads, 1, length), lambda s, counts: (0, 0, s)),
            ],
            scratch_shapes=[
                pltpu.VMEM((heads, length, depth + EXTRA), LOW),
                pltpu.VMEM((2, length, TILE), jnp.float32),
            ],
        ),
        out_shape=[
            jax.ShapeDtypeStruct((3, group, tokens), LOW),
            jax.ShapeDtypeStruct((group, tokens), LOW),
            jax.ShapeDtypeStruct((heads, 1, tokens), jnp.float32),
        ],
        cost_estimate=pl.CostEstimate(
            flops=4 * heads * 256 * length * tokens + 6 * group * tokens * width,
            bytes_accessed=2 * tokens * width + 8 * group * tokens,
            transcendentals=heads * length * tokens,
        ),
        name="attention_forward",
    )(counts, normed, mine, other, factor, qx, kx)


def attention_backward_kernel(
    heads,
    depth,
    length,
    ahead,
    counts,
    q_ref,
    k_ref,
    v_ref,
    o_ref,
    do_ref,
    lse_ref,
    qx_ref,
    kx_ref,
    factor_ref,
    d_ref,
    scale_ref,
    kn,
    vn,
    dka,
    dva,
):
    s = pl.program_id(0)
    unit = depth // 2

    @pl.when(s == 0)
    def _():
        scale_ref[...] = jnp.zeros_like(scale_ref)

    dka[...] = jnp.zeros_like(dka)
    dva[...] = jnp.zeros_like(dva)
    ones = jnp.where(lax.broadcasted_iota(jnp.int32, (EXTRA, length), 0) < 3, 1.0, 0.0).astype(LOW)
    for h in range(heads):
        hs = slice(h * depth, (h + 1) * depth)
        kn[h] = jnp.concatenate([k_ref[hs, :], kx_ref[...]], axis=0).T
        vn[h] = jnp.concatenate([v_ref[hs, :], ones], axis=0).T

    def put(h, i, columns, value):
        for part in range(2):
            start = ((part * heads + h) * 3 + i) * unit
            rows = value[part * unit : (part + 1) * unit]
            d_ref[start : start + unit, columns] = rows.astype(LOW)

    def tile(qs, n):
        base = qx_ref[:, qs].astype(jnp.float32)
        queries, grads = [], []
        items = [(h, c) for h in range(heads) for c in range(n)]

        def first(i):
            h, c = items[i]
            hs, ks = slice(h * depth, (h + 1) * depth), slice(c * TILE, (c + 1) * TILE)
            if c == 0:
                q, do, o = q_ref[hs, qs], do_ref[hs, qs], o_ref[hs, qs]
                centre = jnp.sum(
                    do.astype(jnp.float32) * o.astype(jnp.float32), axis=0, keepdims=True
                )
                queries.append(
                    jnp.concatenate([q, three_rows(-lse_ref[h, :, qs], base, 4)], axis=0)
                )
                grads.append(jnp.concatenate([do, three_rows(-centre, 0.0, 0)], axis=0))
            return dot(kn[h, ks, :], queries[h], NN), dot(vn[h, ks, :], grads[h], NN)

        pending = [first(i) for i in range(min(ahead, len(items)))]
        dq = None
        for i, (h, c) in enumerate(items):
            if i + ahead < len(items):
                pending.append(first(i + ahead))
            scores, dp = pending[i]
            pending[i] = None
            hs, ks = slice(h * depth, (h + 1) * depth), slice(c * TILE, (c + 1) * TILE)
            p = jnp.exp2(scores)
            ds = (p * dp).astype(LOW)
            dva[hs, ks] += dot(do_ref[hs, qs], p.astype(LOW), NT)
            dka[hs, ks] += dot(q_ref[hs, qs], ds, NT)
            part = dot(k_ref[hs, ks], ds, NN)
            dq = part if c == 0 else dq + part
            if c == n - 1:
                put(h, 0, qs, dq * factor_ref[...])
                scale_ref[...] += dq * q_ref[hs, qs].astype(jnp.float32)

    for_each_tile(length, lambda t: counts[s, t], tile)
    for h in range(heads):
        put(h, 1, slice(None), dka[h * depth : (h + 1) * depth, :] * LN2)
        put(h, 2, slice(None), dva[h * depth : (h + 1) * depth, :])


def attention_backward(qkv, context, grad_context, lse, qx, kx, counts, factor, depth, length):
    _, group, tokens = qkv.shape
    heads, seqs = group // depth, tokens // length

    def third(i):
        return pl.BlockSpec((None, group, length), lambda s, counts: (i, 0, s))

    whole = pl.BlockSpec((group, length), lambda s, counts: (0, s))
    extra = pl.BlockSpec((EXTRA, length), lambda s, counts: (0, s))
    fixed = pl.BlockSpec((depth, TILE), lambda s, counts: (0, 0))
    return pl.pallas_call(
        functools.partial(attention_backward_kernel, heads, depth, length, 1),
        grid_spec=pltpu.PrefetchScalarGridSpec(
            num_scalar_prefetch=1,
            grid=(seqs,),
            in_specs=[
                third(0),
                third(1),
                third(2),
                whole,
                whole,
                pl.BlockSpec((heads, 1, length), lambda s, counts: (0, 0, s)),
                extra,
                extra,
                fixed,
            ],
            out_specs=[pl.BlockSpec((3 * group, length), lambda s, counts: (0, s)), fixed],
            scratch_shapes=[
                pltpu.VMEM((heads, length, depth + EXTRA), LOW),
                pltpu.VMEM((heads, length, depth + EXTRA), LOW),
                pltpu.VMEM((group, length), jnp.float32),
                pltpu.VMEM((group, length), jnp.float32),
            ],
        ),
        out_shape=[
            jax.ShapeDtypeStruct((3 * group, tokens), LOW),
            jax.ShapeDtypeStruct((depth, TILE), jnp.float32),
        ],
        cost_estimate=pl.CostEstimate(
            flops=7 * heads * 256 * length * tokens,
            bytes_accessed=16 * group * tokens,
            transcendentals=heads * length * tokens,
        ),
        name="attention_backward",
    )(counts, qkv, qkv, qkv, context, grad_context, lse, qx, kx, factor)


def mean_rows(x):
    return jnp.mean(x, axis=-1, keepdims=True)


def middle_kernel(
    unit,
    groups,
    core_ref,
    place_ref,
    x_ref,
    g_ref,
    gain_ref,
    w_ref,
    *rest,
):
    context_refs, rest = rest[:groups], rest[groups:]
    out_ref, grad_hidden_ref, *rest = rest
    grad_context_refs, rest = rest[:groups], rest[groups:]
    keep_ref, send_ref, gain_grad_ref, total, turned = rest
    step = pl.program_id(0)
    core = core_ref[0]
    heads = place_ref.shape[0] // groups

    def pieces():
        for j in range(groups * heads):
            for part in range(2):
                at = (2 * place_ref[j] + (core + part) % 2) * unit
                start = (2 * (j % heads) + part) * unit
                yield j // heads, slice(start, start + unit), pl.ds(pl.multiple_of(at, 8), unit)

    @pl.when(step == 0)
    def _():
        total[...] = jnp.zeros_like(total)
        gain_grad_ref[...] = jnp.zeros_like(gain_grad_ref)

    g = g_ref[...]
    gain = gain_ref[...]
    for p, rows, at in pieces():
        turned[at, :] = context_refs[p][rows, :].astype(jnp.float32)
    context = turned[...].astype(LOW).T
    hidden = x_ref[...].astype(jnp.float32) + dot(context, w_ref[0], NT)
    root = lax.rsqrt(mean_rows(hidden * hidden) + EPSILON)
    scaled = hidden * root
    normed = (scaled * gain).astype(LOW)
    upward = dot(normed, w_ref[1], NT)
    s = jax.nn.sigmoid(upward)
    activated = (upward * s).astype(LOW)
    out_ref[...] = (hidden + dot(activated, w_ref[2], NT)).astype(LOW)
    slope = s * (1.0 + upward * (1.0 - s))
    grad_upward = (dot(g, w_ref[2], NN) * slope).astype(LOW)
    total[2] += dot(g.T, activated, NN)
    grad_normed = dot(grad_upward, w_ref[1], NN)
    total[1] += dot(grad_upward.T, normed, NN)
    gain_grad_ref[...] += fold(grad_normed * scaled, jnp.sum)
    w = grad_normed * gain
    grad_hidden = g.astype(jnp.float32) + root * (w - scaled * mean_rows(w * scaled))
    grad_hidden_ref[...] = grad_hidden
    branch = grad_hidden.astype(LOW)
    turned[...] = dot(branch, w_ref[0], NN).astype(LOW).T.astype(jnp.float32)
    for p, rows, at in pieces():
        grad_context_refs[p][rows, :] = turned[at, :].astype(LOW)
    total[0] += dot(branch.T, context, NN)

    @pl.when(step == pl.num_programs(0) - 1)
    def _():
        @pl.loop(0, groups * heads)
        def _(j):
            for i in range(3):
                at = pl.multiple_of((2 * place_ref[j] + core) * unit, 8)
                keep_ref[j, i] = total[i, pl.ds(at, unit), :].astype(LOW)
                at = pl.multiple_of((2 * place_ref[j] + 1 - core) * unit, 8)
                send_ref[j, i] = total[i, pl.ds(at, unit), :].astype(LOW)


def middle(core, place, x, g, gain, weight, contexts, unit):
    tokens, width = x.shape
    chips = width // (2 * unit)
    rows = pl.BlockSpec((TILE, width), lambda i, core, place: (i, 0))
    columns = [
        pl.BlockSpec((c.shape[0], TILE), lambda i, core, place: (0, i)) for c in contexts
    ]
    once = pl.Buffered(1)
    half = pl.BlockSpec(
        (chips, 3, unit, width), lambda i, core, place: (0, 0, 0, 0), pipeline_mode=once
    )
    halves = jax.ShapeDtypeStruct((chips, 3, unit, width), LOW)
    return pl.pallas_call(
        functools.partial(middle_kernel, unit, len(contexts)),
        grid_spec=pltpu.PrefetchScalarGridSpec(
            num_scalar_prefetch=2,
            grid=(tokens // TILE,),
            in_specs=[
                rows,
                rows,
                pl.BlockSpec((1, width), lambda i, core, place: (0, 0)),
                pl.BlockSpec(
                    (3, width, width), lambda i, core, place: (0, 0, 0), pipeline_mode=once
                ),
                *columns,
            ],
            out_specs=[
                rows,
                rows,
                *columns,
                half,
                half,
                pl.BlockSpec((8, width), lambda i, core, place: (0, 0)),
            ],
            scratch_shapes=[
                pltpu.VMEM((3, width, width), jnp.float32),
                pltpu.VMEM((width, TILE), jnp.float32),
            ],
        ),
        out_shape=[
            jax.ShapeDtypeStruct((tokens, width), LOW),
            jax.ShapeDtypeStruct((tokens, width), jnp.float32),
            *[jax.ShapeDtypeStruct(c.shape, LOW) for c in contexts],
            halves,
            halves,
            jax.ShapeDtypeStruct((8, width), jnp.float32),
        ],
        compiler_params=pltpu.CompilerParams(vmem_limit_bytes=66_000_000),
        cost_estimate=pl.CostEstimate(
            flops=18 * tokens * width * width,
            bytes_accessed=14 * tokens * width + 12 * width * width,
            transcendentals=tokens * width,
        ),
        name="middle",
    )(core, place, x, g, gain, weight, *contexts)


def back_kernel(groups, x_ref, grad_hidden_ref, gain_ref, *rest):
    w_refs, d_refs, (out_ref, gain_grad_ref) = rest[: 2 * groups], rest[2 * groups : -2], rest[-2:]

    @pl.when(pl.program_id(0) == 0)
    def _():
        gain_grad_ref[...] = jnp.zeros_like(gain_grad_ref)

    x = x_ref[...].astype(jnp.float32)
    root = lax.rsqrt(mean_rows(x * x) + EPSILON)
    scaled = x * root
    grad_normed = None
    for p in range(groups):
        d = d_refs[p][...].T
        rows = d.shape[1] // 2
        for i in range(2):
            part = dot(d[:, i * rows : (i + 1) * rows], w_refs[2 * p + i][...], NN)
            grad_normed = part if grad_normed is None else grad_normed + part
    gain_grad_ref[...] += fold(grad_normed * scaled, jnp.sum)
    w = grad_normed * gain_ref[...]
    out_ref[...] = grad_hidden_ref[...] + root * (w - scaled * mean_rows(w * scaled))


def back(x, grad_hidden, gain, weights, grads):
    tokens, width = x.shape
    rows = pl.BlockSpec((TILE, width), lambda i: (i, 0))
    return pl.pallas_call(
        functools.partial(back_kernel, len(grads)),
        grid=(tokens // TILE,),
        in_specs=[
            rows,
            rows,
            pl.BlockSpec((1, width), lambda i: (0, 0)),
            *[pl.BlockSpec(w.shape, lambda i: (0, 0)) for w in weights],
            *[pl.BlockSpec((d.shape[0], TILE), lambda i: (0, i)) for d in grads],
        ],
        out_specs=[rows, pl.BlockSpec((8, width), lambda i: (0, 0))],
        out_shape=[
            jax.ShapeDtypeStruct((tokens, width), jnp.float32),
            jax.ShapeDtypeStruct((8, width), jnp.float32),
        ],
        cost_estimate=pl.CostEstimate(
            flops=6 * tokens * width * width, bytes_accessed=18 * tokens * width, transcendentals=0
        ),
        name="back",
    )(x, grad_hidden, gain, *weights, *grads)


GROUPS = ((0, 1, 2, 4), (3, 5, 6, 8), (7, 9, 10, 12), (11, 13, 14, 15))
FULL = 32
FAR = ((16, 0), (8, 3), (16, 0))


def exchange(x, bit, n):
    return lax.ppermute(x, AXIS, [(i, i ^ bit) for i in range(n)])


def tie(*values):
    return lax.optimization_barrier(values)


def next_group(group, step, n):
    bit, source = FAR[step]
    return [
        exchange(group[2:4], 2, n),
        exchange(group[3:4], 4, n),
        exchange(group[source : source + 1], bit, n),
    ]


def add(*terms):
    return functools.reduce(jnp.add, [t.astype(jnp.float32) for t in terms])


def send_group(terms, step, n):
    sums = [add(*t).astype(LOW) for t in terms]
    if step == 0:
        away = sums[1:]
        return [exchange(x, bit, n) for x, bit in zip(away, (2, 4, 8))], away
    away = [jnp.stack(sums[:2]), sums[2], sums[3]]
    return [exchange(x, bit, n) for x, bit in zip(away, (2, 4, FAR[step - 1][0]))], away


def arrivals(came, step):
    terms = [[], [], [came[0][0]], [came[0][1], came[1]]]
    terms[FAR[step - 1][1]].append(came[2])
    return terms


def sum_all(x, n):
    if n & (n - 1):
        return lax.psum(x, AXIS)
    bit = 1
    while bit < n:
        x = x + exchange(x, bit, n)
        bit *= 2
    return x


def gather_small(x, n):
    if n != FULL:
        return lax.all_gather(x, AXIS)
    x = jnp.stack([x, exchange(x, 1, n)])
    x = jnp.concatenate([x] + [exchange(x, bit, n) for bit in (2, 4, 6)])
    x = jnp.concatenate([x] + [exchange(x, bit, n) for bit in (8, 16, 24)])
    for axis, bit in ((0, 16), (1, 8), (2, 4), (3, 2), (4, 1)):
        x = x.reshape(2, 2, 2, 2, 2, -1)
        x = jnp.where((lax.axis_index(AXIS) // bit) % 2 == 1, jnp.flip(x, axis), x)
    return x.reshape(n, -1)


def on_device(n, *arguments):
    (
        inputs,
        block_ids,
        cotangent,
        first_gain,
        query_weight,
        key_weight,
        value_weight,
        output_weight,
        second_gain,
        up_weight,
        down_weight,
        query_scale,
    ) = arguments
    seqs, length, width = inputs.shape
    tokens = seqs * length
    depth = query_scale.shape[0]
    unit = depth // 2
    shard = first_gain.shape[0]
    me = lax.axis_index(AXIS)
    whole = n == FULL
    here = me if whole else jnp.zeros_like(me)
    core = (here % 2).reshape(1)
    slots = jnp.array([r for group in GROUPS for r in group], jnp.int32)
    place = jnp.bitwise_xor(here // 2, slots)

    early = jnp.stack([query_weight.T, key_weight.T, value_weight.T])
    late = jnp.stack([output_weight.T, up_weight.T, down_weight.T])
    gains = jnp.concatenate([first_gain, second_gain]).astype(jnp.float32)
    gains = gather_small(gains, n).reshape(n, 2, shard)
    gains = jnp.swapaxes(gains, 0, 1).reshape(2, width)

    ids = block_ids.reshape(1, tokens)
    row = lax.broadcasted_iota(jnp.int32, (EXTRA, tokens), 0)
    qx = ((ids == row) & (row < BLOCKS)).astype(LOW)
    kx = jnp.where(
        row < BLOCKS, jnp.where(ids > row, -1e30, 0.0), jnp.where(row < BLOCKS + 3, 1.0, 0.0)
    ).astype(LOW)
    last = block_ids[:, TILE - 1 :: TILE]
    seen = jnp.sum(block_ids[:, None, :] <= last[:, :, None], axis=-1)
    counts = ((seen + TILE - 1) // TILE).astype(jnp.int32)

    x = inputs.reshape(tokens, width)
    g = cotangent.reshape(tokens, width)
    factor = query_scale / math.sqrt(depth)
    mine_first = jnp.where(core[0] == 0, factor, jnp.roll(factor, unit))
    factor_rows = jnp.broadcast_to(mine_first[:, None], (depth, TILE))
    wide = x.astype(jnp.float32)
    root = lax.rsqrt(jnp.mean(wide * wide, axis=-1, keepdims=True) + EPSILON)
    normed = (wide * root * gains[0]).astype(LOW)

    def forward(mine, other, normed):
        return attention_forward(
            normed, mine.reshape(-1, width), other.reshape(-1, width), factor_rows * LOG2E,
            qx, kx, counts, depth, length,
        )

    mines, others, firsts = [], [], []
    if whole:
        mine = jnp.stack([early] + [exchange(early, bit, n) for bit in (2, 4, 8)])
        for step in range(4):
            other = exchange(mine, 1, n)
            mines.append(mine)
            others.append(other)
            if step < 3:
                came = next_group(mine, step, n)
                mine, normed = tie(mine, normed)
            result = forward(mine, other, normed)
            if step < 3:
                *came, first = tie(*came, result[0])
                result = [first, *result[1:]]
                mine = jnp.concatenate(came)
            firsts.append(result)
    else:
        both = lax.all_gather(early, AXIS, axis=1, tiled=True)
        both = both.reshape(3, -1, 2, unit, width)
        for group in GROUPS:
            rows = jnp.stack([both[:, r] for r in group])
            mines.append(rows[:, :, 0])
            others.append(rows[:, :, 1])
            firsts.append(forward(mines[-1], others[-1], normed))
    late = lax.all_gather(late, AXIS, axis=1, tiled=True)
    contexts = [context for _, context, _ in firsts]
    output, grad_hidden, *rest = middle(core, place, x, g, gains[1:], late, contexts, unit)
    grad_contexts, (keep, send, gain2_rows) = rest[:4], rest[4:]

    def backward(p, grad_context):
        qkv, context, lse = firsts[p]
        return attention_backward(
            qkv, context, grad_context, lse, qx, kx, counts, factor_rows, depth, length
        )

    def weight_grad(rows):
        return dot(rows, normed, NN).astype(LOW)

    grads, scale_parts = [None] * 4, []
    if whole:
        late_came = exchange(send, 1, n)
        came = None
        for p in (3, 2, 1, 0):
            grad_context = grad_contexts[p]
            if came is not None:
                *away, grad_context = tie(*away, grad_context)
            d, part = backward(p, grad_context)
            scale_parts.append(part)
            half = d.shape[0] // 2
            own_send = weight_grad(d[half:]).reshape(4, 3, unit, width)
            own_came = exchange(own_send, 1, n)
            own_keep = weight_grad(d[:half]).reshape(4, 3, unit, width)
            if p == 3:
                late_came, d = tie(late_came, d)
            else:
                *came, d = tie(*came, d)
            own_keep, own_came = tie(own_keep, own_came)
            grads[p] = d
            terms = [
                [
                    jnp.concatenate([own_keep[i], keep[4 * p + i]]),
                    jnp.concatenate([own_came[i], late_came[4 * p + i]]),
                ]
                for i in range(4)
            ]
            if came is not None:
                terms = [a + b for a, b in zip(terms, arrivals(came, p + 1))]
            came, away = send_group(terms, p, n)
        final = terms[0]
    else:
        for p in range(4):
            grads[p], part = backward(p, grad_contexts[p])
            scale_parts.append(part)
        order = jnp.argsort(slots)
        late_rows = jnp.stack([keep, send], axis=2)[order]
        own_rows = jnp.stack([weight_grad(d).reshape(2, 4, 3, unit, width) for d in grads])
        own_rows = own_rows.transpose(0, 2, 3, 1, 4, 5).reshape(16, 3, 2, unit, width)[order]
        rows = jnp.concatenate([own_rows, late_rows], axis=1).astype(jnp.float32)
        rows = rows.transpose(1, 0, 2, 3, 4).reshape(6, width, width)
        sums = lax.psum_scatter(rows, AXIS, scatter_dimension=1, tiled=True)

    weights = [w.reshape(-1, width) for pair in zip(mines, others) for w in pair]
    grad_inputs, gain1_rows = back(x, grad_hidden, gains[:1], weights, grads)
    if whole:
        *came, grad_inputs = tie(*came, grad_inputs)
        sums = add(*final, *came)
    scale_part = jnp.sum(functools.reduce(jnp.add, scale_parts), axis=1)
    scale_part = jnp.where(core[0] == 0, scale_part, jnp.roll(scale_part, unit))
    scale_part = scale_part / (factor * LOG2E) / math.sqrt(depth)
    grad_gain1, grad_gain2 = jnp.sum(gain1_rows, axis=0), jnp.sum(gain2_rows, axis=0)
    small = sum_all(jnp.concatenate([grad_gain1, grad_gain2, scale_part]), n)
    gain1 = lax.dynamic_slice_in_dim(small, me * shard, shard)
    gain2 = lax.dynamic_slice_in_dim(small, width + me * shard, shard)

    return (
        output.reshape(seqs, length, width),
        grad_inputs.reshape(seqs, length, width),
        gain1,
        sums[0].T,
        sums[1].T,
        sums[2].T,
        sums[3].T,
        gain2,
        sums[4].T,
        sums[5].T,
        small[2 * width :],
    )


def solution(mesh):
    rows, columns = P(AXIS), P(None, AXIS)
    in_specs = (rows, rows, rows, rows, *[columns] * 4, rows, columns, columns, P())
    out_specs = (rows, rows, rows, *[columns] * 4, rows, columns, columns, P())
    return jax.shard_map(
        functools.partial(on_device, mesh.shape[AXIS]),
        mesh=mesh,
        in_specs=in_specs,
        out_specs=out_specs,
        check_vma=False,
    )
```

time: 640 us -> 520 us (0.81)
  matrix products: 214 us -> 46.1 us
  Pallas kernels: 133 us -> 283 us
  waiting for transfers between devices: 128 us -> 69.2 us
  blocking collectives: 43.3 us -> 0 us
  starting transfers between devices: 21.5 us -> 43.9 us
  other arithmetic: 50.7 us -> 34.2 us
    dot_general x14 -> x8, matrix products: 214 us -> 46.1 us  [dot(): lax.dot_general(left, right, dims, preferred_element_type=jnp.float32)]
    pallas_call x0 -> x2, Pallas kernels: none -> 118 us  [the longest x1 84.5 us: middle(): pl.pallas_call(functools.partial(middle_kernel, unit, len(contexts)), gri...]
    all_gather x1 -> x0, blocking collectives: 43.3 us -> none  [on_device(): lax.all_gather(jnp.stack([first_gain, second_gain]).astype(jnp.float32),...]
    pallas_call x1 -> x4, Pallas kernels: 48.1 us -> 78.5 us  [attention_forward(): pl.pallas_call(functools.partial(attention_forward_kernel, heads, depth,...]
    all_gather x1 -> x0, waiting for transfers between devices: 27.1 us -> none  [on_device(): lax.all_gather(wide, AXIS, axis=1, tiled=True).reshape(3 * width, width)]
    ppermute x24 -> x45, starting transfers between devices: 18 us -> 43.9 us  [exchange(): return lax.ppermute(x, AXIS, [(i, i ^ bit) for i in range(n)])]
    ppermute x24 -> x45, waiting for transfers between devices: 91.2 us -> 69.2 us  [exchange(): return lax.ppermute(x, AXIS, [(i, i ^ bit) for i in range(n)])]
    sub x2 -> x0, other arithmetic: 18.7 us -> none  [the longest x1 11.5 us: on_device(): grad_hidden + root1 * w]
  transfers between devices with their start and end apart: 28 -> 46, of which waited for: 14 -> 17; matrix products, arithmetic and copies ran while one was open for 26% -> 15% of each run, Pallas kernels for 8% -> 38%
where the time goes in v3:
time: 520 us; the launch traced here: 517 us
  Pallas kernels  283 us (54%)
  waiting for transfers between devices  69.2 us (13%)
  matrix products  46.1 us (9%)
  starting transfers between devices  43.9 us (8%)
  other arithmetic  34.2 us (7%)
  local copies, waits for them, and re-layouts  24.6 us (5%)
  between operations  15.2 us (3%)
    pallas_call x4, Pallas kernels, attention_backward(): pl.pallas_call(functools.partial(attention_backward_kernel, heads, depth,...  86.3 us
    pallas_call x1, Pallas kernels, middle(): pl.pallas_call(functools.partial(middle_kernel, unit, len(contexts)), gri...  84.5 us
    pallas_call x4, Pallas kernels, attention_forward(): pl.pallas_call(functools.partial(attention_forward_kernel, heads, depth,...  78.5 us
    ppermute x45, waiting for transfers between devices, exchange(): return lax.ppermute(x, AXIS, [(i, i ^ bit) for i in range(n)])  69.2 us
    dot_general x8, matrix products, dot(): lax.dot_general(left, right, dims, preferred_element_type=jnp.float32)  46.1 us
    ppermute x45, starting transfers between devices, exchange(): return lax.ppermute(x, AXIS, [(i, i ^ bit) for i in range(n)])  43.9 us
    pallas_call x1, Pallas kernels, back(): pl.pallas_call(functools.partial(back_kernel, len(grads)), grid=(tokens /...  34 us
    convert_element_type x10, other arithmetic, send_group(): sums = [add(*t).astype(LOW) for t in terms]  11.5 us
  transfers between devices with their start and end apart: 46, of which 17 were waited for; matrix products, arithmetic and copies ran while one was open for 15% of the time, Pallas kernels for 38%

profile of v3, /device:TPU:0, one launch (start us, length us, event | category | flops | bytes accessed | tf_op | source)
XLA Modules:
  0.0 516.5 jit_solution(16595254591268975437)
XLA Ops:
  10.1 3.1 collective-permute-start.9
  16.0 3.6 multiply_reduce_fusion
  39.6 6.5 %multiply_convert_fusion.normed_ref = bf16[2048,1280]{1,0:T(8,128)(2,1)} fusion(f32[1280]{0:T(1024)S(1)} %mul.41, f32[2048]{0:T(1024)S(1)} %bitcast.237, bf16[2,1024,1280]{2,1,0:T(8,128)(2,1)} %param.13), kind=kLoop, calls=%fused_computation | loop fusion | flops 10485760 | bytes 10499072 | tf_op jit(solution)/shard_map/convert_element_type | solution.py:573
  49.5 19.5 %attention_forward.4 = (bf16[3,320,2048]{2,1,0:T(8,128)(2,1)}, bf16[320,2048]{1,0:T(8,128)(2,1)}, f32[4,1,2048]{2,1,0:T(1,128)}) custom-call(s32[2,4]{1,0:T(2,128)} %and_select_fusion.counts, bf16[2048,1280]{1,0:T(8,128)(2,1)} %multiply_convert_fusion.normed_ref, bf16[480,1280]{1,0:T(8,128)(2,1)} %bitcast.207, bf16[480,1280]{1,0:T(8,128)(2,1)} %bitcast.242, ...), custom_call_target="tpu_custom_call" | custom-call | flops 13623099392 | bytes 10485760 | tf_op jit(solution)/shard_map/attention_forward/pallas_call | solution.py:112
  69.0 3.2 collective-permute-done.11
  77.4 20.1 %attention_forward.5 = (bf16[3,320,2048]{2,1,0:T(8,128)(2,1)}, bf16[320,2048]{1,0:T(8,128)(2,1)}, f32[4,1,2048]{2,1,0:T(1,128)}) custom-call(s32[2,4]{1,0:T(2,128)} %and_select_fusion.counts, bf16[2048,1280]{1,0:T(8,128)(2,1)} %multiply_convert_fusion.normed_ref, bf16[480,1280]{1,0:T(8,128)(2,1)} %bitcast.220, bf16[480,1280]{1,0:T(8,128)(2,1)} %bitcast.244, ...), custom_call_target="tpu_custom_call" | custom-call | flops 13623099392 | bytes 10485760 | tf_op jit(solution)/shard_map/attention_forward/pallas_call | solution.py:112
  106.7 19.6 %attention_forward.6 = (bf16[3,320,2048]{2,1,0:T(8,128)(2,1)}, bf16[320,2048]{1,0:T(8,128)(2,1)}, f32[4,1,2048]{2,1,0:T(1,128)}) custom-call(s32[2,4]{1,0:T(2,128)} %and_select_fusion.counts, bf16[2048,1280]{1,0:T(8,128)(2,1)} %multiply_convert_fusion.normed_ref, bf16[480,1280]{1,0:T(8,128)(2,1)} %bitcast.222, bf16[480,1280]{1,0:T(8,128)(2,1)} %bitcast.246, ...), custom_call_target="tpu_custom_call" | custom-call | flops 13623099392 | bytes 10485760 | tf_op jit(solution)/shard_map/attention_forward/pallas_call | solution.py:112
  126.3 4.7 collective-permute-done.21
  135.1 19.3 %attention_forward.7 = (bf16[3,320,2048]{2,1,0:T(8,128)(2,1)}, bf16[320,2048]{1,0:T(8,128)(2,1)}, f32[4,1,2048]{2,1,0:T(1,128)}) custom-call(s32[2,4]{1,0:T(2,128)} %and_select_fusion.counts, bf16[2048,1280]{1,0:T(8,128)(2,1)} %multiply_convert_fusion.normed_ref, bf16[480,1280]{1,0:T(8,128)(2,1)} %bitcast.218, bf16[480,1280]{1,0:T(8,128)(2,1)} %bitcast.248, ...), custom_call_target="tpu_custom_call" | custom-call | flops 13623099392 | bytes 10485760 | tf_op jit(solution)/shard_map/attention_forward/pallas_call | solution.py:112
  154.5 84.5 %middle.1 = (bf16[2048,1280]{1,0:T(8,128)(2,1)}, f32[2048,1280]{1,0:T(8,128)}, bf16[320,2048]{1,0:T(8,128)(2,1)}, bf16[320,2048]{1,0:T(8,128)(2,1)}, bf16[320,20...) custom-call(s32[1]{0:T(128)} %bitcast.core_ref, ...), custom_call_target="tpu_custom_call" | custom-call | flops 60397977600 | bytes 56360960 | tf_op jit(solution)/shard_map/middle/pallas_call | solution.py:368
  240.7 21.4 %attention_backward.4 = (bf16[960,2048]{1,0:T(8,128)(2,1)}, f32[80,256]{1,0:T(8,128)}) custom-call(s32[2,4]{1,0:T(2,128)} %and_select_fusion.counts, bf16[3,320,2048]{2,1,0:T(8,128)(2,1)} %get-tuple-element.115.q_ref.k_ref.v_ref, bf16[3,320,2048]{2,1,0:T(8,128)(2,1)} %get-tuple-element.115.q_ref.k_ref.v_ref, ...), custom_call_target="tpu_custom_call" | custom-call | flops 15032385536 | bytes 10485760 | tf_op jit(solution)/shard_map/attention_backward/pallas_call | solution.py:245
  262.1 5.9 %convolution_convert_fusion.6 = bf16[480,1280]{1,0:T(8,128)(2,1)S(1)} fusion(bf16[2048,1280]{1,0:T(8,128)(2,1)} %multiply_convert_fusion.normed_ref, bf16[960,2048]{1,0:T(8,128)(2,1)} %get-tuple-element.154.rest_11_), kind=kOutput, calls=%fused_computation.8 | convolution fusion | flops 2517196800 | bytes 8437760 | tf_op jit(solution)/shard_map/dot_general | solution.py:27
  271.9 5.2 %convolution_convert_fusion.7 = bf16[480,1280]{1,0:T(8,128)(2,1)S(1)} fusion(bf16[2048,1280]{1,0:T(8,128)(2,1)} %multiply_convert_fusion.normed_ref, bf16[960,2048]{1,0:T(8,128)(2,1)S(1)} %copy-done.38), kind=kOutput, calls=%fused_computation.9 | convolution fusion | flops 2517196800 | bytes 8437760 | tf_op jit(solution)/shard_map/dot_general | solution.py:27
  277.4 3.7 slice_bitcast_fusion
  287.5 21.6 %attention_backward.5 = (bf16[960,2048]{1,0:T(8,128)(2,1)}, f32[80,256]{1,0:T(8,128)}) custom-call(s32[2,4]{1,0:T(2,128)} %and_select_fusion.counts, bf16[3,320,2048]{2,1,0:T(8,128)(2,1)} %get-tuple-element.114.q_ref.k_ref.v_ref, bf16[3,320,2048]{2,1,0:T(8,128)(2,1)} %get-tuple-element.114.q_ref.k_ref.v_ref, ...), custom_call_target="tpu_custom_call" | custom-call | flops 15032385536 | bytes 10485760 | tf_op jit(solution)/shard_map/attention_backward/pallas_call | solution.py:245
  309.1 5.9 %convolution_convert_fusion.4 = bf16[480,1280]{1,0:T(8,128)(2,1)S(1)} fusion(bf16[2048,1280]{1,0:T(8,128)(2,1)} %multiply_convert_fusion.normed_ref, bf16[960,2048]{1,0:T(8,128)(2,1)} %get-tuple-element.153.rest_10_), kind=kOutput, calls=%fused_computation.6 | convolution fusion | flops 2517196800 | bytes 8437760 | tf_op jit(solution)/shard_map/dot_general | solution.py:27
  316.4 5.2 %convolution_convert_fusion.5 = bf16[480,1280]{1,0:T(8,128)(2,1)S(1)} fusion(bf16[2048,1280]{1,0:T(8,128)(2,1)} %multiply_convert_fusion.normed_ref, bf16[960,2048]{1,0:T(8,128)(2,1)S(1)} %copy-done.39), kind=kOutput, calls=%fused_computation.7 | convolution fusion | flops 2517196800 | bytes 8437760 | tf_op jit(solution)/shard_map/dot_general | solution.py:27
  321.6 24.2 %collective-permute-done.28 = bf16[6,40,1280]{2,1,0:T(8,128)(2,1)S(1)} collective-permute-done((bf16[6,40,1280]{2,1,0:T(8,128)(2,1)S(1)}, bf16[6,40,1280]{2,1,0:T(8,128)(2,1)S(1)}, u32[]{:S(2)}, u32[]{:S(2)}) %collective-permute-start.28) | collective-permute-done | bytes 614432 | tf_op jit(solution)/shard_map/ppermute | solution.py:466
  352.4 21.8 %attention_backward.6 = (bf16[960,2048]{1,0:T(8,128)(2,1)}, f32[80,256]{1,0:T(8,128)}) custom-call(s32[2,4]{1,0:T(2,128)} %and_select_fusion.counts, bf16[3,320,2048]{2,1,0:T(8,128)(2,1)} %get-tuple-element.113.q_ref.k_ref.v_ref, bf16[3,320,2048]{2,1,0:T(8,128)(2,1)} %get-tuple-element.113.q_ref.k_ref.v_ref, ...), custom_call_target="tpu_custom_call" | custom-call | flops 15032385536 | bytes 10485760 | tf_op jit(solution)/shard_map/attention_backward/pallas_call | solution.py:245
  374.2 6.9 %convolution_convert_fusion.2 = bf16[480,1280]{1,0:T(8,128)(2,1)} fusion(bf16[2048,1280]{1,0:T(8,128)(2,1)} %multiply_convert_fusion.normed_ref, bf16[960,2048]{1,0:T(8,128)(2,1)} %get-tuple-element.152.rest_9_), kind=kOutput, calls=%fused_computation.4 | convolution fusion | flops 2517196800 | bytes 8437760 | tf_op jit(solution)/shard_map/dot_general | solution.py:27
  382.7 5.8 %convolution_convert_fusion.3 = bf16[480,1280]{1,0:T(8,128)(2,1)S(1)} fusion(bf16[2048,1280]{1,0:T(8,128)(2,1)} %multiply_convert_fusion.normed_ref, bf16[960,2048]{1,0:T(8,128)(2,1)} %get-tuple-element.152.rest_9_), kind=kOutput, calls=%fused_computation.5 | convolution fusion | flops 2517196800 | bytes 8437760 | tf_op jit(solution)/shard_map/dot_general | solution.py:27
  388.5 10.1 %collective-permute-done.31 = bf16[6,40,1280]{2,1,0:T(8,128)(2,1)S(1)} collective-permute-done((bf16[6,40,1280]{2,1,0:T(8,128)(2,1)}, bf16[6,40,1280]{2,1,0:T(8,128)(2,1)S(1)}, u32[]{:S(2)}, u32[]{:S(2)}) %collective-permute-start.31) | collective-permute-done | bytes 614432 | tf_op jit(solution)/shard_map/ppermute | solution.py:466
  401.2 3.0 fusion.13
  409.2 21.5 %attention_backward.7 = (bf16[960,2048]{1,0:T(8,128)(2,1)}, f32[80,256]{1,0:T(8,128)}) custom-call(s32[2,4]{1,0:T(2,128)} %and_select_fusion.counts, bf16[3,320,2048]{2,1,0:T(8,128)(2,1)} %get-tuple-element.112.q_ref.k_ref.v_ref, bf16[3,320,2048]{2,1,0:T(8,128)(2,1)} %get-tuple-element.112.q_ref.k_ref.v_ref, ...), custom_call_target="tpu_custom_call" | custom-call | flops 15032385536 | bytes 10485760 | tf_op jit(solution)/shard_map/attention_backward/pallas_call | solution.py:245
  430.8 5.9 %convolution_convert_fusion = bf16[480,1280]{1,0:T(8,128)(2,1)S(1)} fusion(bf16[2048,1280]{1,0:T(8,128)(2,1)} %multiply_convert_fusion.normed_ref, bf16[960,2048]{1,0:T(8,128)(2,1)} %get-tuple-element.151.rest_8_), kind=kOutput, calls=%fused_computation.2 | convolution fusion | flops 2517196800 | bytes 8437760 | tf_op jit(solution)/shard_map/dot_general | solution.py:27
  437.2 5.2 %convolution_convert_fusion.1 = bf16[480,1280]{1,0:T(8,128)(2,1)S(1)} fusion(bf16[2048,1280]{1,0:T(8,128)(2,1)} %multiply_convert_fusion.normed_ref, bf16[960,2048]{1,0:T(8,128)(2,1)S(1)} %copy-done.40), kind=kOutput, calls=%fused_computation.3 | convolution fusion | flops 2517196800 | bytes 8437760 | tf_op jit(solution)/shard_map/dot_general | solution.py:27
  450.1 3.6 collective-permute-start.34
  453.7 34.0 %back.1 = (f32[2048,1280]{1,0:T(8,128)}, f32[8,1280]{1,0:T(8,128)}) custom-call(bf16[2048,1280]{1,0:T(8,128)(2,1)} %bitcast.204, f32[2048,1280]{1,0:T(8,128)} %get-tuple-element.150.grad_hidden_ref, f32[1,1280]{1,0:T(1,128)} %slice.375.gain_ref, bf16[480,1280]{1,0:T(8,128)(2,1)} %bitcast.208, bf16[480,1280]{1,0:T(8,128)(2,1)} %bitcast.243, ...), custom_call_target="tpu_custom_call" | custom-call | flops 20132659200 | bytes 47185920 | tf_op jit(solution)/shard_map/back/pallas_call | solution.py:438
  489.9 3.7 collective-permute-done.41
  494.1 3.2 collective-permute-done.42
  497.2 3.7 collective-permute-done.43
  500.9 4.6 collective-permute-done.44
  (255 shorter events, 91.2 us)
Async XLA Ops:
  7.2 147.3 %all-gather.2.cloned.1.call-start = ((), (), s32[]{:S(2)}) async-start(), calls=%async_computation | async-start | bytes 10137600 | tf_op jit(solution)/shard_map/all_gather | solution.py:605
  10.1 27.0 %collective-permute-start.9 = (bf16[3,40,1280]{2,1,0:T(8,128)(2,1)S(1)}, bf16[3,40,1280]{2,1,0:T(8,128)(2,1)S(1)}, u32[]{:S(2)}, u32[]{:S(2)}) collective-permute-start(bf16[3,40,1280]{2,1,0:T(8,128)(2,1)S(1)} %get-tuple-element.248), channel_id=1, source_target_pairs={{0,8},{1,9},{2,10},{3,11},{4,12},{5,13},{6,14},{7,15},{8,0},{9,1},... | collective-permute-start | bytes 921608 | tf_op jit(solution)/shard_map/ppermute | solution.py:466
  13.2 23.9 %collective-permute-start.8 = (bf16[3,40,1280]{2,1,0:T(8,128)(2,1)S(1)}, bf16[3,40,1280]{2,1,0:T(8,128)(2,1)S(1)}, u32[]{:S(2)}, u32[]{:S(2)}) collective-permute-start(bf16[3,40,1280]{2,1,0:T(8,128)(2,1)S(1)} %get-tuple-element.248), channel_id=1, source_target_pairs={{0,4},{1,5},{2,6},{3,7},{4,0},{5,1},{6,2},{7,3},{8,12},{9,13},{10,... | collective-permute-start | bytes 921608 | tf_op jit(solution)/shard_map/ppermute | solution.py:466
  14.8 6.3 %collective-permute-start = (f32[80]{0:T(128)S(1)}, f32[80]{0:T(128)S(1)}, u32[]{:S(2)}, u32[]{:S(2)}) collective-permute-start(f32[80]{0:T(128)S(1)} %maximum_convert_fusion.1), channel_id=1, source_target_pairs={{0,1},{1,0},{2,3},{3,2},{4,5},{5,4},{6,7},{7,6},{8,9},{9,8},{10,11... | collective-permute-start | bytes 968 | tf_op jit(solution)/shard_map/ppermute | solution.py:466
  32.0 7.3 %collective-permute-start.7 = (bf16[3,40,1280]{2,1,0:T(8,128)(2,1)S(1)}, bf16[3,40,1280]{2,1,0:T(8,128)(2,1)S(1)}, u32[]{:S(2)}, u32[]{:S(2)}) collective-permute-start(bf16[3,40,1280]{2,1,0:T(8,128)(2,1)S(1)} %get-tuple-element.248), channel_id=1, source_target_pairs={{0,2},{1,3},{2,0},{3,1},{4,6},{5,7},{6,4},{7,5},{8,10},{9,11},{10,... | collective-permute-start | bytes 921608 | tf_op jit(solution)/shard_map/ppermute | solution.py:466
  32.6 36.4 %collective-permute-start.13 = (bf16[1,3,40,1280]{3,2,1,0:T(8,128)(2,1)S(1)}, bf16[1,3,40,1280]{3,2,1,0:T(8,128)(2,1)S(1)}, u32[]{:S(2)}, u32[]{:S(2)}) collective-permute-start(bf16[1,3,40,1280]{3,2,1,0:T(8,128)(2,1)S(1)} %get-tuple-element.247), channel_id=1, source_target_pairs={{0,16},{1,17},{2,18},{3,19},{4,20},{5,21},{6,22},{7,23},{8,24},{9,... | collective-permute-start | bytes 921608 | tf_op jit(solution)/shard_map/ppermute | solution.py:466
  39.5 8.9 %collective-permute-start.10 = (bf16[4,3,40,1280]{3,2,1,0:T(8,128)(2,1)S(1)}, bf16[4,3,40,1280]{3,2,1,0:T(8,128)(2,1)S(1)}, u32[]{:S(2)}, u32[]{:S(2)}) collective-permute-start(bf16[4,3,40,1280]{3,2,1,0:T(8,128)(2,1)S(1)} %pad_maximum_fusion), channel_id=1, source_target_pairs={{0,1},{1,0},{2,3},{3,2},{4,5},{5,4},{6,7},{7,6},{8,9},{9,8},{10,11... | collective-permute-start | bytes 3686408 | tf_op jit(solution)/shard_map/ppermute | solution.py:466
  46.1 23.0 %collective-permute-start.12 = (bf16[1,3,40,1280]{3,2,1,0:T(8,128)(2,1)S(1)}, bf16[1,3,40,1280]{3,2,1,0:T(8,128)(2,1)S(1)}, u32[]{:S(2)}, u32[]{:S(2)}) collective-permute-start(bf16[1,3,40,1280]{3,2,1,0:T(8,128)(2,1)S(1)} %bitcast.214), channel_id=1, source_target_pairs={{0,4},{1,5},{2,6},{3,7},{4,0},{5,1},{6,2},{7,3},{8,12},{9,13},{10,... | collective-permute-start | bytes 921608 | tf_op jit(solution)/shard_map/ppermute | solution.py:466
  47.8 24.4 %collective-permute-start.11 = (bf16[2,3,40,1280]{3,2,1,0:T(8,128)(2,1)S(1)}, bf16[2,3,40,1280]{3,2,1,0:T(8,128)(2,1)}, u32[]{:S(2)}, u32[]{:S(2)}) collective-permute-start(bf16[2,3,40,1280]{3,2,1,0:T(8,128)(2,1)S(1)} %pad_maximum_fusion.4), channel_id=1, source_target_pairs={{0,2},{1,3},{2,0},{3,1},{4,6},{5,7},{6,4},{7,5},{8,10},{9,11},{10,... | collective-permute-start | bytes 1843208 | tf_op jit(solution)/shard_map/ppermute | solution.py:466
  73.5 24.0 %collective-permute-start.16 = (bf16[1,3,40,1280]{3,2,1,0:T(8,128)(2,1)S(1)}, bf16[1,3,40,1280]{3,2,1,0:T(8,128)(2,1)S(1)}, u32[]{:S(2)}, u32[]{:S(2)}) collective-permute-start(bf16[1,3,40,1280]{3,2,1,0:T(8,128)(2,1)S(1)} %collective-permute-done.13), channel_id=1, source_target_pairs={{0,4},{1,5},{2,6},{3,7},{4,0},{5,1},{6,2},{7,3},{8,12},{9,13},{10,... | collective-permute-start | bytes 921608 | tf_op jit(solution)/shard_map/ppermute | solution.py:466
  74.0 23.5 %collective-permute-start.17 = (bf16[1,3,40,1280]{3,2,1,0:T(8,128)(2,1)S(1)}, bf16[1,3,40,1280]{3,2,1,0:T(8,128)(2,1)S(1)}, u32[]{:S(2)}, u32[]{:S(2)}) collective-permute-start(bf16[1,3,40,1280]{3,2,1,0:T(8,128)(2,1)S(1)} %collective-permute-done.13), channel_id=1, source_target_pairs={{0,8},{1,9},{2,10},{3,11},{4,12},{5,13},{6,14},{7,15},{8,0},{9,1},... | collective-permute-start | bytes 921608 | tf_op jit(solution)/shard_map/ppermute | solution.py:466
  74.6 25.1 %collective-permute-start.15 = (bf16[2,3,40,1280]{3,2,1,0:T(8,128)(2,1)S(1)}, bf16[2,3,40,1280]{3,2,1,0:T(8,128)(2,1)S(1)}, u32[]{:S(2)}, u32[]{:S(2)}) collective-permute-start(bf16[2,3,40,1280]{3,2,1,0:T(8,128)(2,1)S(1)} %pad_maximum_fusion.5), channel_id=1, source_target_pairs={{0,2},{1,3},{2,0},{3,1},{4,6},{5,7},{6,4},{7,5},{8,10},{9,11},{10,... | collective-permute-start | bytes 1843208 | tf_op jit(solution)/shard_map/ppermute | solution.py:466
  100.8 30.2 %collective-permute-start.20 = (bf16[1,3,40,1280]{3,2,1,0:T(8,128)(2,1)S(1)}, bf16[1,3,40,1280]{3,2,1,0:T(8,128)(2,1)S(1)}, u32[]{:S(2)}, u32[]{:S(2)}) collective-permute-start(bf16[1,3,40,1280]{3,2,1,0:T(8,128)(2,1)S(1)} %collective-permute-done.17), channel_id=1, source_target_pairs={{0,4},{1,5},{2,6},{3,7},{4,0},{5,1},{6,2},{7,3},{8,12},{9,13},{10,... | collective-permute-start | bytes 921608 | tf_op jit(solution)/shard_map/ppermute | solution.py:466
  102.7 28.3 %collective-permute-start.19 = (bf16[2,3,40,1280]{3,2,1,0:T(8,128)(2,1)S(1)}, bf16[2,3,40,1280]{3,2,1,0:T(8,128)(2,1)S(1)}, u32[]{:S(2)}, u32[]{:S(2)}) collective-permute-start(bf16[2,3,40,1280]{3,2,1,0:T(8,128)(2,1)S(1)} %pad_maximum_fusion.6), channel_id=1, source_target_pairs={{0,2},{1,3},{2,0},{3,1},{4,6},{5,7},{6,4},{7,5},{8,10},{9,11},{10,... | collective-permute-start | bytes 1843208 | tf_op jit(solution)/shard_map/ppermute | solution.py:466
  103.3 27.7 %collective-permute-start.21 = (bf16[1,3,40,1280]{3,2,1,0:T(8,128)(2,1)}, bf16[1,3,40,1280]{3,2,1,0:T(8,128)(2,1)S(1)}, u32[]{:S(2)}, u32[]{:S(2)}) collective-permute-start(bf16[1,3,40,1280]{3,2,1,0:T(8,128)(2,1)} %slice.300), channel_id=1, source_target_pairs={{0,16},{1,17},{2,18},{3,19},{4,20},{5,21},{6,22},{7,23},{8,24},{9,... | collective-permute-start | bytes 921608 | tf_op jit(solution)/shard_map/ppermute | solution.py:466
  238.9 38.4 %collective-permute-start.24 = (bf16[16,3,40,1280]{3,2,1,0:T(8,128)(2,1)}, bf16[16,3,40,1280]{3,2,1,0:T(8,128)(2,1)}, u32[]{:S(2)}, u32[]{:S(2)}) collective-permute-start(bf16[16,3,40,1280]{3,2,1,0:T(8,128)(2,1)} %get-tuple-element.122), channel_id=1, source_target_pairs={{0,1},{1,0},{2,3},{3,2},{4,5},{5,4},{6,7},{7,6},{8,9},{9,8},{10,11... | collective-permute-start | bytes 14745608 | tf_op jit(solution)/shard_map/ppermute | solution.py:466
  268.1 9.1 %collective-permute-start.23 = (bf16[4,3,40,1280]{3,2,1,0:T(8,128)(2,1)S(1)}, bf16[4,3,40,1280]{3,2,1,0:T(8,128)(2,1)S(1)}, u32[]{:S(2)}, u32[]{:S(2)}) collective-permute-start(bf16[4,3,40,1280]{3,2,1,0:T(8,128)(2,1)S(1)} %bitcast.252), channel_id=1, source_target_pairs={{0,1},{1,0},{2,3},{3,2},{4,5},{5,4},{6,7},{7,6},{8,9},{9,8},{10,11... | collective-permute-start | bytes 3686408 | tf_op jit(solution)/shard_map/ppermute | solution.py:466
  282.6 63.2 %collective-permute-start.26 = (bf16[2,6,40,1280]{3,2,1,0:T(8,128)(2,1)}, bf16[2,6,40,1280]{3,2,1,0:T(8,128)(2,1)}, u32[]{:S(2)}, u32[]{:S(2)}) collective-permute-start(bf16[2,6,40,1280]{3,2,1,0:T(8,128)(2,1)} %pad_maximum_fusion.1), channel_id=1, source_target_pairs={{0,2},{1,3},{2,0},{3,1},{4,6},{5,7},{6,4},{7,5},{8,10},{9,11},{10,... | collective-permute-start | bytes 3686408 | tf_op jit(solution)/shard_map/ppermute | solution.py:466
  315.1 30.8 %collective-permute-start.25 = (bf16[4,3,40,1280]{3,2,1,0:T(8,128)(2,1)S(1)}, bf16[4,3,40,1280]{3,2,1,0:T(8,128)(2,1)S(1)}, u32[]{:S(2)}, u32[]{:S(2)}) collective-permute-start(bf16[4,3,40,1280]{3,2,1,0:T(8,128)(2,1)S(1)} %bitcast.251), channel_id=1, source_target_pairs={{0,1},{1,0},{2,3},{3,2},{4,5},{5,4},{6,7},{7,6},{8,9},{9,8},{10,11... | collective-permute-start | bytes 3686408 | tf_op jit(solution)/shard_map/ppermute | solution.py:466
  315.9 29.9 %collective-permute-start.28 = (bf16[6,40,1280]{2,1,0:T(8,128)(2,1)S(1)}, bf16[6,40,1280]{2,1,0:T(8,128)(2,1)S(1)}, u32[]{:S(2)}, u32[]{:S(2)}) collective-permute-start(bf16[6,40,1280]{2,1,0:T(8,128)(2,1)S(1)} %copy-done.14), channel_id=1, source_target_pairs={{0,16},{1,17},{2,18},{3,19},{4,20},{5,21},{6,22},{7,23},{8,24},{9,... | collective-permute-start | bytes 1843208 | tf_op jit(solution)/shard_map/ppermute | solution.py:466
  315.9 29.9 %collective-permute-start.27 = (bf16[6,40,1280]{2,1,0:T(8,128)(2,1)S(1)}, bf16[6,40,1280]{2,1,0:T(8,128)(2,1)S(1)}, u32[]{:S(2)}, u32[]{:S(2)}) collective-permute-start(bf16[6,40,1280]{2,1,0:T(8,128)(2,1)S(1)} %copy-done.15), channel_id=1, source_target_pairs={{0,4},{1,5},{2,6},{3,7},{4,0},{5,1},{6,2},{7,3},{8,12},{9,13},{10,... | collective-permute-start | bytes 1843208 | tf_op jit(solution)/shard_map/ppermute | solution.py:466
  348.4 50.2 %collective-permute-start.30 = (bf16[2,6,40,1280]{3,2,1,0:T(8,128)(2,1)}, bf16[2,6,40,1280]{3,2,1,0:T(8,128)(2,1)}, u32[]{:S(2)}, u32[]{:S(2)}) collective-permute-start(bf16[2,6,40,1280]{3,2,1,0:T(8,128)(2,1)} %pad_maximum_fusion.2), channel_id=1, source_target_pairs={{0,2},{1,3},{2,0},{3,1},{4,6},{5,7},{6,4},{7,5},{8,10},{9,11},{10,... | collective-permute-start | bytes 3686408 | tf_op jit(solution)/shard_map/ppermute | solution.py:466
  381.1 17.5 %collective-permute-start.29 = (bf16[4,3,40,1280]{3,2,1,0:T(8,128)(2,1)}, bf16[4,3,40,1280]{3,2,1,0:T(8,128)(2,1)}, u32[]{:S(2)}, u32[]{:S(2)}) collective-permute-start(bf16[4,3,40,1280]{3,2,1,0:T(8,128)(2,1)} %bitcast.61), channel_id=1, source_target_pairs={{0,1},{1,0},{2,3},{3,2},{4,5},{5,4},{6,7},{7,6},{8,9},{9,8},{10,11... | collective-permute-start | bytes 3686408 | tf_op jit(solution)/shard_map/ppermute | solution.py:466
  382.6 16.0 %collective-permute-start.31 = (bf16[6,40,1280]{2,1,0:T(8,128)(2,1)}, bf16[6,40,1280]{2,1,0:T(8,128)(2,1)S(1)}, u32[]{:S(2)}, u32[]{:S(2)}) collective-permute-start(bf16[6,40,1280]{2,1,0:T(8,128)(2,1)} %get-tuple-element.230), channel_id=1, source_target_pairs={{0,4},{1,5},{2,6},{3,7},{4,0},{5,1},{6,2},{7,3},{8,12},{9,13},{10,... | collective-permute-start | bytes 1843208 | tf_op jit(solution)/shard_map/ppermute | solution.py:466
  382.6 16.0 %collective-permute-start.32 = (bf16[6,40,1280]{2,1,0:T(8,128)(2,1)S(1)}, bf16[6,40,1280]{2,1,0:T(8,128)(2,1)S(1)}, u32[]{:S(2)}, u32[]{:S(2)}) collective-permute-start(bf16[6,40,1280]{2,1,0:T(8,128)(2,1)S(1)} %copy-done.18), channel_id=1, source_target_pairs={{0,8},{1,9},{2,10},{3,11},{4,12},{5,13},{6,14},{7,15},{8,0},{9,1},... | collective-permute-start | bytes 1843208 | tf_op jit(solution)/shard_map/ppermute | solution.py:466
  404.1 38.3 %collective-permute-start.36 = (bf16[6,40,1280]{2,1,0:T(8,128)(2,1)}, bf16[6,40,1280]{2,1,0:T(8,128)(2,1)}, u32[]{:S(2)}, u32[]{:S(2)}) collective-permute-start(bf16[6,40,1280]{2,1,0:T(8,128)(2,1)} %get-tuple-element.220), channel_id=1, source_target_pairs={{0,4},{1,5},{2,6},{3,7},{4,0},{5,1},{6,2},{7,3},{8,12},{9,13},{10,... | collective-permute-start | bytes 1843208 | tf_op jit(solution)/shard_map/ppermute | solution.py:466
  405.7 36.8 %collective-permute-start.37 = (bf16[6,40,1280]{2,1,0:T(8,128)(2,1)}, bf16[6,40,1280]{2,1,0:T(8,128)(2,1)S(1)}, u32[]{:S(2)}, u32[]{:S(2)}) collective-permute-start(bf16[6,40,1280]{2,1,0:T(8,128)(2,1)} %get-tuple-element.219), channel_id=1, source_target_pairs={{0,16},{1,17},{2,18},{3,19},{4,20},{5,21},{6,22},{7,23},{8,24},{9,... | collective-permute-start | bytes 1843208 | tf_op jit(solution)/shard_map/ppermute | solution.py:466
  409.2 33.3 %collective-permute-start.35 = (bf16[2,6,40,1280]{3,2,1,0:T(8,128)(2,1)}, bf16[2,6,40,1280]{3,2,1,0:T(8,128)(2,1)S(1)}, u32[]{:S(2)}, u32[]{:S(2)}) collective-permute-start(bf16[2,6,40,1280]{3,2,1,0:T(8,128)(2,1)} %pad_maximum_fusion.3), channel_id=1, source_target_pairs={{0,2},{1,3},{2,0},{3,1},{4,6},{5,7},{6,4},{7,5},{8,10},{9,11},{10,... | collective-permute-start | bytes 3686408 | tf_op jit(solution)/shard_map/ppermute | solution.py:466
  436.7 5.8 %collective-permute-start.33 = (bf16[4,3,40,1280]{3,2,1,0:T(8,128)(2,1)S(1)}, bf16[4,3,40,1280]{3,2,1,0:T(8,128)(2,1)S(1)}, u32[]{:S(2)}, u32[]{:S(2)}) collective-permute-start(bf16[4,3,40,1280]{3,2,1,0:T(8,128)(2,1)S(1)} %bitcast.250), channel_id=1, source_target_pairs={{0,1},{1,0},{2,3},{3,2},{4,5},{5,4},{6,7},{7,6},{8,9},{9,8},{10,11... | collective-permute-start | bytes 3686408 | tf_op jit(solution)/shard_map/ppermute | solution.py:466
  447.3 59.3 %collective-permute-start.38 = (bf16[6,40,1280]{2,1,0:T(8,128)(2,1)}, bf16[6,40,1280]{2,1,0:T(8,128)(2,1)S(1)}, u32[]{:S(2)}, u32[]{:S(2)}) collective-permute-start(bf16[6,40,1280]{2,1,0:T(8,128)(2,1)} %get-tuple-element.218), channel_id=1, source_target_pairs={{0,4},{1,5},{2,6},{3,7},{4,0},{5,1},{6,2},{7,3},{8,12},{9,13},{10,... | collective-permute-start | bytes 1843208 | tf_op jit(solution)/shard_map/ppermute | solution.py:466
  447.6 59.1 %collective-permute-start.39 = (bf16[6,40,1280]{2,1,0:T(8,128)(2,1)}, bf16[6,40,1280]{2,1,0:T(8,128)(2,1)}, u32[]{:S(2)}, u32[]{:S(2)}) collective-permute-start(bf16[6,40,1280]{2,1,0:T(8,128)(2,1)} %get-tuple-element.217), channel_id=1, source_target_pairs={{0,8},{1,9},{2,10},{3,11},{4,12},{5,13},{6,14},{7,15},{8,0},{9,1},... | collective-permute-start | bytes 1843208 | tf_op jit(solution)/shard_map/ppermute | solution.py:466
  450.1 56.5 %collective-permute-start.34 = (bf16[6,40,1280]{2,1,0:T(8,128)(2,1)S(1)}, bf16[6,40,1280]{2,1,0:T(8,128)(2,1)}, u32[]{:S(2)}, u32[]{:S(2)}) collective-permute-start(bf16[6,40,1280]{2,1,0:T(8,128)(2,1)S(1)} %add_convert_fusion), channel_id=1, source_target_pairs={{0,2},{1,3},{2,0},{3,1},{4,6},{5,7},{6,4},{7,5},{8,10},{9,11},{10,... | collective-permute-start | bytes 1843208 | tf_op jit(solution)/shard_map/ppermute | solution.py:466
  (57 other events, 281.3 us)
Sparse Core Ops, SparseCore 0:
  11.5 121.4 all-gather.1
